TPU v7x, 256 devices: a whole 4x4x8 slice. The times are simulated.
256 devices in a mesh: dp: 32 (over z, y_hi, core), owner: 8 (over y_lo, x).
Axes of the slice: x: 4, y: 4 (y_hi: 2, y_lo: 2; y = y_hi * 2 + y_lo), z: 8, core: 2. Of those that a mesh axis runs over, the one named last changes fastest.
Arguments:
- inputs: bfloat16 [4096, 8192], P('dp'), may hold values from -12 to 12
- out_grads: bfloat16 [4096, 8192], P('dp', 'owner'), may hold values from -16 to 16
- weights: float32 [256, 512, 512], P(('dp', 'owner')), may hold values from -0.0625 to 0.0625
- left_stats: float32 [256, 512, 512], P(('dp', 'owner')), as said below
- right_stats: float32 [256, 512, 512], P(('dp', 'owner')), as said below
- left_roots: float32 [256, 512, 512], P(('dp', 'owner')), as said below
- right_roots: float32 [256, 512, 512], P(('dp', 'owner')), as said below
- refresh: int32 [256], P(('dp', 'owner')), may hold values from 0 to 1, as said below
Outputs:
- new_left_stats: float32 [256, 512, 512], P(('dp', 'owner'))
- new_right_stats: float32 [256, 512, 512], P(('dp', 'owner'))
- new_left_roots: float32 [256, 512, 512], P(('dp', 'owner'))
- new_right_roots: float32 [256, 512, 512], P(('dp', 'owner'))
- update: float32 [256, 512, 512], P(('dp', 'owner'))
- queries: bfloat16 [4096, 8192], P('dp', 'owner')
Inputs may be any that keep to these rules, and one draw needn't show every extreme that they name: For every k, refresh[2k] + refresh[2k + 1] is at most 1, and refresh[0] + refresh[1] is 1. `left_stats`: every block is symmetric positive definite. `right_stats`: every block is symmetric positive definite. `left_roots`: every block is symmetric positive definite. `right_roots`: every block is symmetric positive definite.
All inputs are finite; a program needn't handle non-finite values.
Results may differ from a plain program's by a relative error of at most 0.015.
Values may be sent and summed in bfloat16 or wider, within the bound.
No kernel may reach another device: no remote copies, remote signals or barrier semaphores. Data moves between devices by JAX's collectives and lax.ppermute only.
A program may use at most 128 MiB of HBM per device.

v0:
```python
import math

import jax
import jax.numpy as jnp
from jax import lax
from jax.sharding import PartitionSpec as P

NEWTON = 2


BETA = 0.95
DAMPING = 0.0001


def matmul(left_mat, right_mat):
    return jnp.dot(left_mat, right_mat, preferred_element_type=jnp.float32)


def inverse_root(statistic):
    identity = jnp.eye(statistic.shape[0], dtype=jnp.float32)
    damped = statistic + DAMPING * identity
    factor_z = 2.5 / jnp.sqrt(jnp.sum(damped * damped))
    current = factor_z * damped
    result = jnp.sqrt(jnp.sqrt(factor_z)) * identity
    for turn in range(NEWTON):
        factor = 1.25 * identity - 0.25 * current
        result = matmul(result, factor)
        square = matmul(factor, factor)
        current = matmul(matmul(square, square), current)
    return result


def both_roots(left_stat, right_stat, left_old, right_old):
    return (inverse_root(left_stat), inverse_root(right_stat))


def stale_roots(left_stat, right_stat, left_old, right_old):
    return (left_old, right_old)


def body(inputs, out_grads, weights, left_stats, right_stats, left_roots, right_roots, refresh):
    tok_local, model_width = inputs.shape
    block_size = weights.shape[1]
    col_count = out_grads.shape[1]
    row_blocks = model_width // block_size
    col_blocks = col_count // block_size
    replicas = lax.axis_size("dp")
    tok_total = tok_local * replicas
    x_blocks = inputs.reshape(tok_local, row_blocks, block_size)
    g_blocks = out_grads.reshape(tok_local, col_blocks, block_size)
    feature_send = jnp.repeat(x_blocks, col_blocks, axis=1)
    grad_send = jnp.tile(g_blocks, (1, row_blocks, 1))
    feature_recv, grad_recv = (
        lax.all_to_all(feature_send, "dp", split_axis=1, concat_axis=1, tiled=True),
        lax.all_to_all(grad_send, "dp", split_axis=1, concat_axis=1, tiled=True),
    )
    group_size = 4

    def add_group(turn_index, running):
        x_group = lax.dynamic_slice_in_dim(feature_recv, turn_index * group_size, group_size, 1)
        g_group = lax.dynamic_slice_in_dim(grad_recv, turn_index * group_size, group_size, 1)
        products = (
            jnp.einsum("tsb,tsc->sbc", x_group, g_group, preferred_element_type=jnp.float32)
            / tok_total
        )
        products = lax.optimization_barrier(products.astype(jnp.bfloat16))
        return running + jnp.sum(products.astype(jnp.float32), 0)

    gradient = lax.fori_loop(
        0, replicas // group_size, add_group, jnp.zeros((block_size, block_size), jnp.float32)
    )
    left_new = BETA * left_stats[0] + (1.0 - BETA) * matmul(gradient, gradient.T)
    right_new = BETA * right_stats[0] + (1.0 - BETA) * matmul(gradient.T, gradient)
    refreshing = refresh[0] > 0
    left_root, right_root = lax.cond(
        refreshing, both_roots, stale_roots, left_new, right_new, left_roots[0], right_roots[0]
    )
    direction = matmul(matmul(left_root, gradient), right_root)
    direction = direction * (block_size / jnp.sqrt(jnp.sum(direction * direction) + 1e-12))
    rate = 0.25 / math.sqrt(model_width)
    updated = (weights[0] - rate * direction).astype(jnp.bfloat16)
    partial_out = jnp.einsum(
        "tsb,bc->tsc", feature_recv, updated, preferred_element_type=jnp.float32
    )
    returned = lax.all_to_all(
        partial_out.astype(jnp.bfloat16), "dp", split_axis=1, concat_axis=1, tiled=True
    ).astype(partial_out.dtype)
    queries = returned.reshape(tok_local, row_blocks, col_blocks, block_size).sum(1)
    queries = queries.reshape(tok_local, col_count).astype(jnp.bfloat16)
    return (
        left_new[None],
        right_new[None],
        left_root[None],
        right_root[None],
        direction[None],
        queries,
    )


def solution(mesh):
    in_specs = (
        P("dp", None),
        P("dp", "owner"),
        P(("dp", "owner"), None, None),
        P(("dp", "owner"), None, None),
        P(("dp", "owner"), None, None),
        P(("dp", "owner"), None, None),
        P(("dp", "owner"), None, None),
        P(("dp", "owner")),
    )
    out_specs = (
        P(("dp", "owner"), None, None),
        P(("dp", "owner"), None, None),
        P(("dp", "owner"), None, None),
        P(("dp", "owner"), None, None),
        P(("dp", "owner"), None, None),
        P("dp", "owner"),
    )
    return jax.shard_map(body, mesh=mesh, in_specs=in_specs, out_specs=out_specs, check_vma=False)
```

profile of v0, /device:TPU:1, one launch (start us, length us, event | category | flops | bytes accessed | tf_op | source)
XLA Modules:
  0.0 378.0 jit_solution(8345739376024094570)
XLA Ops:
  0.6 2.4 copy.53
  3.3 2.5 broadcast_in_dim.26
  5.8 12.9 %all-to-all-start = ((bf16[128,32,512]{2,0,1:T(8,128)(2,1)}), bf16[128,32,512]{2,0,1:T(8,128)(2,1)}, u32[]{:S(2)}, u32[]{:S(2)}) async-start(bf16[128,32,512]{2,0,1:T(8,128)(2,1)} %bitcast.52), calls=%async_computation | async-start | bytes 8388608 | tf_op jit(solution)/shard_map/all_to_all | solution.py:54
  18.8 94.0 %all-to-all-done = bf16[128,32,512]{2,0,1:T(8,128)(2,1)} async-done(((bf16[128,32,512]{2,0,1:T(8,128)(2,1)}), bf16[128,32,512]{2,0,1:T(8,128)(2,1)}, u32[]{:S(2)}, u32[]{:S(2)}) %all-to-all-start) | async-done | bytes 4194336 | tf_op jit(solution)/shard_map/all_to_all | solution.py:54
  112.8 2.4 tile.11
  115.2 7.5 %all-to-all-start.1 = ((bf16[128,32,512]{2,0,1:T(8,128)(2,1)}), bf16[128,32,512]{2,0,1:T(8,128)(2,1)}, u32[]{:S(2)}, u32[]{:S(2)}) async-start(bf16[128,32,512]{2,0,1:T(8,128)(2,1)} %bitcast.51), calls=%async_computation.1 | async-start | bytes 8388608 | tf_op jit(solution)/shard_map/all_to_all | solution.py:55
  123.4 93.4 %all-to-all-done.1 = bf16[128,32,512]{2,0,1:T(8,128)(2,1)} async-done(((bf16[128,32,512]{2,0,1:T(8,128)(2,1)}), bf16[128,32,512]{2,0,1:T(8,128)(2,1)}, u32[]{:S(2)}, u32[]{:S(2)}) %all-to-all-start.1) | async-done | bytes 4194336 | tf_op jit(solution)/shard_map/all_to_all | solution.py:55
  216.8 21.4 %while.14 = (s32[]{:T(128)}, f32[512,512]{1,0:T(8,128)S(1)}, bf16[128,32,512]{2,0,1:T(8,128)(2,1)}, bf16[128,32,512]{2,0,1:T(8,128)(2,1)}, s32[]{:T(128)}, /*index=5*/s32[]{:T(128)}, s32[]{:T(128)}, s32[]{:T(128)}) while((s32[]{:T(128)}, f32[512,512]{1,0:T(8,128)S(1)}, bf16[128,32,512]{2,0,1:T(8,128)(2,1)}, ...), condition=%wide.region_2.0_spmd.clone, body=%wide.region_0.0_spmd.clone.sunk | while | flops 272891904 | bytes 9438349 | solution.py:69
  219.5 2.0 multiply_convert_fusion.2
  222.1 2.0 multiply_convert_fusion.2
  224.8 2.0 multiply_convert_fusion.2
  227.5 2.0 multiply_convert_fusion.2
  230.2 2.0 multiply_convert_fusion.2
  232.8 2.0 multiply_convert_fusion.2
  235.5 2.0 multiply_convert_fusion.2
  241.6 20.0 %conditional.1 = (f32[512,512]{1,0:T(8,128)}, f32[512,512]{1,0:T(8,128)S(1)}, f32[1,512,512]{2,1,0:T(8,128)S(1)}, f32[1,512,512]{2,1,0:T(8,128)}) conditional(s32[]{:T(128)} %bitcast.10, (f32[1,512,512]{2,1,0:T(8,128)}, f32[1,512,512]{2,1,0:T(8,128)S(1)}) %tuple.61, (f32[512,512]{1,0:T(8,128)S(1)}, f32[512,512]{1,0:T(8,128)S(1)}) %tuple.36), branch_computations={%region_3.0_spmd, %region_4.0_spmd} | conditional | flops 2699558912 | bytes 35651832 | solution.py:75
  250.3 4.7 %fusion.3 = bf16[512,512]{1,0:T(8,128)(2,1)} fusion(f32[]{:T(128)S(6)} %div.11, f32[512,512]{1,0:T(8,128)} %copy-done.5), kind=kOutput, calls=%fused_computation.6 | convolution fusion | flops 538705920 | bytes 1572868 | tf_op jit(solution)/shard_map/cond/branch_1_fun/dot_general | solution.py:16
  255.1 2.3 select_subtract_fusion.2
  257.5 2.9 fusion.9
  262.5 2.7 multiply_reduce_fusion.2
  265.9 6.9 %convert_bitcast_fusion = bf16[128,32,512]{0,2,1:T(8,128)(2,1)} fusion(bf16[128,32,512]{2,0,1:T(8,128)(2,1)} %all-to-all-done, f32[512,512]{1,0:T(8,128)S(1)} %get-tuple-element.156, f32[1,512,512]{2,1,0:T(8,128)} %param.14, f32[]{:T(128)S(6)} %div.14), kind=kOutput, calls=%fused_computation.69 | convolution fusion | flops 2150629376 | bytes 10485764 | tf_op jit(solution)/shard_map/tsb,bc->tsc/dot_general | solution.py:82
  272.8 7.4 %all-to-all-start.2 = ((bf16[128,32,512]{0,2,1:T(8,128)(2,1)}), bf16[128,32,512]{0,2,1:T(8,128)(2,1)}, u32[]{:S(2)}, u32[]{:S(2)}) async-start(bf16[128,32,512]{0,2,1:T(8,128)(2,1)} %convert_bitcast_fusion), calls=%async_computation.2 | async-start | bytes 8388608 | tf_op jit(solution)/shard_map/all_to_all | solution.py:85
  281.3 93.0 %all-to-all-done.2 = bf16[128,32,512]{0,2,1:T(8,128)(2,1)} async-done(((bf16[128,32,512]{0,2,1:T(8,128)(2,1)}), bf16[128,32,512]{0,2,1:T(8,128)(2,1)}, u32[]{:S(2)}, u32[]{:S(2)}) %all-to-all-start.2) | async-done | bytes 4194336 | tf_op jit(solution)/shard_map/all_to_all | solution.py:85
  374.3 2.9 reduce
  (52 shorter events, 22.2 us)
Async XLA Ops:
  0.6 2.4 copy-start.7
  5.8 13.0 %copy-start.10 = (bf16[128,1024]{1,0:T(8,128)(2,1)S(1)}, bf16[128,1024]{1,0:T(8,128)(2,1)}, u32[]{:S(2)}) copy-start(bf16[128,1024]{1,0:T(8,128)(2,1)} %param.13) | copy-start | bytes 786436
  5.8 107.0 %all-to-all-start = ((bf16[128,32,512]{2,0,1:T(8,128)(2,1)}), bf16[128,32,512]{2,0,1:T(8,128)(2,1)}, u32[]{:S(2)}, u32[]{:S(2)}) async-start(bf16[128,32,512]{2,0,1:T(8,128)(2,1)} %bitcast.52), calls=%async_computation | async-start | bytes 8388608 | tf_op jit(solution)/shard_map/all_to_all | solution.py:54
  115.2 101.6 %all-to-all-start.1 = ((bf16[128,32,512]{2,0,1:T(8,128)(2,1)}), bf16[128,32,512]{2,0,1:T(8,128)(2,1)}, u32[]{:S(2)}, u32[]{:S(2)}) async-start(bf16[128,32,512]{2,0,1:T(8,128)(2,1)} %bitcast.51), calls=%async_computation.1 | async-start | bytes 8388608 | tf_op jit(solution)/shard_map/all_to_all | solution.py:55
  238.2 1.9 copy-start.9
  238.2 2.4 copy-start.2
  240.1 1.0 copy-start.3
  240.6 1.0 copy-start.4
  241.6 1.0 copy-start.5
  248.5 8.9 %copy-start = (f32[512,512]{1,0:T(8,128)}, f32[512,512]{1,0:T(8,128)S(1)}, u32[]{:S(2)}) copy-start(f32[512,512]{1,0:T(8,128)S(1)} %fusion.6) | copy-start | bytes 3145732 | tf_op jit(solution)/shard_map/cond
  248.5 6.5 %copy-start.6 = (f32[512,512]{1,0:T(8,128)S(1)}, f32[512,512]{1,0:T(8,128)}, u32[]{:S(2)}) copy-start(f32[512,512]{1,0:T(8,128)} %copy-done.5) | copy-start | bytes 3145732 | tf_op jit(solution)/shard_map/cond
  257.4 4.1 %copy-start.1 = (f32[512,512]{1,0:T(8,128)S(1)}, f32[512,512]{1,0:T(8,128)}, u32[]{:S(2)}) copy-start(f32[512,512]{1,0:T(8,128)} %copy-done) | copy-start | bytes 3145732 | tf_op jit(solution)/shard_map/cond
  261.6 1.0 copy-start.8
  272.8 101.4 %all-to-all-start.2 = ((bf16[128,32,512]{0,2,1:T(8,128)(2,1)}), bf16[128,32,512]{0,2,1:T(8,128)(2,1)}, u32[]{:S(2)}, u32[]{:S(2)}) async-start(bf16[128,32,512]{0,2,1:T(8,128)(2,1)} %convert_bitcast_fusion), calls=%async_computation.2 | async-start | bytes 8388608 | tf_op jit(solution)/shard_map/all_to_all | solution.py:85
where the time goes:
time: 380 us; the launch traced here: 378 us
  waiting for transfers between devices  280 us (74%)
  matrix products  41.7 us (11%)
  starting transfers between devices  27.9 us (7%)
  local copies, waits for them, and re-layouts  13.5 us (4%)
  other arithmetic  10.3 us (3%)
    all_to_all x1, waiting for transfers between devices, body(): lax.all_to_all(feature_send, 'dp', split_axis=1, concat_axis=1, tiled=True)  94 us
    all_to_all x1, waiting for transfers between devices, body(): lax.all_to_all(grad_send, 'dp', split_axis=1, concat_axis=1, tiled=True)  93.4 us
    all_to_all x1, waiting for transfers between devices, body(): lax.all_to_all(partial_out.astype(jnp.bfloat16), 'dp', split_axis=1, conc...  93 us
    dot_general x9, matrix products, matmul(): return jnp.dot(left_mat, right_mat, preferred_element_type=jnp.float32)  19.1 us
    dot_general x8, matrix products, add_group(): jnp.einsum('tsb,tsc->sbc', x_group, g_group, preferred_element_type=jnp.f...  15.6 us
    all_to_all x1, starting transfers between devices, body(): lax.all_to_all(feature_send, 'dp', split_axis=1, concat_axis=1, tiled=True)  12.9 us
  transfers between devices with their start and end apart: 3, of which 3 were waited for; matrix products, arithmetic and copies ran while one was open for 0% of the time, Pallas kernels for 0%

commit v1 on v0

v1 whole, which is shorter than its diff:
```python
import math

import jax
import jax.numpy as jnp
from jax import lax
from jax.experimental import pallas as pl
from jax.experimental.pallas import tpu as pltpu
from jax.sharding import Mesh
from jax.sharding import PartitionSpec as P

BETA = 0.95
DAMPING = 0.0001
FINE = ("z", "yh", "c", "yl", "x")
SIZES = (8, 2, 2, 2, 4)
NZ, NX = 8, 4
DP = ("z", "yh", "c")
OWNER = ("yl", "x")
F32 = jnp.float32
BF16 = jnp.bfloat16
VMEM = pl.BlockSpec(memory_space=pltpu.VMEM)
SMEM = pl.BlockSpec(memory_space=pltpu.SMEM)
RING = (0, -1, -2, -3, 1, 2, 3, 4)
ROW = (0, -1, 1, 2)


def shift(value, axis, step):
    size = SIZES[FINE.index(axis)]
    return lax.ppermute(value, axis, [(i, (i + step) % size) for i in range(size)])


def dot(a, b, dims=((1,), (0,))):
    return lax.dot_general(a, b, (dims, ((), ())), preferred_element_type=F32)


def gradient_kernel(place, *refs):
    own_x, other_x, parts = refs[0:4], refs[4:8], refs[8:17]
    keep, send, blocks = refs[17:20]
    z, x, yh = place[0], place[1], place[2]
    cots = jnp.concatenate([part[...] for part in parts], 0)
    for piece in range(NX):
        feats = []
        for step in RING:
            source = (z + step + NZ) % NZ
            feats += [own_x[piece][source], other_x[piece][source]]
        product = dot(jnp.concatenate(feats, 0), cots, ((0,), (0,)))
        blocks[(x + ROW[piece] + NX) % NX] = product * (1.0 / 4096)
    half = blocks.shape[1]
    for j in range(2):
        keep[pl.ds(j * half, half), :] = blocks[2 * yh + j]
        send[pl.ds(j * half, half), :] = blocks[2 * (1 - yh) + j].astype(BF16)


def eye_mask(order):
    rows = lax.broadcasted_iota(jnp.int32, (order, order), 0)
    cols = lax.broadcasted_iota(jnp.int32, (order, order), 1)
    return rows == cols


def root_of(stat):
    mask = eye_mask(stat.shape[0])
    damped = jnp.where(mask, stat + DAMPING, stat)
    scale = 2.5 / jnp.sqrt(jnp.sum(damped * damped, keepdims=True))
    start = scale * damped
    small = 0.25 * start
    small_b = small.astype(BF16)
    square = dot(small_b, small_b) - 2.5 * small
    square_b = square.astype(BF16)
    fourth = dot(square_b, square_b) + 3.125 * square
    moved = 2.44140625 * start + dot(fourth.astype(BF16), start.astype(BF16))
    small2 = 0.25 * moved
    result = dot(small_b, small2.astype(BF16)) - 1.25 * (small + small2)
    result = jnp.where(mask, result + 1.5625, result)
    return jnp.sqrt(jnp.sqrt(scale)) * result


def step_kernel(
    flag, keep, got, weights, left_stats, right_stats, left_roots, right_roots,
    left_new, right_new, left_root, right_root, update, updated,
):
    grad = keep[...] + got[...].astype(F32)
    grad_b = grad.astype(BF16)
    grad_t = grad_b.T
    left_new[...] = BETA * left_stats[...] + (1.0 - BETA) * dot(grad_b, grad_b, ((1,), (1,)))
    right_new[...] = BETA * right_stats[...] + (1.0 - BETA) * dot(grad_t, grad_t, ((1,), (1,)))

    @pl.when(flag[0] > 0)
    def _():
        left_root[...] = root_of(left_new[...])
        right_root[...] = root_of(right_new[...])

    @pl.when(flag[0] <= 0)
    def _():
        left_root[...] = left_roots[...]
        right_root[...] = right_roots[...]

    inner = dot(left_root[...].astype(BF16), grad_b).astype(BF16)
    direction = dot(inner, right_root[...].astype(BF16))
    total = jnp.sum(direction * direction, keepdims=True)
    direction = direction * (direction.shape[0] / jnp.sqrt(total + 1e-12))
    update[...] = direction
    updated[...] = (weights[...] - (0.25 / math.sqrt(8192)) * direction).astype(BF16)


def query_kernel(place, *refs):
    own_x, other_x = refs[0:4], refs[4:8]
    own_w, other_w, out, rows = refs[8:12]
    z, x, yh = place[0], place[1], place[2]
    half = rows.shape[1]
    for j in range(2):
        rows[2 * yh + j] = own_w[pl.ds(j * half, half), :]
        rows[2 * (1 - yh) + j] = other_w[pl.ds(j * half, half), :]
    weight = jnp.concatenate([rows[(x + step + NX) % NX] for step in ROW], 0)
    for k in range(NZ):
        target = (z + k) % NZ
        tokens = jnp.concatenate(
            [
                jnp.concatenate([piece[target] for piece in own_x], 1),
                jnp.concatenate([piece[target] for piece in other_x], 1),
            ],
            0,
        )
        out[k] = dot(tokens, weight).astype(BF16)


def call(kernel, out_shape, count, scratch=(), limit=32):
    return pl.pallas_call(
        kernel,
        out_shape=out_shape,
        in_specs=[SMEM] + [VMEM] * count,
        out_specs=jax.tree.map(lambda _: VMEM, out_shape),
        scratch_shapes=scratch,
        compiler_params=pltpu.CompilerParams(vmem_limit_bytes=limit * 1024 * 1024),
    )


def body(inputs, out_grads, weights, left_stats, right_stats, left_roots, right_roots, refresh):
    tokens, width = inputs.shape
    block = weights.shape[1]
    z, yh, core, x = (lax.axis_index(name) for name in ("z", "yh", "c", "x"))
    place = jnp.stack([z, x, yh]).astype(jnp.int32)

    low, high = out_grads[:, :block], out_grads[:, block:]
    mine = jnp.where(core == 0, low, high)
    theirs = jnp.where(core == 0, high, low)
    start = jnp.concatenate([mine, shift(theirs, "c", 1)], 0)
    up, down = [start], [start]
    for _ in range(3):
        up.append(shift(up[-1], "z", 1))
        down.append(shift(down[-1], "z", -1))
    far_low = shift(up[-1][:tokens], "z", 1)
    far_high = shift(down[-1][tokens:], "z", -1)
    cots = up + down[1:] + [far_low, far_high]

    quarter = width // (NZ * NX)
    split = inputs.reshape(tokens, NZ, NX, quarter)
    split = lax.dynamic_index_in_dim(split, x, 2, keepdims=False).transpose(1, 0, 2)
    split = lax.all_to_all(split, "z", 0, 0, tiled=True)
    own_x = [split, shift(split, "x", 1), shift(split, "x", -1), shift(split, "x", 2)]
    other_x = [shift(piece, "c", 1) for piece in own_x]

    square = (block, block)
    keep, send = call(
        gradient_kernel,
        (jax.ShapeDtypeStruct(square, F32), jax.ShapeDtypeStruct(square, BF16)),
        17,
        [pltpu.VMEM((NX, quarter, block), F32)],
    )(place, *own_x, *other_x, *cots)
    got = shift(send, "yh", 1)

    full = jax.ShapeDtypeStruct(square, F32)
    left_new, right_new, left_root, right_root, direction, updated = call(
        step_kernel, (full,) * 5 + (jax.ShapeDtypeStruct(square, BF16),), 7
    )(refresh, keep, got, weights[0], left_stats[0], right_stats[0], left_roots[0], right_roots[0])
    neighbour = shift(updated, "yh", 1)

    parts = call(
        query_kernel,
        jax.ShapeDtypeStruct((NZ, 2 * tokens, block), BF16),
        10,
        [pltpu.VMEM((NX, quarter, block), BF16)],
    )(place, *own_x, *other_x, updated, neighbour)

    near_up = shift(parts[1], "z", 1)
    near_down = shift(parts[7], "z", -1)
    up3 = shift(parts[3], "z", 1).astype(F32)
    down3 = shift(parts[5], "z", -1).astype(F32)
    up4 = shift(parts[4, :tokens], "z", 2).astype(F32)
    down4 = shift(parts[4, tokens:], "z", -2).astype(F32)
    up2 = parts[2].astype(F32) + up3
    up2 = jnp.concatenate([up2[:tokens] + up4, up2[tokens:]], 0).astype(BF16)
    down2 = parts[6].astype(F32) + down3
    down2 = jnp.concatenate([down2[:tokens], down2[tokens:] + down4], 0).astype(BF16)
    far_up = shift(up2, "z", 2)
    far_down = shift(down2, "z", -2)
    total = parts[0].astype(F32)
    for part in (near_up, near_down, far_up, far_down):
        total = total + part.astype(F32)
    total = total.astype(BF16)
    mine = total[:tokens]
    theirs = shift(total[tokens:], "c", 1)
    queries = jnp.concatenate(
        [jnp.where(core == 0, mine, theirs), jnp.where(core == 0, theirs, mine)], 1
    )
    return (
        left_new[None],
        right_new[None],
        left_root[None],
        right_root[None],
        direction[None],
        queries,
    )


def solution(mesh):
    fine = Mesh(mesh.devices.reshape(SIZES), FINE)
    blocks = P(DP + OWNER, None, None)
    in_specs = (P(DP, None), P(DP, OWNER)) + (blocks,) * 5 + (P(DP + OWNER),)
    out_specs = (blocks,) * 5 + (P(DP, OWNER),)
    return jax.shard_map(body, mesh=fine, in_specs=in_specs, out_specs=out_specs, check_vma=False)
```

time: 380 us -> 158 us (0.42)
  waiting for transfers between devices: 280 us -> 68.9 us
  matrix products: 41.7 us -> 0 us
  starting transfers between devices: 27.9 us -> 58 us
  Pallas kernels: 0 us -> 10.6 us
  other arithmetic: 10.3 us -> 1.29 us
    all_to_all x3 -> x1, waiting for transfers between devices: 280 us -> 0.01 us  [body(): split = lax.all_to_all(split, 'z', 0, 0, tiled=True)]
    ppermute x0 -> x27, waiting for transfers between devices: none -> 68.9 us  [shift(): lax.ppermute(value, axis, [(i, (i + step) % size) for i in range(size)])]
    ppermute x0 -> x27, starting transfers between devices: none -> 48.9 us  [shift(): lax.ppermute(value, axis, [(i, (i + step) % size) for i in range(size)])]
    dot_general x18 -> x0, matrix products: 41.7 us -> none  [the longest x9 19.1 us: matmul(): return jnp.dot(left_mat, right_mat, preferred_element_type=jnp.float32)]
    all_to_all x3 -> x1, starting transfers between devices: 27.9 us -> 9.01 us  [body(): split = lax.all_to_all(split, 'z', 0, 0, tiled=True)]
    pallas_call x0 -> x3, Pallas kernels: none -> 10.6 us  [the longest x1 3.7 us: body(): call(gradient_kernel, (jax.ShapeDtypeStruct(square, F32), jax.ShapeDtypeS...]
    reduce_sum x10 -> x0, other arithmetic: 6.37 us -> none  [the longest x1 2.87 us: body(): returned.reshape(tok_local, row_blocks, col_blocks, block_size).sum(1)]
    unnamed x16 -> x37, local copies, waits for them, and re-layouts: 5.21 us -> 10.3 us
  transfers between devices with their start and end apart: 3 -> 28, of which waited for: 3 -> 14; matrix products, arithmetic and copies ran while one was open for 0% -> 1% of each run, Pallas kernels for 0% -> 0%
where the time goes in v1:
time: 158 us; the launch traced here: 156 us
  waiting for transfers between devices  68.9 us (44%)
  starting transfers between devices  58 us (37%)
  local copies, waits for them, and re-layouts  15.6 us (10%)
  Pallas kernels  10.6 us (7%)
    ppermute x27, waiting for transfers between devices, shift(): lax.ppermute(value, axis, [(i, (i + step) % size) for i in range(size)])  68.9 us
    ppermute x27, starting transfers between devices, shift(): lax.ppermute(value, axis, [(i, (i + step) % size) for i in range(size)])  48.9 us
    unnamed x37, local copies, waits for them, and re-layouts  10.3 us
    all_to_all x1, starting transfers between devices, body(): split = lax.all_to_all(split, 'z', 0, 0, tiled=True)  9.01 us
    pallas_call x1, Pallas kernels, body(): call(gradient_kernel, (jax.ShapeDtypeStruct(square, F32), jax.ShapeDtypeS...  3.7 us
    pallas_call x1, Pallas kernels, body(): call(query_kernel, jax.ShapeDtypeStruct((NZ, 2 * tokens, block), BF16), 1...  3.61 us
    reshape x1, local copies, waits for them, and re-layouts, body(): split = inputs.reshape(tokens, NZ, NX, quarter)  3.32 us
    pallas_call x1, Pallas kernels, body(): call(step_kernel, (full,) * 5 + (jax.ShapeDtypeStruct(square, BF16),), 7)  3.27 us
  transfers between devices with their start and end apart: 28, of which 14 were waited for; matrix products, arithmetic and copies ran while one was open for 1% of the time, Pallas kernels for 0%

profile of v1, /device:TPU:1, one launch (start us, length us, event | category | flops | bytes accessed | tf_op | source)
XLA Modules:
  0.0 155.8 jit_solution(654093332437985289)
XLA Ops:
  0.6 3.3 %reshape.21 = bf16[128,8,4,256]{3,2,1,0:T(4,128)(2,1)S(1)} reshape(bf16[128,8192]{1,0:T(8,128)(2,1)} %param.8) | data formatting | bytes 4194304 | tf_op jit(solution)/shard_map/reshape | solution.py:155
  6.2 9.0 %all-to-all-start = ((bf16[8,128,256]{2,1,0:T(8,128)(2,1)}), bf16[8,128,256]{2,1,0:T(8,128)(2,1)S(1)}, u32[]{:S(2)}, u32[]{:S(2)}) async-start(bf16[8,128,256]{2,1,0:T(8,128)(2,1)} %bitcast.44), calls=%async_computation | async-start | bytes 1048576 | tf_op jit(solution)/shard_map/all_to_all | solution.py:157
  17.3 3.0 %collective-permute-start.11 = (bf16[256,512]{1,0:T(8,128)(2,1)S(1)}, bf16[256,512]{1,0:T(8,128)(2,1)S(1)}, u32[]{:S(2)}, u32[]{:S(2)}) collective-permute-start(bf16[256,512]{1,0:T(8,128)(2,1)S(1)} %pad_maximum_fusion.refs_8_), channel_id=1, source_target_pairs={{0,224},{32,0},{64,32},{96,64},{128,96},{160,128},{192,160},{224,1... | collective-permute-start | bytes 786440 | tf_op jit(solution)/shard_map/ppermute | solution.py:28
  20.3 13.2 %collective-permute-done.11.refs_12_ = bf16[256,512]{1,0:T(8,128)(2,1)S(1)} collective-permute-done((bf16[256,512]{1,0:T(8,128)(2,1)S(1)}, bf16[256,512]{1,0:T(8,128)(2,1)S(1)}, u32[]{:S(2)}, u32[]{:S(2)}) %collective-permute-start.11) | collective-permute-done | bytes 262176 | tf_op jit(solution)/shard_map/ppermute | solution.py:28
  36.1 2.7 %collective-permute-start.2 = (bf16[8,128,256]{2,1,0:T(8,128)(2,1)S(1)}, bf16[8,128,256]{2,1,0:T(8,128)(2,1)S(1)}, u32[]{:S(2)}, u32[]{:S(2)}) collective-permute-start(bf16[8,128,256]{2,1,0:T(8,128)(2,1)S(1)} %all-to-all-done.refs_0_), channel_id=1, source_target_pairs={{0,2},{1,3},{2,0},{3,1},{4,6},{5,7},{6,4},{7,5},{8,10},{9,11},{10,... | collective-permute-start | bytes 1572872 | tf_op jit(solution)/shard_map/ppermute | solution.py:28
  41.0 2.7 %collective-permute-start.13 = (bf16[256,512]{1,0:T(8,128)(2,1)S(1)}, bf16[256,512]{1,0:T(8,128)(2,1)S(1)}, u32[]{:S(2)}, u32[]{:S(2)}) collective-permute-start(bf16[256,512]{1,0:T(8,128)(2,1)S(1)} %collective-permute-done.12.refs_13_), channel_id=1, source_target_pairs={{0,224},{32,0},{64,32},{96,64},{128,96},{160,128},{192,160},{224,1... | collective-permute-start | bytes 786440 | tf_op jit(solution)/shard_map/ppermute | solution.py:28
  44.4 2.6 %collective-permute-done.9.refs_10_ = bf16[256,512]{1,0:T(8,128)(2,1)S(1)} collective-permute-done((bf16[256,512]{1,0:T(8,128)(2,1)S(1)}, bf16[256,512]{1,0:T(8,128)(2,1)S(1)}, u32[]{:S(2)}, u32[]{:S(2)}) %collective-permute-start.9) | collective-permute-done | bytes 262176 | tf_op jit(solution)/shard_map/ppermute | solution.py:28
  47.1 3.4 %collective-permute-start.3 = (bf16[8,128,256]{2,1,0:T(8,128)(2,1)S(1)}, bf16[8,128,256]{2,1,0:T(8,128)(2,1)S(1)}, u32[]{:S(2)}, u32[]{:S(2)}) collective-permute-start(bf16[8,128,256]{2,1,0:T(8,128)(2,1)S(1)} %all-to-all-done.refs_0_), channel_id=1, source_target_pairs={{0,8},{8,0},{1,9},{9,1},{2,10},{10,2},{3,11},{11,3},{4,12},{12,4},... | collective-permute-start | bytes 1572872 | tf_op jit(solution)/shard_map/ppermute | solution.py:28
  50.4 3.5 %collective-permute-start.6 = (bf16[8,128,256]{2,1,0:T(8,128)(2,1)S(1)}, bf16[8,128,256]{2,1,0:T(8,128)(2,1)S(1)}, u32[]{:S(2)}, u32[]{:S(2)}) collective-permute-start(bf16[8,128,256]{2,1,0:T(8,128)(2,1)S(1)} %collective-permute-done.2.refs_3_), channel_id=1, source_target_pairs={{0,8},{8,0},{1,9},{9,1},{2,10},{10,2},{3,11},{11,3},{4,12},{12,4},... | collective-permute-start | bytes 1572872 | tf_op jit(solution)/shard_map/ppermute | solution.py:28
  54.0 7.8 %collective-permute-done.1.refs_2_ = bf16[8,128,256]{2,1,0:T(8,128)(2,1)S(1)} collective-permute-done((bf16[8,128,256]{2,1,0:T(8,128)(2,1)S(1)}, bf16[8,128,256]{2,1,0:T(8,128)(2,1)S(1)}, u32[]{:S(2)}, u32[]{:S(2)}) %collective-permute-start.1) | collective-permute-done | bytes 524320 | tf_op jit(solution)/shard_map/ppermute | solution.py:28
  68.7 5.3 %collective-permute-done.14.refs_15_ = bf16[128,512]{1,0:T(8,128)(2,1)} collective-permute-done((bf16[128,512]{1,0:T(8,128)(2,1)}, bf16[128,512]{1,0:T(8,128)(2,1)}, u32[]{:S(2)}, u32[]{:S(2)}) %collective-permute-start.14) | collective-permute-done | bytes 131104 | tf_op jit(solution)/shard_map/ppermute | solution.py:28
  79.7 3.7 %shard_map.127 = (f32[512,512]{1,0:T(8,128)S(1)}, bf16[512,512]{1,0:T(8,128)(2,1)S(1)}) custom-call(s32[3]{0:T(128)S(1)} %pad_add_fusion.place, bf16[8,128,256]{2,1,0:T(8,128)(2,1)S(1)} %all-to-all-done.refs_0_, bf16[8,128,256]{2,1,0:T(8,128)(2,1)S(1)} %collective-permute-done.refs_1_, bf16[8,128,256]{2,1,0:T(8,128)(2,1)S(1)} %collective-permute-done.1.refs_2_, ...), custom_call_target="tpu_custom_call" | custom-call | tf_op jit(solution)/shard_map/pallas_call | solution.py:162
  83.4 3.0 %collective-permute-start.16 = (bf16[512,512]{1,0:T(8,128)(2,1)S(1)}, bf16[512,512]{1,0:T(8,128)(2,1)S(1)}, u32[]{:S(2)}, u32[]{:S(2)}) collective-permute-start(bf16[512,512]{1,0:T(8,128)(2,1)S(1)} %get-tuple-element.15), channel_id=1, source_target_pairs={{0,16},{16,0},{1,17},{17,1},{2,18},{18,2},{3,19},{19,3},{4,20},{20... | collective-permute-start | bytes 1572872 | tf_op jit(solution)/shard_map/ppermute | solution.py:28
  87.1 8.9 %collective-permute-done.16.got = bf16[512,512]{1,0:T(8,128)(2,1)S(1)} collective-permute-done((bf16[512,512]{1,0:T(8,128)(2,1)S(1)}, bf16[512,512]{1,0:T(8,128)(2,1)S(1)}, u32[]{:S(2)}, u32[]{:S(2)}) %collective-permute-start.16) | collective-permute-done | bytes 524320 | tf_op jit(solution)/shard_map/ppermute | solution.py:28
  96.0 3.3 %shard_map.128 = (f32[512,512]{1,0:T(8,128)}, f32[512,512]{1,0:T(8,128)}, f32[512,512]{1,0:T(8,128)}, f32[512,512]{1,0:T(8,128)}, f32[512,512]{1,0:T(8,128)}, /*index=5*/bf16[512,512]{1,0:T(8,128)(2,1)S(1)}) custom-call(s32[1]{0:T(128)S(6)} %copy.18.flag, f32[512,512]{1,0:T(8,128)S(1)} %get-tuple-element.14.keep, ...), custom_call_target="tpu_custom_call" | custom-call | tf_op jit(solution)/shard_map/pallas_call | solution.py:171
  99.2 6.4 %collective-permute-start.17 = (bf16[512,512]{1,0:T(8,128)(2,1)S(1)}, bf16[512,512]{1,0:T(8,128)(2,1)S(1)}, u32[]{:S(2)}, u32[]{:S(2)}) collective-permute-start(bf16[512,512]{1,0:T(8,128)(2,1)S(1)} %get-tuple-element.21.refs_8_), channel_id=1, source_target_pairs={{0,16},{16,0},{1,17},{17,1},{2,18},{18,2},{3,19},{19,3},{4,20},{20... | collective-permute-start | bytes 1572872 | tf_op jit(solution)/shard_map/ppermute | solution.py:28
  105.6 8.5 %collective-permute-done.17.refs_9_ = bf16[512,512]{1,0:T(8,128)(2,1)S(1)} collective-permute-done((bf16[512,512]{1,0:T(8,128)(2,1)S(1)}, bf16[512,512]{1,0:T(8,128)(2,1)S(1)}, u32[]{:S(2)}, u32[]{:S(2)}) %collective-permute-start.17) | collective-permute-done | bytes 524320 | tf_op jit(solution)/shard_map/ppermute | solution.py:28
  114.1 3.6 %shard_map.129 = bf16[8,256,512]{2,1,0:T(8,128)(2,1)S(1)} custom-call(s32[3]{0:T(128)S(1)} %pad_add_fusion.place, bf16[8,128,256]{2,1,0:T(8,128)(2,1)S(1)} %all-to-all-done.refs_0_, bf16[8,128,256]{2,1,0:T(8,128)(2,1)S(1)} %collective-permute-done.refs_1_, bf16[8,128,256]{2,1,0:T(8,128)(2,1)S(1)} %collective-permute-done.1.refs_2_, ...), custom_call_target="tpu_custom_call" | custom-call | tf_op jit(solution)/shard_map/pallas_call | solution.py:176
  119.4 5.3 %collective-permute-start.21 = (bf16[128,512]{1,0:T(8,128)(2,1)S(1)}, bf16[128,512]{1,0:T(8,128)(2,1)S(1)}, u32[]{:S(2)}, u32[]{:S(2)}) collective-permute-start(bf16[128,512]{1,0:T(8,128)(2,1)S(1)} %get-tuple-element.26), channel_id=1, source_target_pairs={{0,64},{32,96},{64,128},{96,160},{128,192},{160,224},{192,0},{224,... | collective-permute-start | bytes 393224 | tf_op jit(solution)/shard_map/ppermute | solution.py:28
  125.1 2.3 %collective-permute-start.18 = (bf16[256,512]{1,0:T(8,128)(2,1)S(1)}, bf16[256,512]{1,0:T(8,128)(2,1)S(1)}, u32[]{:S(2)}, u32[]{:S(2)}) collective-permute-start(bf16[256,512]{1,0:T(8,128)(2,1)S(1)} %get-tuple-element.22), channel_id=1, source_target_pairs={{0,32},{32,64},{64,96},{96,128},{128,160},{160,192},{192,224},{224... | collective-permute-start | bytes 786440 | tf_op jit(solution)/shard_map/ppermute | solution.py:28
  127.9 5.3 %collective-permute-done.24 = bf16[128,512]{1,0:T(8,128)(2,1)S(1)} collective-permute-done((bf16[128,512]{1,0:T(8,128)(2,1)S(1)}, bf16[128,512]{1,0:T(8,128)(2,1)S(1)}, u32[]{:S(2)}, u32[]{:S(2)}) %collective-permute-start.24) | collective-permute-done | bytes 131104 | tf_op jit(solution)/shard_map/ppermute | solution.py:28
  133.3 2.3 %collective-permute-start.25 = (bf16[256,512]{1,0:T(8,128)(2,1)S(1)}, bf16[256,512]{1,0:T(8,128)(2,1)S(1)}, u32[]{:S(2)}, u32[]{:S(2)}) collective-permute-start(bf16[256,512]{1,0:T(8,128)(2,1)S(1)} %pad_maximum_fusion.2), channel_id=1, source_target_pairs={{0,192},{32,224},{64,0},{96,32},{128,64},{160,96},{192,128},{224,1... | collective-permute-start | bytes 786440 | tf_op jit(solution)/shard_map/ppermute | solution.py:28
  138.6 11.9 %collective-permute-done.25 = bf16[256,512]{1,0:T(8,128)(2,1)S(1)} collective-permute-done((bf16[256,512]{1,0:T(8,128)(2,1)S(1)}, bf16[256,512]{1,0:T(8,128)(2,1)S(1)}, u32[]{:S(2)}, u32[]{:S(2)}) %collective-permute-start.25) | collective-permute-done | bytes 262176 | tf_op jit(solution)/shard_map/ppermute | solution.py:28
  150.7 3.4 %collective-permute-start.26 = (bf16[128,512]{1,0:T(8,128)(2,1)S(1)}, bf16[128,512]{1,0:T(8,128)(2,1)S(1)}, u32[]{:S(2)}, u32[]{:S(2)}) collective-permute-start(bf16[128,512]{1,0:T(8,128)(2,1)S(1)} %slice.94), channel_id=1, source_target_pairs={{0,8},{8,0},{1,9},{9,1},{2,10},{10,2},{3,11},{11,3},{4,12},{12,4},... | collective-permute-start | bytes 393224 | tf_op jit(solution)/shard_map/ppermute | solution.py:28
  (92 shorter events, 30.0 us)
Async XLA Ops:
  6.2 29.9 %all-to-all-start = ((bf16[8,128,256]{2,1,0:T(8,128)(2,1)}), bf16[8,128,256]{2,1,0:T(8,128)(2,1)S(1)}, u32[]{:S(2)}, u32[]{:S(2)}) async-start(bf16[8,128,256]{2,1,0:T(8,128)(2,1)} %bitcast.44), calls=%async_computation | async-start | bytes 1048576 | tf_op jit(solution)/shard_map/all_to_all | solution.py:157
  17.3 16.2 %collective-permute-start.11 = (bf16[256,512]{1,0:T(8,128)(2,1)S(1)}, bf16[256,512]{1,0:T(8,128)(2,1)S(1)}, u32[]{:S(2)}, u32[]{:S(2)}) collective-permute-start(bf16[256,512]{1,0:T(8,128)(2,1)S(1)} %pad_maximum_fusion.refs_8_), channel_id=1, source_target_pairs={{0,224},{32,0},{64,32},{96,64},{128,96},{160,128},{192,160},{224,1... | collective-permute-start | bytes 786440 | tf_op jit(solution)/shard_map/ppermute | solution.py:28
  20.3 20.0 %collective-permute-start.8 = (bf16[256,512]{1,0:T(8,128)(2,1)S(1)}, bf16[256,512]{1,0:T(8,128)(2,1)S(1)}, u32[]{:S(2)}, u32[]{:S(2)}) collective-permute-start(bf16[256,512]{1,0:T(8,128)(2,1)S(1)} %pad_maximum_fusion.refs_8_), channel_id=1, source_target_pairs={{0,32},{32,64},{64,96},{96,128},{128,160},{160,192},{192,224},{224... | collective-permute-start | bytes 786440 | tf_op jit(solution)/shard_map/ppermute | solution.py:28
  33.5 7.5 %collective-permute-start.12 = (bf16[256,512]{1,0:T(8,128)(2,1)S(1)}, bf16[256,512]{1,0:T(8,128)(2,1)S(1)}, u32[]{:S(2)}, u32[]{:S(2)}) collective-permute-start(bf16[256,512]{1,0:T(8,128)(2,1)S(1)} %collective-permute-done.11.refs_12_), channel_id=1, source_target_pairs={{0,224},{32,0},{64,32},{96,64},{128,96},{160,128},{192,160},{224,1... | collective-permute-start | bytes 786440 | tf_op jit(solution)/shard_map/ppermute | solution.py:28
  36.1 14.3 %collective-permute-start.2 = (bf16[8,128,256]{2,1,0:T(8,128)(2,1)S(1)}, bf16[8,128,256]{2,1,0:T(8,128)(2,1)S(1)}, u32[]{:S(2)}, u32[]{:S(2)}) collective-permute-start(bf16[8,128,256]{2,1,0:T(8,128)(2,1)S(1)} %all-to-all-done.refs_0_), channel_id=1, source_target_pairs={{0,2},{1,3},{2,0},{3,1},{4,6},{5,7},{6,4},{7,5},{8,10},{9,11},{10,... | collective-permute-start | bytes 1572872 | tf_op jit(solution)/shard_map/ppermute | solution.py:28
  38.9 22.9 %collective-permute-start.1 = (bf16[8,128,256]{2,1,0:T(8,128)(2,1)S(1)}, bf16[8,128,256]{2,1,0:T(8,128)(2,1)S(1)}, u32[]{:S(2)}, u32[]{:S(2)}) collective-permute-start(bf16[8,128,256]{2,1,0:T(8,128)(2,1)S(1)} %all-to-all-done.refs_0_), channel_id=1, source_target_pairs={{0,3},{1,0},{2,1},{3,2},{4,7},{5,4},{6,5},{7,6},{8,11},{9,8},{10,9... | collective-permute-start | bytes 1572872 | tf_op jit(solution)/shard_map/ppermute | solution.py:28
  39.7 23.6 %collective-permute-start = (bf16[8,128,256]{2,1,0:T(8,128)(2,1)S(1)}, bf16[8,128,256]{2,1,0:T(8,128)(2,1)S(1)}, u32[]{:S(2)}, u32[]{:S(2)}) collective-permute-start(bf16[8,128,256]{2,1,0:T(8,128)(2,1)S(1)} %all-to-all-done.refs_0_), channel_id=1, source_target_pairs={{0,1},{1,2},{2,3},{3,0},{4,5},{5,6},{6,7},{7,4},{8,9},{9,10},{10,1... | collective-permute-start | bytes 1572872 | tf_op jit(solution)/shard_map/ppermute | solution.py:28
  40.3 6.7 %collective-permute-start.9 = (bf16[256,512]{1,0:T(8,128)(2,1)S(1)}, bf16[256,512]{1,0:T(8,128)(2,1)S(1)}, u32[]{:S(2)}, u32[]{:S(2)}) collective-permute-start(bf16[256,512]{1,0:T(8,128)(2,1)S(1)} %collective-permute-done.8.refs_9_), channel_id=1, source_target_pairs={{0,32},{32,64},{64,96},{96,128},{128,160},{160,192},{192,224},{224... | collective-permute-start | bytes 786440 | tf_op jit(solution)/shard_map/ppermute | solution.py:28
  41.0 6.0 %collective-permute-start.13 = (bf16[256,512]{1,0:T(8,128)(2,1)S(1)}, bf16[256,512]{1,0:T(8,128)(2,1)S(1)}, u32[]{:S(2)}, u32[]{:S(2)}) collective-permute-start(bf16[256,512]{1,0:T(8,128)(2,1)S(1)} %collective-permute-done.12.refs_13_), channel_id=1, source_target_pairs={{0,224},{32,0},{64,32},{96,64},{128,96},{160,128},{192,160},{224,1... | collective-permute-start | bytes 786440 | tf_op jit(solution)/shard_map/ppermute | solution.py:28
  47.1 17.0 %collective-permute-start.10 = (bf16[256,512]{1,0:T(8,128)(2,1)S(1)}, bf16[256,512]{1,0:T(8,128)(2,1)S(1)}, u32[]{:S(2)}, u32[]{:S(2)}) collective-permute-start(bf16[256,512]{1,0:T(8,128)(2,1)S(1)} %collective-permute-done.9.refs_10_), channel_id=1, source_target_pairs={{0,32},{32,64},{64,96},{96,128},{128,160},{160,192},{192,224},{224... | collective-permute-start | bytes 786440 | tf_op jit(solution)/shard_map/ppermute | solution.py:28
  47.1 26.9 %collective-permute-start.3 = (bf16[8,128,256]{2,1,0:T(8,128)(2,1)S(1)}, bf16[8,128,256]{2,1,0:T(8,128)(2,1)S(1)}, u32[]{:S(2)}, u32[]{:S(2)}) collective-permute-start(bf16[8,128,256]{2,1,0:T(8,128)(2,1)S(1)} %all-to-all-done.refs_0_), channel_id=1, source_target_pairs={{0,8},{8,0},{1,9},{9,1},{2,10},{10,2},{3,11},{11,3},{4,12},{12,4},... | collective-permute-start | bytes 1572872 | tf_op jit(solution)/shard_map/ppermute | solution.py:28
  50.4 23.5 %collective-permute-start.6 = (bf16[8,128,256]{2,1,0:T(8,128)(2,1)S(1)}, bf16[8,128,256]{2,1,0:T(8,128)(2,1)S(1)}, u32[]{:S(2)}, u32[]{:S(2)}) collective-permute-start(bf16[8,128,256]{2,1,0:T(8,128)(2,1)S(1)} %collective-permute-done.2.refs_3_), channel_id=1, source_target_pairs={{0,8},{8,0},{1,9},{9,1},{2,10},{10,2},{3,11},{11,3},{4,12},{12,4},... | collective-permute-start | bytes 1572872 | tf_op jit(solution)/shard_map/ppermute | solution.py:28
  61.8 12.2 %collective-permute-start.5 = (bf16[8,128,256]{2,1,0:T(8,128)(2,1)S(1)}, bf16[8,128,256]{2,1,0:T(8,128)(2,1)}, u32[]{:S(2)}, u32[]{:S(2)}) collective-permute-start(bf16[8,128,256]{2,1,0:T(8,128)(2,1)S(1)} %collective-permute-done.1.refs_2_), channel_id=1, source_target_pairs={{0,8},{8,0},{1,9},{9,1},{2,10},{10,2},{3,11},{11,3},{4,12},{12,4},... | collective-permute-start | bytes 1572872 | tf_op jit(solution)/shard_map/ppermute | solution.py:28
  63.3 10.7 %collective-permute-start.4 = (bf16[8,128,256]{2,1,0:T(8,128)(2,1)S(1)}, bf16[8,128,256]{2,1,0:T(8,128)(2,1)}, u32[]{:S(2)}, u32[]{:S(2)}) collective-permute-start(bf16[8,128,256]{2,1,0:T(8,128)(2,1)S(1)} %collective-permute-done.refs_1_), channel_id=1, source_target_pairs={{0,8},{8,0},{1,9},{9,1},{2,10},{10,2},{3,11},{11,3},{4,12},{12,4},... | collective-permute-start | bytes 1572872 | tf_op jit(solution)/shard_map/ppermute | solution.py:28
  83.4 12.5 %collective-permute-start.16 = (bf16[512,512]{1,0:T(8,128)(2,1)S(1)}, bf16[512,512]{1,0:T(8,128)(2,1)S(1)}, u32[]{:S(2)}, u32[]{:S(2)}) collective-permute-start(bf16[512,512]{1,0:T(8,128)(2,1)S(1)} %get-tuple-element.15), channel_id=1, source_target_pairs={{0,16},{16,0},{1,17},{17,1},{2,18},{18,2},{3,19},{19,3},{4,20},{20... | collective-permute-start | bytes 1572872 | tf_op jit(solution)/shard_map/ppermute | solution.py:28
  99.2 14.9 %collective-permute-start.17 = (bf16[512,512]{1,0:T(8,128)(2,1)S(1)}, bf16[512,512]{1,0:T(8,128)(2,1)S(1)}, u32[]{:S(2)}, u32[]{:S(2)}) collective-permute-start(bf16[512,512]{1,0:T(8,128)(2,1)S(1)} %get-tuple-element.21.refs_8_), channel_id=1, source_target_pairs={{0,16},{16,0},{1,17},{17,1},{2,18},{18,2},{3,19},{19,3},{4,20},{20... | collective-permute-start | bytes 1572872 | tf_op jit(solution)/shard_map/ppermute | solution.py:28
  117.8 9.5 %collective-permute-start.23 = (bf16[256,512]{1,0:T(8,128)(2,1)S(1)}, bf16[256,512]{1,0:T(8,128)(2,1)S(1)}, u32[]{:S(2)}, u32[]{:S(2)}) collective-permute-start(bf16[256,512]{1,0:T(8,128)(2,1)S(1)} %get-tuple-element.23), channel_id=1, source_target_pairs={{0,224},{32,0},{64,32},{96,64},{128,96},{160,128},{192,160},{224,1... | collective-permute-start | bytes 786440 | tf_op jit(solution)/shard_map/ppermute | solution.py:28
  117.9 9.8 %collective-permute-start.20 = (bf16[256,512]{1,0:T(8,128)(2,1)S(1)}, bf16[256,512]{1,0:T(8,128)(2,1)S(1)}, u32[]{:S(2)}, u32[]{:S(2)}) collective-permute-start(bf16[256,512]{1,0:T(8,128)(2,1)S(1)} %get-tuple-element.24), channel_id=1, source_target_pairs={{0,32},{32,64},{64,96},{96,128},{128,160},{160,192},{192,224},{224... | collective-permute-start | bytes 786440 | tf_op jit(solution)/shard_map/ppermute | solution.py:28
  119.4 16.2 %collective-permute-start.21 = (bf16[128,512]{1,0:T(8,128)(2,1)S(1)}, bf16[128,512]{1,0:T(8,128)(2,1)S(1)}, u32[]{:S(2)}, u32[]{:S(2)}) collective-permute-start(bf16[128,512]{1,0:T(8,128)(2,1)S(1)} %get-tuple-element.26), channel_id=1, source_target_pairs={{0,64},{32,96},{64,128},{96,160},{128,192},{160,224},{192,0},{224,... | collective-permute-start | bytes 393224 | tf_op jit(solution)/shard_map/ppermute | solution.py:28
  124.7 8.6 %collective-permute-start.24 = (bf16[128,512]{1,0:T(8,128)(2,1)S(1)}, bf16[128,512]{1,0:T(8,128)(2,1)S(1)}, u32[]{:S(2)}, u32[]{:S(2)}) collective-permute-start(bf16[128,512]{1,0:T(8,128)(2,1)S(1)} %get-tuple-element.27), channel_id=1, source_target_pairs={{0,192},{32,224},{64,0},{96,32},{128,64},{160,96},{192,128},{224,1... | collective-permute-start | bytes 393224 | tf_op jit(solution)/shard_map/ppermute | solution.py:28
  125.1 12.4 %collective-permute-start.18 = (bf16[256,512]{1,0:T(8,128)(2,1)S(1)}, bf16[256,512]{1,0:T(8,128)(2,1)S(1)}, u32[]{:S(2)}, u32[]{:S(2)}) collective-permute-start(bf16[256,512]{1,0:T(8,128)(2,1)S(1)} %get-tuple-element.22), channel_id=1, source_target_pairs={{0,32},{32,64},{64,96},{96,128},{128,160},{160,192},{192,224},{224... | collective-permute-start | bytes 786440 | tf_op jit(solution)/shard_map/ppermute | solution.py:28
  127.4 11.2 %collective-permute-start.19 = (bf16[256,512]{1,0:T(8,128)(2,1)S(1)}, bf16[256,512]{1,0:T(8,128)(2,1)S(1)}, u32[]{:S(2)}, u32[]{:S(2)}) collective-permute-start(bf16[256,512]{1,0:T(8,128)(2,1)S(1)} %get-tuple-element.25), channel_id=1, source_target_pairs={{0,224},{32,0},{64,32},{96,64},{128,96},{160,128},{192,160},{224,1... | collective-permute-start | bytes 786440 | tf_op jit(solution)/shard_map/ppermute | solution.py:28
  133.3 17.1 %collective-permute-start.25 = (bf16[256,512]{1,0:T(8,128)(2,1)S(1)}, bf16[256,512]{1,0:T(8,128)(2,1)S(1)}, u32[]{:S(2)}, u32[]{:S(2)}) collective-permute-start(bf16[256,512]{1,0:T(8,128)(2,1)S(1)} %pad_maximum_fusion.2), channel_id=1, source_target_pairs={{0,192},{32,224},{64,0},{96,32},{128,64},{160,96},{192,128},{224,1... | collective-permute-start | bytes 786440 | tf_op jit(solution)/shard_map/ppermute | solution.py:28
  135.7 14.9 %collective-permute-start.22 = (bf16[256,512]{1,0:T(8,128)(2,1)S(1)}, bf16[256,512]{1,0:T(8,128)(2,1)S(1)}, u32[]{:S(2)}, u32[]{:S(2)}) collective-permute-start(bf16[256,512]{1,0:T(8,128)(2,1)S(1)} %pad_maximum_fusion.1), channel_id=1, source_target_pairs={{0,64},{32,96},{64,128},{96,160},{128,192},{160,224},{192,0},{224,... | collective-permute-start | bytes 786440 | tf_op jit(solution)/shard_map/ppermute | solution.py:28
  (22 other events, 192.2 us)

commit v2 on v1

v2 whole, which is shorter than its diff:
```python
import math
from functools import partial

import jax
import jax.numpy as jnp
from jax import lax
from jax.experimental import pallas as pl
from jax.experimental.pallas import tpu as pltpu
from jax.sharding import Mesh
from jax.sharding import PartitionSpec as P

BETA = 0.95
DAMPING = 0.0001
FINE = ("z", "yh", "c", "yl", "x")
SIZES = (8, 2, 2, 2, 4)
NZ, NX = 8, 4
DP = ("z", "yh", "c")
OWNER = ("yl", "x")
F32 = jnp.float32
BF16 = jnp.bfloat16
VMEM = pl.BlockSpec(memory_space=pltpu.VMEM)
SMEM = pl.BlockSpec(memory_space=pltpu.SMEM)
ANY = pl.BlockSpec(memory_space=pl.ANY)
HBM = pl.BlockSpec(memory_space=pltpu.HBM)
RING = (0, -1, -2, -3, 1, 2, 3)
NEAR = (2, 6, 1, 7, 0)
ROW = (0, -1, 1, 2)


def shift(value, axis, step):
    size = SIZES[FINE.index(axis)]
    return lax.ppermute(value, axis, [(i, (i + step) % size) for i in range(size)])


def dot(a, b, dims=((1,), (0,))):
    return lax.dot_general(a, b, (dims, ((), ())), preferred_element_type=F32)


def tie(*values):
    return lax.optimization_barrier(values)


def feature_kernel(place, inputs, out, sems):
    x = place[1]
    copies = []
    for target in range(NZ):
        for j in range(2):
            column = pl.multiple_of((2 * target + j) * 512 + x * 128, 128)
            copy = pltpu.make_async_copy(
                inputs.at[:, pl.ds(column, 128)],
                out.at[target, :, pl.ds(j * 128, 128)],
                sems.at[2 * target + j],
            )
            copy.start()
            copies.append(copy)
    for copy in copies:
        copy.wait()


def copies_of(pairs, sems):
    copies = [
        pltpu.make_async_copy(source, target, sems.at[i]) for i, (source, target) in enumerate(pairs)
    ]
    for copy in copies:
        copy.start()
    return copies


def gradient_kernel(place, *refs):
    own_x, other_x, parts = refs[0:3], refs[3:6], refs[6:13]
    sums, feats, cots, sems = refs[13:17]
    z = place[0]
    pairs = [(part, cots.at[(z + step + NZ) % NZ]) for part, step in zip(parts, RING)]
    for piece in range(3):
        pairs.append((own_x[piece], feats.at[piece, :, 0]))
        pairs.append((other_x[piece], feats.at[piece, :, 1]))
    copies = copies_of(pairs, sems)
    cots[(z + 4) % NZ] = jnp.zeros(cots.shape[1:], BF16)
    for copy in copies[:7]:
        copy.wait()
    tokens = cots.shape[0] * cots.shape[1] * cots.shape[2]
    right = cots[...].reshape(tokens, cots.shape[3])
    for piece in range(3):
        copies[7 + 2 * piece].wait()
        copies[8 + 2 * piece].wait()
        left = feats[piece].reshape(tokens, feats.shape[4])
        sums[piece] = dot(left, right, ((0,), (0,)))


def put(total, yh, piece, keep, send):
    total = total * (1.0 / 4096)
    upper, lower = total[:128], total[128:]
    keep[piece] = jnp.where(yh == 0, upper, lower)
    send[piece] = jnp.where(yh == 0, lower, upper).astype(BF16)


def far_gradient_kernel(place, sums, feats, low, high, keep, send, cots, sems):
    copies = copies_of([(low, cots.at[0]), (high, cots.at[1])], sems)
    z, yh = place[0], place[2]
    for copy in copies:
        copy.wait()
    right = cots[...].reshape(256, cots.shape[2])
    for piece in range(3):
        left = feats[piece, (z + 4) % NZ].reshape(256, feats.shape[4])
        put(sums[piece] + dot(left, right, ((0,), (0,))), yh, piece, keep, send)


def last_gradient_kernel(place, own_r, own_l, other_r, other_l, cots, far, keep, send, feats, sems):
    half = NZ // 2
    copies = copies_of(
        [
            (own_r, feats.at[0, :half, 0]),
            (own_l, feats.at[0, half:, 0]),
            (other_r, feats.at[0, :half, 1]),
            (other_l, feats.at[0, half:, 1]),
        ],
        sems,
    )
    z, yh = place[0], place[2]
    tokens = cots.shape[0] * cots.shape[1] * cots.shape[2]
    for copy in copies:
        copy.wait()
    total = dot(
        feats[0].reshape(tokens, feats.shape[4]),
        cots[...].reshape(tokens, cots.shape[3]),
        ((0,), (0,)),
    )
    left = feats[0, (z + 4) % NZ].reshape(256, feats.shape[4])
    total = total + dot(left, far[...].reshape(256, far.shape[2]), ((0,), (0,)))
    put(total, yh, 0, keep, send)


def eye_mask(order):
    rows = lax.broadcasted_iota(jnp.int32, (order, order), 0)
    cols = lax.broadcasted_iota(jnp.int32, (order, order), 1)
    return rows == cols


def roots_of(stats):
    mask = eye_mask(stats[0].shape[0])
    damped = [jnp.where(mask, stat + DAMPING, stat) for stat in stats]
    scale = [2.5 / jnp.sqrt(jnp.sum(value * value, keepdims=True)) for value in damped]
    start = [a * b for a, b in zip(scale, damped)]
    start_b = [value.astype(BF16) for value in start]
    small = [0.25 * value for value in start]
    small_b = [value.astype(BF16) for value in small]
    square = [dot(b, b) - 2.5 * a for a, b in zip(small, small_b)]
    square_b = [value.astype(BF16) for value in square]
    fourth = [(dot(b, b) + 3.125 * a).astype(BF16) for a, b in zip(square, square_b)]
    moved = [2.44140625 * a + dot(c, b) for a, b, c in zip(start, start_b, fourth)]
    small2 = [0.25 * value for value in moved]
    small2_b = [value.astype(BF16) for value in small2]
    result = [
        dot(b, d) - 1.25 * (a + c) for a, b, c, d in zip(small, small_b, small2, small2_b)
    ]
    result = [jnp.where(mask, value + 1.5625, value) for value in result]
    return [jnp.sqrt(jnp.sqrt(a)) * b for a, b in zip(scale, result)]


def step_kernel(
    flag, place, keep3, keep1, got3, got1, weights, left_stats, right_stats, left_roots, right_roots,
    left_new, right_new, left_root, right_root, update, low_cols, high_cols, rows,
):
    x = place[1]
    for piece, step in enumerate(ROW):
        if piece < 3:
            value = keep3[piece] + got3[piece].astype(F32)
        else:
            value = keep1[0] + got1[0].astype(F32)
        rows[(x + step + NX) % NX] = value
    grad = rows[...].reshape(weights.shape)
    grad_b = grad.astype(BF16)
    grad_t = grad_b.T
    left_new[...] = BETA * left_stats[...] + (1.0 - BETA) * dot(grad_b, grad_b, ((1,), (1,)))
    right_new[...] = BETA * right_stats[...] + (1.0 - BETA) * dot(grad_t, grad_t, ((1,), (1,)))

    @pl.when(flag[0] > 0)
    def _():
        left_root[...], right_root[...] = roots_of((left_new[...], right_new[...]))

    @pl.when(flag[0] <= 0)
    def _():
        left_root[...] = left_roots[...]
        right_root[...] = right_roots[...]

    inner = dot(left_root[...].astype(BF16), grad_b).astype(BF16)
    direction = dot(inner, right_root[...].astype(BF16))
    total = jnp.sum(direction * direction, keepdims=True)
    direction = direction * (direction.shape[0] / jnp.sqrt(total + 1e-12))
    update[...] = direction
    updated = (weights[...] - (0.25 / math.sqrt(8192)) * direction).astype(BF16)
    low_cols[...] = updated[:, :256]
    high_cols[...] = updated[:, 256:]


def query_parts(place, feats3, feats1, own_w, other_w, rows):
    z, x, yh = place[0], place[1], place[2]
    for q in range(NX):
        rows[q, yh] = own_w[pl.ds(q * 128, 128), :]
        rows[q, 1 - yh] = other_w[pl.ds(q * 128, 128), :]
    weight = jnp.concatenate(
        [rows[(x + step + NX) % NX].reshape(256, rows.shape[3]) for step in ROW], 0
    )

    def part(k):
        target = (z + k) % NZ
        pieces = [feats3[piece, target] for piece in range(3)] + [feats1[0, target]]
        tokens = jnp.concatenate([piece.reshape(256, 256) for piece in pieces], 1)
        return dot(tokens, weight).astype(BF16)

    return part


def low_query_kernel(place, feats3, feats1, own_w, other_w, out, rows):
    part = query_parts(place, feats3, feats1, own_w, other_w, rows)
    for k in range(NZ):
        out[k] = part(k)


def high_query_kernel(
    place, feats3, feats1, own_w, other_w, low, up3, down3, up4, down4, up2, down2, up1, down1, here, rows
):
    part = query_parts(place, feats3, feats1, own_w, other_w, rows)
    for k, out in ((3, up3), (5, down3)):
        out[:, :256] = low[k]
        out[:, 256:] = part(k)
    both = part(4)
    up4[:, :256] = low[4, :128]
    up4[:, 256:] = both[:128]
    down4[:, :256] = low[4, 128:]
    down4[:, 256:] = both[128:]
    for k, out in zip(NEAR, (up2, down2, up1, down1, here)):
        out[:, :256] = low[k]
        out[:, 256:] = part(k)


def relay_kernel(half, mine, three, four, out):
    total = mine[...].astype(F32) + three[...].astype(F32)
    for i in range(2):
        value = total[i * 128 : i * 128 + 128]
        if i == half:
            value = value + four[...].astype(F32)
        out[pl.ds(i * 128, 128), :] = value.astype(BF16)


def call(kernel, out_shape, in_specs, out_specs=None, scratch=(), cost=None, limit=40):
    if out_specs is None:
        out_specs = jax.tree.map(lambda _: VMEM, out_shape)
    if cost is not None:
        cost = pl.CostEstimate(flops=cost[0], bytes_accessed=cost[1], transcendentals=0)
    return pl.pallas_call(
        kernel,
        out_shape=out_shape,
        in_specs=in_specs,
        out_specs=out_specs,
        scratch_shapes=scratch,
        cost_estimate=cost,
        compiler_params=pltpu.CompilerParams(vmem_limit_bytes=limit * 1024 * 1024),
    )


def body(inputs, out_grads, weights, left_stats, right_stats, left_roots, right_roots, refresh):
    tokens, width = inputs.shape
    block = weights.shape[1]
    z, yh, core, x = (lax.axis_index(name) for name in ("z", "yh", "c", "x"))
    place = jnp.stack([z, x, yh]).astype(jnp.int32)

    quarter = width // (NZ * NX)
    split = call(
        feature_kernel,
        jax.ShapeDtypeStruct((NZ, tokens, quarter), BF16),
        [SMEM, HBM],
        VMEM,
        [pltpu.SemaphoreType.DMA((2 * NZ,))],
    )(place, pltpu.with_memory_space_constraint(inputs, pltpu.HBM))

    low, high = out_grads[:, :block], out_grads[:, block:]
    mine = jnp.where(core == 0, low, high)
    theirs = jnp.where(core == 0, high, low)
    start = jnp.stack([mine, shift(theirs, "c", 1)], 0)
    up1, down1 = shift(start, "z", 1), shift(start, "z", -1)
    split = lax.all_to_all(split, "z", 0, 0, tiled=True)
    up1, down1, split = tie(up1, down1, split)
    right, left = shift(split, "x", 1), shift(split, "x", -1)
    other0 = shift(split, "c", 1)
    up2, down2 = shift(up1, "z", 1), shift(down1, "z", -1)
    up2, down2 = tie(up2, down2)
    up3, down3 = tie(shift(up2, "z", 1), shift(down2, "z", -1))
    far_low, far_high = shift(up3[0], "z", 1), shift(down3[1], "z", -1)
    other1, other2 = shift(right, "c", 1), shift(left, "c", 1)
    across_r = shift(right[: NZ // 2], "x", 1)
    across_l = shift(left[NZ // 2 :], "x", -1)

    feat_shape = (NZ, 2, tokens, quarter)
    cot_shape = (NZ, 2, tokens, block)
    sums, feats3, cots = call(
        gradient_kernel,
        (
            jax.ShapeDtypeStruct((3, quarter, block), F32),
            jax.ShapeDtypeStruct((3,) + feat_shape, BF16),
            jax.ShapeDtypeStruct(cot_shape, BF16),
        ),
        [SMEM] + [ANY] * 13,
        scratch=[pltpu.SemaphoreType.DMA((13,))],
        cost=(2 * NZ * 2 * tokens * 3 * quarter * block, 6 << 20),
    )(
        place, split, right, left, other0, other1, other2,
        start, up1, up2, up3, down1, down2, down3,
    )
    keep3, send3 = call(
        far_gradient_kernel,
        (
            jax.ShapeDtypeStruct((3, 128, block), F32),
            jax.ShapeDtypeStruct((3, 128, block), BF16),
        ),
        [SMEM, VMEM, VMEM, ANY, ANY],
        scratch=[pltpu.VMEM((2, tokens, block), BF16), pltpu.SemaphoreType.DMA((2,))],
    )(place, sums, feats3, far_low, far_high)
    keep3, across_r, across_l = tie(keep3, across_r, across_l)
    got3 = shift(send3, "yh", 1)
    far = jnp.stack([far_low, far_high], 0)
    keep1, send1, feats1 = call(
        last_gradient_kernel,
        (
            jax.ShapeDtypeStruct((1, 128, block), F32),
            jax.ShapeDtypeStruct((1, 128, block), BF16),
            jax.ShapeDtypeStruct((1,) + feat_shape, BF16),
        ),
        [SMEM] + [ANY] * 4 + [VMEM] * 2,
        scratch=[pltpu.SemaphoreType.DMA((4,))],
    )(place, across_r, across_l, shift(across_r, "c", 1), shift(across_l, "c", 1), cots, far)
    got1 = shift(send1, "yh", 1)

    square = (block, block)
    full = jax.ShapeDtypeStruct(square, F32)
    tall = jax.ShapeDtypeStruct((block, 256), BF16)
    left_new, right_new, left_root, right_root, direction, low_w, high_w = call(
        step_kernel,
        (full,) * 5 + (tall, tall),
        [SMEM, SMEM] + [VMEM] * 9,
        scratch=[pltpu.VMEM((NX, 128, block), F32)],
    )(
        refresh, place, keep3, keep1, got3, got1, weights[0],
        left_stats[0], right_stats[0], left_roots[0], right_roots[0],
    )
    low_got = shift(low_w, "yh", 1)
    high_got = shift(high_w, "yh", 1)

    half = jax.ShapeDtypeStruct((tokens, block), BF16)
    whole = jax.ShapeDtypeStruct((2 * tokens, block), BF16)
    rows = [pltpu.VMEM((NX, 2, 128, 256), BF16)]
    cost = (2 * NZ * 2 * tokens * NX * quarter * 256, 4 << 20)
    low_parts = call(
        low_query_kernel,
        jax.ShapeDtypeStruct((NZ, 2 * tokens, 256), BF16),
        [SMEM] + [VMEM] * 4,
        scratch=rows,
        cost=cost,
    )(place, feats3, feats1, low_w, low_got)
    up3, down3, up4, down4, up2, down2, up1, down1, here = call(
        high_query_kernel,
        (whole, whole, half, half) + (whole,) * 5,
        [SMEM] + [VMEM] * 5,
        scratch=rows,
        cost=cost,
    )(place, feats3, feats1, high_w, high_got, low_parts)
    up3, down3 = shift(up3, "z", 1), shift(down3, "z", -1)
    up4, down4 = shift(up4, "z", 2), shift(down4, "z", -2)
    up1, down1 = shift(up1, "z", 1), shift(down1, "z", -1)
    up2 = call(partial(relay_kernel, 0), whole, [VMEM] * 3)(up2, up3, up4)
    down2 = call(partial(relay_kernel, 1), whole, [VMEM] * 3)(down2, down3, down4)
    up2, down2 = shift(up2, "z", 2), shift(down2, "z", -2)
    total = here.astype(F32)
    for value in (up1, down1, up2, down2):
        total = total + value.astype(F32)
    total = total.astype(BF16)
    mine = total[:tokens]
    theirs = shift(total[tokens:], "c", 1)
    queries = jnp.concatenate(
        [jnp.where(core == 0, mine, theirs), jnp.where(core == 0, theirs, mine)], 1
    )
    return (
        left_new[None],
        right_new[None],
        left_root[None],
        right_root[None],
        direction[None],
        queries,
    )


def solution(mesh):
    fine = Mesh(mesh.devices.reshape(SIZES), FINE)
    blocks = P(DP + OWNER, None, None)
    in_specs = (P(DP, None), P(DP, OWNER)) + (blocks,) * 5 + (P(DP + OWNER),)
    out_specs = (blocks,) * 5 + (P(DP, OWNER),)
    return jax.shard_map(body, mesh=fine, in_specs=in_specs, out_specs=out_specs, check_vma=False)
```

time: 158 us -> 141 us (0.89); the launches traced: 156 us -> 142 us
  local copies, waits for them, and re-layouts: 15.6 us -> 0.1 us
  Pallas kernels: 10.6 us -> 19.6 us
  waiting for transfers between devices: 68.9 us -> 62.8 us
  starting transfers between devices: 58 us -> 56.4 us
    unnamed x37 -> x12, local copies, waits for them, and re-layouts: 10.3 us -> 0.03 us
    pallas_call x3 -> x9, Pallas kernels: 10.6 us -> 19.6 us  [the longest x1 7 us: body(): call(step_kernel, (full,) * 5 + (tall, tall), [SMEM, SMEM] + [VMEM] * 9,...]
    ppermute x27 -> x31, waiting for transfers between devices: 68.9 us -> 62.8 us  [shift(): lax.ppermute(value, axis, [(i, (i + step) % size) for i in range(size)])]
    reshape x1 -> x0, local copies, waits for them, and re-layouts: 3.32 us -> none  [body(): split = inputs.reshape(tokens, NZ, NX, quarter)]
    ppermute x27 -> x31, starting transfers between devices: 48.9 us -> 47.4 us  [shift(): lax.ppermute(value, axis, [(i, (i + step) % size) for i in range(size)])]
  transfers between devices with their start and end apart: 28 -> 32, of which waited for: 14 -> 14; matrix products, arithmetic and copies ran while one was open for 1% -> 0% of each run, Pallas kernels for 0% -> 6%
where the time goes in v2:
time: 141 us; the launch traced here: 142 us
  waiting for transfers between devices  62.8 us (45%)
  starting transfers between devices  56.4 us (40%)
  Pallas kernels  19.6 us (14%)
  between operations  1.54 us (1%)
    ppermute x31, waiting for transfers between devices, shift(): lax.ppermute(value, axis, [(i, (i + step) % size) for i in range(size)])  62.8 us
    ppermute x31, starting transfers between devices, shift(): lax.ppermute(value, axis, [(i, (i + step) % size) for i in range(size)])  47.4 us
    all_to_all x1, starting transfers between devices, body(): split = lax.all_to_all(split, 'z', 0, 0, tiled=True)  9.03 us
    pallas_call x1, Pallas kernels, body(): call(step_kernel, (full,) * 5 + (tall, tall), [SMEM, SMEM] + [VMEM] * 9,...  7 us
    pallas_call x1, Pallas kernels, body(): call(gradient_kernel, (jax.ShapeDtypeStruct((3, quarter, block), F32), ja...  3.45 us
  transfers between devices with their start and end apart: 32, of which 14 were waited for; matrix products, arithmetic and copies ran while one was open for 0% of the time, Pallas kernels for 6%

profile of v2, /device:TPU:1, one launch (start us, length us, event | category | flops | bytes accessed | tf_op | source)
XLA Modules:
  0.0 141.6 jit_solution(389875979253230097)
XLA Ops:
  0.7 2.5 %shard_map.127 = bf16[8,128,256]{2,1,0:T(8,128)(2,1)} custom-call(s32[3]{0:T(128)S(1)} %pad_add_fusion.place, bf16[128,8192]{1,0:T(8,128)(2,1)} %inputs.1), custom_call_target="tpu_custom_call" | custom-call | tf_op jit(solution)/shard_map/pallas_call | solution.py:269
  3.2 9.0 %all-to-all-start = ((bf16[8,128,256]{2,1,0:T(8,128)(2,1)}), bf16[8,128,256]{2,1,0:T(8,128)(2,1)S(1)}, u32[]{:S(2)}, u32[]{:S(2)}) async-start(bf16[8,128,256]{2,1,0:T(8,128)(2,1)} %shard_map.127), calls=%async_computation | async-start | bytes 1048576 | tf_op jit(solution)/shard_map/all_to_all | solution.py:282
  14.3 3.0 %collective-permute-start.2 = (bf16[2,128,512]{2,1,0:T(8,128)(2,1)S(1)}, bf16[2,128,512]{2,1,0:T(8,128)(2,1)S(1)}, u32[]{:S(2)}, u32[]{:S(2)}) collective-permute-start(bf16[2,128,512]{2,1,0:T(8,128)(2,1)S(1)} %pad_maximum_fusion.refs_6_), channel_id=1, source_target_pairs={{0,224},{32,0},{64,32},{96,64},{128,96},{160,128},{192,160},{224,1... | collective-permute-start | bytes 786440 | tf_op jit(solution)/shard_map/ppermute | solution.py:32
  17.4 13.2 %collective-permute-done.2.refs_10_ = bf16[2,128,512]{2,1,0:T(8,128)(2,1)S(1)} collective-permute-done((bf16[2,128,512]{2,1,0:T(8,128)(2,1)S(1)}, bf16[2,128,512]{2,1,0:T(8,128)(2,1)S(1)}, u32[]{:S(2)}, u32[]{:S(2)}) %collective-permute-start.2) | collective-permute-done | bytes 262176 | tf_op jit(solution)/shard_map/ppermute | solution.py:32
  32.2 2.5 %collective-permute-start.4 = (bf16[8,128,256]{2,1,0:T(8,128)(2,1)S(1)}, bf16[8,128,256]{2,1,0:T(8,128)(2,1)S(1)}, u32[]{:S(2)}, u32[]{:S(2)}) collective-permute-start(bf16[8,128,256]{2,1,0:T(8,128)(2,1)S(1)} %all-to-all-done.refs_0_), channel_id=1, source_target_pairs={{0,3},{1,0},{2,1},{3,2},{4,7},{5,4},{6,5},{7,6},{8,11},{9,8},{10,9... | collective-permute-start | bytes 1572872 | tf_op jit(solution)/shard_map/ppermute | solution.py:32
  34.7 2.7 %collective-permute-start.9 = (bf16[2,128,512]{2,1,0:T(8,128)(2,1)S(1)}, bf16[2,128,512]{2,1,0:T(8,128)(2,1)S(1)}, u32[]{:S(2)}, u32[]{:S(2)}) collective-permute-start(bf16[2,128,512]{2,1,0:T(8,128)(2,1)S(1)} %collective-permute-done.2.refs_10_), channel_id=1, source_target_pairs={{0,224},{32,0},{64,32},{96,64},{128,96},{160,128},{192,160},{224,1... | collective-permute-start | bytes 786440 | tf_op jit(solution)/shard_map/ppermute | solution.py:32
  37.3 4.6 %collective-permute-done.8.refs_8_ = bf16[2,128,512]{2,1,0:T(8,128)(2,1)S(1)} collective-permute-done((bf16[2,128,512]{2,1,0:T(8,128)(2,1)S(1)}, bf16[2,128,512]{2,1,0:T(8,128)(2,1)S(1)}, u32[]{:S(2)}, u32[]{:S(2)}) %collective-permute-start.8) | collective-permute-done | bytes 262176 | tf_op jit(solution)/shard_map/ppermute | solution.py:32
  42.2 2.4 %collective-permute-start.11 = (bf16[2,128,512]{2,1,0:T(8,128)(2,1)S(1)}, bf16[2,128,512]{2,1,0:T(8,128)(2,1)S(1)}, u32[]{:S(2)}, u32[]{:S(2)}) collective-permute-start(bf16[2,128,512]{2,1,0:T(8,128)(2,1)S(1)} %collective-permute-done.9.refs_11_), channel_id=1, source_target_pairs={{0,224},{32,0},{64,32},{96,64},{128,96},{160,128},{192,160},{224,1... | collective-permute-start | bytes 786440 | tf_op jit(solution)/shard_map/ppermute | solution.py:32
  44.6 3.2 %collective-permute-start.5 = (bf16[8,128,256]{2,1,0:T(8,128)(2,1)S(1)}, bf16[8,128,256]{2,1,0:T(8,128)(2,1)S(1)}, u32[]{:S(2)}, u32[]{:S(2)}) collective-permute-start(bf16[8,128,256]{2,1,0:T(8,128)(2,1)S(1)} %all-to-all-done.refs_0_), channel_id=1, source_target_pairs={{0,8},{8,0},{1,9},{9,1},{2,10},{10,2},{3,11},{11,3},{4,12},{12,4},... | collective-permute-start | bytes 1572872 | tf_op jit(solution)/shard_map/ppermute | solution.py:32
  47.8 2.4 %collective-permute-start.6 = (bf16[8,128,256]{2,1,0:T(8,128)(2,1)S(1)}, bf16[8,128,256]{2,1,0:T(8,128)(2,1)S(1)}, u32[]{:S(2)}, u32[]{:S(2)}) collective-permute-start(bf16[8,128,256]{2,1,0:T(8,128)(2,1)S(1)} %collective-permute-done.3.refs_1_), channel_id=1, source_target_pairs={{0,8},{8,0},{1,9},{9,1},{2,10},{10,2},{3,11},{11,3},{4,12},{12,4},... | collective-permute-start | bytes 1572872 | tf_op jit(solution)/shard_map/ppermute | solution.py:32
  53.8 3.5 %shard_map.128 = (f32[3,256,512]{2,1,0:T(8,128)S(1)}, bf16[3,8,2,128,256]{4,3,2,1,0:T(8,128)(2,1)S(1)}, bf16[8,2,128,512]{3,2,1,0:T(8,128)(2,1)S(1)}) custom-call(s32[3]{0:T(128)S(1)} %pad_add_fusion.place, bf16[8,128,256]{2,1,0:T(8,128)(2,1)S(1)} %all-to-all-done.refs_0_, bf16[8,128,256]{2,1,0:T(8,128)(2,1)S(1)} %collective-permute-done.3.refs_1_, ...), custom_call_target="tpu_custom_call" | custom-call | flops 1610612736 | bytes 6291456 | tf_op jit(solution)/shard_map/pallas_call | solution.py:296
  60.2 6.2 %collective-permute-start.16 = (bf16[4,128,256]{2,1,0:T(8,128)(2,1)S(1)}, bf16[4,128,256]{2,1,0:T(8,128)(2,1)S(1)}, u32[]{:S(2)}, u32[]{:S(2)}) collective-permute-start(bf16[4,128,256]{2,1,0:T(8,128)(2,1)S(1)} %collective-permute-done.14.own_r), channel_id=1, source_target_pairs={{0,8},{8,0},{1,9},{9,1},{2,10},{10,2},{3,11},{11,3},{4,12},{12,4},... | collective-permute-start | bytes 786440 | tf_op jit(solution)/shard_map/ppermute | solution.py:32
  66.5 2.9 %collective-permute-start.18 = (bf16[3,128,512]{2,1,0:T(8,128)(2,1)S(1)}, bf16[3,128,512]{2,1,0:T(8,128)(2,1)S(1)}, u32[]{:S(2)}, u32[]{:S(2)}) collective-permute-start(bf16[3,128,512]{2,1,0:T(8,128)(2,1)S(1)} %get-tuple-element.55), channel_id=1, source_target_pairs={{0,16},{16,0},{1,17},{17,1},{2,18},{18,2},{3,19},{19,3},{4,20},{20... | collective-permute-start | bytes 1179656 | tf_op jit(solution)/shard_map/ppermute | solution.py:32
  73.1 8.0 %collective-permute-done.19.got1 = bf16[1,128,512]{2,1,0:T(8,128)(2,1)S(1)} collective-permute-done((bf16[1,128,512]{2,1,0:T(8,128)(2,1)S(1)}, bf16[1,128,512]{2,1,0:T(8,128)(2,1)S(1)}, u32[]{:S(2)}, u32[]{:S(2)}) %collective-permute-start.19) | collective-permute-done | bytes 131104 | tf_op jit(solution)/shard_map/ppermute | solution.py:32
  81.1 7.0 %shard_map.131 = (f32[512,512]{1,0:T(8,128)}, f32[512,512]{1,0:T(8,128)}, f32[512,512]{1,0:T(8,128)}, f32[512,512]{1,0:T(8,128)}, f32[512,512]{1,0:T(8,128)}, /*...) custom-call(s32[1]{0:T(128)S(6)} %copy.14.flag, s32[3]{0:T(128)S(1)} %pad_add_fusion.place, ...), custom_call_target="tpu_custom_call" | custom-call | tf_op jit(solution)/shard_map/pallas_call | solution.py:337
  88.1 3.0 %collective-permute-start.20 = (bf16[512,256]{1,0:T(8,128)(2,1)S(1)}, bf16[512,256]{1,0:T(8,128)(2,1)S(1)}, u32[]{:S(2)}, u32[]{:S(2)}) collective-permute-start(bf16[512,256]{1,0:T(8,128)(2,1)S(1)} %get-tuple-element.63.own_w), channel_id=1, source_target_pairs={{0,16},{16,0},{1,17},{17,1},{2,18},{18,2},{3,19},{19,3},{4,20},{20... | collective-permute-start | bytes 786440 | tf_op jit(solution)/shard_map/ppermute | solution.py:32
  91.1 6.9 %collective-permute-done.21.other_w = bf16[512,256]{1,0:T(8,128)(2,1)S(1)} collective-permute-done((bf16[512,256]{1,0:T(8,128)(2,1)S(1)}, bf16[512,256]{1,0:T(8,128)(2,1)S(1)}, u32[]{:S(2)}, u32[]{:S(2)}) %collective-permute-start.21) | collective-permute-done | bytes 262176 | tf_op jit(solution)/shard_map/ppermute | solution.py:32
  103.9 2.7 %collective-permute-start.27 = (bf16[256,512]{1,0:T(8,128)(2,1)S(1)}, bf16[256,512]{1,0:T(8,128)(2,1)S(1)}, u32[]{:S(2)}, u32[]{:S(2)}) collective-permute-start(bf16[256,512]{1,0:T(8,128)(2,1)S(1)} %get-tuple-element.72), channel_id=1, source_target_pairs={{0,224},{32,0},{64,32},{96,64},{128,96},{160,128},{192,160},{224,1... | collective-permute-start | bytes 786440 | tf_op jit(solution)/shard_map/ppermute | solution.py:32
  106.5 3.6 %collective-permute-start.28 = (bf16[128,512]{1,0:T(8,128)(2,1)S(1)}, bf16[128,512]{1,0:T(8,128)(2,1)S(1)}, u32[]{:S(2)}, u32[]{:S(2)}) collective-permute-start(bf16[128,512]{1,0:T(8,128)(2,1)S(1)} %get-tuple-element.73), channel_id=1, source_target_pairs={{0,192},{32,224},{64,0},{96,32},{128,64},{160,96},{192,128},{224,1... | collective-permute-start | bytes 393224 | tf_op jit(solution)/shard_map/ppermute | solution.py:32
  110.1 7.1 %collective-permute-done.25.four = bf16[128,512]{1,0:T(8,128)(2,1)S(1)} collective-permute-done((bf16[128,512]{1,0:T(8,128)(2,1)S(1)}, bf16[128,512]{1,0:T(8,128)(2,1)S(1)}, u32[]{:S(2)}, u32[]{:S(2)}) %collective-permute-start.25) | collective-permute-done | bytes 131104 | tf_op jit(solution)/shard_map/ppermute | solution.py:32
  118.4 2.9 %collective-permute-start.26 = (bf16[256,512]{1,0:T(8,128)(2,1)S(1)}, bf16[256,512]{1,0:T(8,128)(2,1)S(1)}, u32[]{:S(2)}, u32[]{:S(2)}) collective-permute-start(bf16[256,512]{1,0:T(8,128)(2,1)S(1)} %shard_map.134), channel_id=1, source_target_pairs={{0,64},{32,96},{64,128},{96,160},{128,192},{160,224},{192,0},{224,... | collective-permute-start | bytes 786440 | tf_op jit(solution)/shard_map/ppermute | solution.py:32
  124.1 2.3 %collective-permute-done.23 = bf16[256,512]{1,0:T(8,128)(2,1)S(1)} collective-permute-done((bf16[256,512]{1,0:T(8,128)(2,1)S(1)}, bf16[256,512]{1,0:T(8,128)(2,1)S(1)}, u32[]{:S(2)}, u32[]{:S(2)}) %collective-permute-start.23) | collective-permute-done | bytes 262176 | tf_op jit(solution)/shard_map/ppermute | solution.py:32
  126.4 8.1 %collective-permute-done.26 = bf16[256,512]{1,0:T(8,128)(2,1)S(1)} collective-permute-done((bf16[256,512]{1,0:T(8,128)(2,1)S(1)}, bf16[256,512]{1,0:T(8,128)(2,1)S(1)}, u32[]{:S(2)}, u32[]{:S(2)}) %collective-permute-start.26) | collective-permute-done | bytes 262176 | tf_op jit(solution)/shard_map/ppermute | solution.py:32
  134.6 4.0 %collective-permute-done.29 = bf16[256,512]{1,0:T(8,128)(2,1)S(1)} collective-permute-done((bf16[256,512]{1,0:T(8,128)(2,1)S(1)}, bf16[256,512]{1,0:T(8,128)(2,1)S(1)}, u32[]{:S(2)}, u32[]{:S(2)}) %collective-permute-start.29) | collective-permute-done | bytes 262176 | tf_op jit(solution)/shard_map/ppermute | solution.py:32
  (73 shorter events, 26.5 us)
Async XLA Ops:
  3.2 29.0 %all-to-all-start = ((bf16[8,128,256]{2,1,0:T(8,128)(2,1)}), bf16[8,128,256]{2,1,0:T(8,128)(2,1)S(1)}, u32[]{:S(2)}, u32[]{:S(2)}) async-start(bf16[8,128,256]{2,1,0:T(8,128)(2,1)} %shard_map.127), calls=%async_computation | async-start | bytes 1048576 | tf_op jit(solution)/shard_map/all_to_all | solution.py:282
  14.3 16.2 %collective-permute-start.2 = (bf16[2,128,512]{2,1,0:T(8,128)(2,1)S(1)}, bf16[2,128,512]{2,1,0:T(8,128)(2,1)S(1)}, u32[]{:S(2)}, u32[]{:S(2)}) collective-permute-start(bf16[2,128,512]{2,1,0:T(8,128)(2,1)S(1)} %pad_maximum_fusion.refs_6_), channel_id=1, source_target_pairs={{0,224},{32,0},{64,32},{96,64},{128,96},{160,128},{192,160},{224,1... | collective-permute-start | bytes 786440 | tf_op jit(solution)/shard_map/ppermute | solution.py:32
  17.4 14.8 %collective-permute-start.1 = (bf16[2,128,512]{2,1,0:T(8,128)(2,1)S(1)}, bf16[2,128,512]{2,1,0:T(8,128)(2,1)S(1)}, u32[]{:S(2)}, u32[]{:S(2)}) collective-permute-start(bf16[2,128,512]{2,1,0:T(8,128)(2,1)S(1)} %pad_maximum_fusion.refs_6_), channel_id=1, source_target_pairs={{0,32},{32,64},{64,96},{96,128},{128,160},{160,192},{192,224},{224... | collective-permute-start | bytes 786440 | tf_op jit(solution)/shard_map/ppermute | solution.py:32
  32.2 15.7 %collective-permute-start.4 = (bf16[8,128,256]{2,1,0:T(8,128)(2,1)S(1)}, bf16[8,128,256]{2,1,0:T(8,128)(2,1)S(1)}, u32[]{:S(2)}, u32[]{:S(2)}) collective-permute-start(bf16[8,128,256]{2,1,0:T(8,128)(2,1)S(1)} %all-to-all-done.refs_0_), channel_id=1, source_target_pairs={{0,3},{1,0},{2,1},{3,2},{4,7},{5,4},{6,5},{7,6},{8,11},{9,8},{10,9... | collective-permute-start | bytes 1572872 | tf_op jit(solution)/shard_map/ppermute | solution.py:32
  34.7 13.2 %collective-permute-start.3 = (bf16[8,128,256]{2,1,0:T(8,128)(2,1)S(1)}, bf16[8,128,256]{2,1,0:T(8,128)(2,1)S(1)}, u32[]{:S(2)}, u32[]{:S(2)}) collective-permute-start(bf16[8,128,256]{2,1,0:T(8,128)(2,1)S(1)} %all-to-all-done.refs_0_), channel_id=1, source_target_pairs={{0,1},{1,2},{2,3},{3,0},{4,5},{5,6},{6,7},{7,4},{8,9},{9,10},{10,1... | collective-permute-start | bytes 1572872 | tf_op jit(solution)/shard_map/ppermute | solution.py:32
  34.7 7.3 %collective-permute-start.9 = (bf16[2,128,512]{2,1,0:T(8,128)(2,1)S(1)}, bf16[2,128,512]{2,1,0:T(8,128)(2,1)S(1)}, u32[]{:S(2)}, u32[]{:S(2)}) collective-permute-start(bf16[2,128,512]{2,1,0:T(8,128)(2,1)S(1)} %collective-permute-done.2.refs_10_), channel_id=1, source_target_pairs={{0,224},{32,0},{64,32},{96,64},{128,96},{160,128},{192,160},{224,1... | collective-permute-start | bytes 786440 | tf_op jit(solution)/shard_map/ppermute | solution.py:32
  41.9 8.3 %collective-permute-start.10 = (bf16[2,128,512]{2,1,0:T(8,128)(2,1)S(1)}, bf16[2,128,512]{2,1,0:T(8,128)(2,1)S(1)}, u32[]{:S(2)}, u32[]{:S(2)}) collective-permute-start(bf16[2,128,512]{2,1,0:T(8,128)(2,1)S(1)} %collective-permute-done.8.refs_8_), channel_id=1, source_target_pairs={{0,32},{32,64},{64,96},{96,128},{128,160},{160,192},{192,224},{224... | collective-permute-start | bytes 786440 | tf_op jit(solution)/shard_map/ppermute | solution.py:32
  42.2 8.0 %collective-permute-start.11 = (bf16[2,128,512]{2,1,0:T(8,128)(2,1)S(1)}, bf16[2,128,512]{2,1,0:T(8,128)(2,1)S(1)}, u32[]{:S(2)}, u32[]{:S(2)}) collective-permute-start(bf16[2,128,512]{2,1,0:T(8,128)(2,1)S(1)} %collective-permute-done.9.refs_11_), channel_id=1, source_target_pairs={{0,224},{32,0},{64,32},{96,64},{128,96},{160,128},{192,160},{224,1... | collective-permute-start | bytes 786440 | tf_op jit(solution)/shard_map/ppermute | solution.py:32
  44.6 7.3 %collective-permute-start.5 = (bf16[8,128,256]{2,1,0:T(8,128)(2,1)S(1)}, bf16[8,128,256]{2,1,0:T(8,128)(2,1)S(1)}, u32[]{:S(2)}, u32[]{:S(2)}) collective-permute-start(bf16[8,128,256]{2,1,0:T(8,128)(2,1)S(1)} %all-to-all-done.refs_0_), channel_id=1, source_target_pairs={{0,8},{8,0},{1,9},{9,1},{2,10},{10,2},{3,11},{11,3},{4,12},{12,4},... | collective-permute-start | bytes 1572872 | tf_op jit(solution)/shard_map/ppermute | solution.py:32
  50.2 10.0 %collective-permute-start.15 = (bf16[4,128,256]{2,1,0:T(8,128)(2,1)S(1)}, bf16[4,128,256]{2,1,0:T(8,128)(2,1)S(1)}, u32[]{:S(2)}, u32[]{:S(2)}) collective-permute-start(bf16[4,128,256]{2,1,0:T(8,128)(2,1)S(1)} %slice.33), channel_id=1, source_target_pairs={{0,3},{1,0},{2,1},{3,2},{4,7},{5,4},{6,5},{7,6},{8,11},{9,8},{10,9... | collective-permute-start | bytes 786440 | tf_op jit(solution)/shard_map/ppermute | solution.py:32
  51.2 9.1 %collective-permute-start.14 = (bf16[4,128,256]{2,1,0:T(8,128)(2,1)S(1)}, bf16[4,128,256]{2,1,0:T(8,128)(2,1)S(1)}, u32[]{:S(2)}, u32[]{:S(2)}) collective-permute-start(bf16[4,128,256]{2,1,0:T(8,128)(2,1)S(1)} %slice.32), channel_id=1, source_target_pairs={{0,1},{1,2},{2,3},{3,0},{4,5},{5,6},{6,7},{7,4},{8,9},{9,10},{10,1... | collective-permute-start | bytes 786440 | tf_op jit(solution)/shard_map/ppermute | solution.py:32
  60.2 9.2 %collective-permute-start.16 = (bf16[4,128,256]{2,1,0:T(8,128)(2,1)S(1)}, bf16[4,128,256]{2,1,0:T(8,128)(2,1)S(1)}, u32[]{:S(2)}, u32[]{:S(2)}) collective-permute-start(bf16[4,128,256]{2,1,0:T(8,128)(2,1)S(1)} %collective-permute-done.14.own_r), channel_id=1, source_target_pairs={{0,8},{8,0},{1,9},{9,1},{2,10},{10,2},{3,11},{11,3},{4,12},{12,4},... | collective-permute-start | bytes 786440 | tf_op jit(solution)/shard_map/ppermute | solution.py:32
  66.5 14.6 %collective-permute-start.18 = (bf16[3,128,512]{2,1,0:T(8,128)(2,1)S(1)}, bf16[3,128,512]{2,1,0:T(8,128)(2,1)S(1)}, u32[]{:S(2)}, u32[]{:S(2)}) collective-permute-start(bf16[3,128,512]{2,1,0:T(8,128)(2,1)S(1)} %get-tuple-element.55), channel_id=1, source_target_pairs={{0,16},{16,0},{1,17},{17,1},{2,18},{18,2},{3,19},{19,3},{4,20},{20... | collective-permute-start | bytes 1179656 | tf_op jit(solution)/shard_map/ppermute | solution.py:32
  70.9 10.1 %collective-permute-start.19 = (bf16[1,128,512]{2,1,0:T(8,128)(2,1)S(1)}, bf16[1,128,512]{2,1,0:T(8,128)(2,1)S(1)}, u32[]{:S(2)}, u32[]{:S(2)}) collective-permute-start(bf16[1,128,512]{2,1,0:T(8,128)(2,1)S(1)} %get-tuple-element.56), channel_id=1, source_target_pairs={{0,16},{16,0},{1,17},{17,1},{2,18},{18,2},{3,19},{19,3},{4,20},{20... | collective-permute-start | bytes 393224 | tf_op jit(solution)/shard_map/ppermute | solution.py:32
  88.1 9.9 %collective-permute-start.21 = (bf16[512,256]{1,0:T(8,128)(2,1)S(1)}, bf16[512,256]{1,0:T(8,128)(2,1)S(1)}, u32[]{:S(2)}, u32[]{:S(2)}) collective-permute-start(bf16[512,256]{1,0:T(8,128)(2,1)S(1)} %get-tuple-element.64.own_w), channel_id=1, source_target_pairs={{0,16},{16,0},{1,17},{17,1},{2,18},{18,2},{3,19},{19,3},{4,20},{20... | collective-permute-start | bytes 786440 | tf_op jit(solution)/shard_map/ppermute | solution.py:32
  88.1 13.8 %collective-permute-start.20 = (bf16[512,256]{1,0:T(8,128)(2,1)S(1)}, bf16[512,256]{1,0:T(8,128)(2,1)S(1)}, u32[]{:S(2)}, u32[]{:S(2)}) collective-permute-start(bf16[512,256]{1,0:T(8,128)(2,1)S(1)} %get-tuple-element.63.own_w), channel_id=1, source_target_pairs={{0,16},{16,0},{1,17},{17,1},{2,18},{18,2},{3,19},{19,3},{4,20},{20... | collective-permute-start | bytes 786440 | tf_op jit(solution)/shard_map/ppermute | solution.py:32
  103.8 14.5 %collective-permute-start.24 = (bf16[256,512]{1,0:T(8,128)(2,1)S(1)}, bf16[256,512]{1,0:T(8,128)(2,1)S(1)}, u32[]{:S(2)}, u32[]{:S(2)}) collective-permute-start(bf16[256,512]{1,0:T(8,128)(2,1)S(1)} %get-tuple-element.69), channel_id=1, source_target_pairs={{0,32},{32,64},{64,96},{96,128},{128,160},{160,192},{192,224},{224... | collective-permute-start | bytes 786440 | tf_op jit(solution)/shard_map/ppermute | solution.py:32
  103.9 17.4 %collective-permute-start.27 = (bf16[256,512]{1,0:T(8,128)(2,1)S(1)}, bf16[256,512]{1,0:T(8,128)(2,1)S(1)}, u32[]{:S(2)}, u32[]{:S(2)}) collective-permute-start(bf16[256,512]{1,0:T(8,128)(2,1)S(1)} %get-tuple-element.72), channel_id=1, source_target_pairs={{0,224},{32,0},{64,32},{96,64},{128,96},{160,128},{192,160},{224,1... | collective-permute-start | bytes 786440 | tf_op jit(solution)/shard_map/ppermute | solution.py:32
  106.5 10.7 %collective-permute-start.25 = (bf16[128,512]{1,0:T(8,128)(2,1)S(1)}, bf16[128,512]{1,0:T(8,128)(2,1)S(1)}, u32[]{:S(2)}, u32[]{:S(2)}) collective-permute-start(bf16[128,512]{1,0:T(8,128)(2,1)S(1)} %get-tuple-element.70), channel_id=1, source_target_pairs={{0,64},{32,96},{64,128},{96,160},{128,192},{160,224},{192,0},{224,... | collective-permute-start | bytes 393224 | tf_op jit(solution)/shard_map/ppermute | solution.py:32
  106.5 14.7 %collective-permute-start.28 = (bf16[128,512]{1,0:T(8,128)(2,1)S(1)}, bf16[128,512]{1,0:T(8,128)(2,1)S(1)}, u32[]{:S(2)}, u32[]{:S(2)}) collective-permute-start(bf16[128,512]{1,0:T(8,128)(2,1)S(1)} %get-tuple-element.73), channel_id=1, source_target_pairs={{0,192},{32,224},{64,0},{96,32},{128,64},{160,96},{192,128},{224,1... | collective-permute-start | bytes 393224 | tf_op jit(solution)/shard_map/ppermute | solution.py:32
  110.1 14.0 %collective-permute-start.22 = (bf16[256,512]{1,0:T(8,128)(2,1)S(1)}, bf16[256,512]{1,0:T(8,128)(2,1)S(1)}, u32[]{:S(2)}, u32[]{:S(2)}) collective-permute-start(bf16[256,512]{1,0:T(8,128)(2,1)S(1)} %get-tuple-element.66), channel_id=1, source_target_pairs={{0,32},{32,64},{64,96},{96,128},{128,160},{160,192},{192,224},{224... | collective-permute-start | bytes 786440 | tf_op jit(solution)/shard_map/ppermute | solution.py:32
  117.2 9.2 %collective-permute-start.23 = (bf16[256,512]{1,0:T(8,128)(2,1)S(1)}, bf16[256,512]{1,0:T(8,128)(2,1)S(1)}, u32[]{:S(2)}, u32[]{:S(2)}) collective-permute-start(bf16[256,512]{1,0:T(8,128)(2,1)S(1)} %get-tuple-element.67), channel_id=1, source_target_pairs={{0,224},{32,0},{64,32},{96,64},{128,96},{160,128},{192,160},{224,1... | collective-permute-start | bytes 786440 | tf_op jit(solution)/shard_map/ppermute | solution.py:32
  118.4 16.2 %collective-permute-start.26 = (bf16[256,512]{1,0:T(8,128)(2,1)S(1)}, bf16[256,512]{1,0:T(8,128)(2,1)S(1)}, u32[]{:S(2)}, u32[]{:S(2)}) collective-permute-start(bf16[256,512]{1,0:T(8,128)(2,1)S(1)} %shard_map.134), channel_id=1, source_target_pairs={{0,64},{32,96},{64,128},{96,160},{128,192},{160,224},{192,0},{224,... | collective-permute-start | bytes 786440 | tf_op jit(solution)/shard_map/ppermute | solution.py:32
  121.3 17.2 %collective-permute-start.29 = (bf16[256,512]{1,0:T(8,128)(2,1)S(1)}, bf16[256,512]{1,0:T(8,128)(2,1)S(1)}, u32[]{:S(2)}, u32[]{:S(2)}) collective-permute-start(bf16[256,512]{1,0:T(8,128)(2,1)S(1)} %shard_map.135), channel_id=1, source_target_pairs={{0,192},{32,224},{64,0},{96,32},{128,64},{160,96},{192,128},{224,1... | collective-permute-start | bytes 786440 | tf_op jit(solution)/shard_map/ppermute | solution.py:32
  (14 other events, 155.7 us)

commit v3 on v2

--- a/solution.py
+++ b/solution.py
@@ -130,6 +130,10 @@
     put(total, yh, 0, keep, send)
 
 
+def combine_kernel(keep, got, out):
+    out[...] = keep[...] + got[...].astype(F32)
+
+
 def eye_mask(order):
     rows = lax.broadcasted_iota(jnp.int32, (order, order), 0)
     cols = lax.broadcasted_iota(jnp.int32, (order, order), 1)
@@ -158,13 +162,13 @@
 
 
 def step_kernel(
-    flag, place, keep3, keep1, got3, got1, weights, left_stats, right_stats, left_roots, right_roots,
+    flag, place, sum3, keep1, got1, weights, left_stats, right_stats, left_roots, right_roots,
     left_new, right_new, left_root, right_root, update, low_cols, high_cols, rows,
 ):
     x = place[1]
     for piece, step in enumerate(ROW):
         if piece < 3:
-            value = keep3[piece] + got3[piece].astype(F32)
+            value = sum3[piece]
         else:
             value = keep1[0] + got1[0].astype(F32)
         rows[(x + step + NX) % NX] = value
@@ -288,6 +292,7 @@
     up3, down3 = tie(shift(up2, "z", 1), shift(down2, "z", -1))
     far_low, far_high = shift(up3[0], "z", 1), shift(down3[1], "z", -1)
     other1, other2 = shift(right, "c", 1), shift(left, "c", 1)
+    right, left, other1, other2 = tie(right, left, other1, other2)
     across_r = shift(right[: NZ // 2], "x", 1)
     across_l = shift(left[NZ // 2 :], "x", -1)
 
@@ -302,7 +307,7 @@
         ),
         [SMEM] + [ANY] * 13,
         scratch=[pltpu.SemaphoreType.DMA((13,))],
-        cost=(2 * NZ * 2 * tokens * 3 * quarter * block, 6 << 20),
+        cost=(2 * NZ * 2 * tokens * 3 * quarter * block * 8, 6 << 20),
     )(
         place, split, right, left, other0, other1, other2,
         start, up1, up2, up3, down1, down2, down3,
@@ -331,16 +336,23 @@
     )(place, across_r, across_l, shift(across_r, "c", 1), shift(across_l, "c", 1), cots, far)
     got1 = shift(send1, "yh", 1)
 
+    sum3 = call(
+        combine_kernel,
+        jax.ShapeDtypeStruct((3, 128, block), F32),
+        [VMEM, VMEM],
+        cost=(1 << 34, 2 << 20),
+    )(keep3, got3)
+
     square = (block, block)
     full = jax.ShapeDtypeStruct(square, F32)
     tall = jax.ShapeDtypeStruct((block, 256), BF16)
     left_new, right_new, left_root, right_root, direction, low_w, high_w = call(
         step_kernel,
         (full,) * 5 + (tall, tall),
-        [SMEM, SMEM] + [VMEM] * 9,
+        [SMEM, SMEM] + [VMEM] * 8,
         scratch=[pltpu.VMEM((NX, 128, block), F32)],
     )(
-        refresh, place, keep3, keep1, got3, got1, weights[0],
+        refresh, place, sum3, keep1, got1, weights[0],
         left_stats[0], right_stats[0], left_roots[0], right_roots[0],
     )
     low_got = shift(low_w, "yh", 1)

time: 141 us -> 136 us (0.965)
  waiting for transfers between devices: 62.8 us -> 57.1 us
  Pallas kernels: 19.6 us -> 16.6 us
  starting transfers between devices: 56.4 us -> 59.4 us
    ppermute x31, waiting for transfers between devices: 62.8 us -> 57.1 us  [shift(): lax.ppermute(value, axis, [(i, (i + step) % size) for i in range(size)])]
    pallas_call x1 -> x2, Pallas kernels: 7 us -> 3.96 us  [the longest x1 3.9 us: body(): call(step_kernel, (full,) * 5 + (tall, tall), [SMEM, SMEM] + [VMEM] * 8,...]
    ppermute x31, starting transfers between devices: 47.4 us -> 50.3 us  [shift(): lax.ppermute(value, axis, [(i, (i + step) % size) for i in range(size)])]
  transfers between devices with their start and end apart: 32 -> 32, of which waited for: 14 -> 13; matrix products, arithmetic and copies ran while one was open for 0% -> 0% of each run, Pallas kernels for 6% -> 6%
where the time goes in v3:
time: 136 us
  starting transfers between devices  59.4 us (44%)
  waiting for transfers between devices  57.1 us (42%)
  Pallas kernels  16.6 us (12%)
  between operations  1.56 us (1%)
    ppermute x31, waiting for transfers between devices, shift(): lax.ppermute(value, axis, [(i, (i + step) % size) for i in range(size)])  57.1 us
    ppermute x31, starting transfers between devices, shift(): lax.ppermute(value, axis, [(i, (i + step) % size) for i in range(size)])  50.3 us
    all_to_all x1, starting transfers between devices, body(): split = lax.all_to_all(split, 'z', 0, 0, tiled=True)  9.03 us
    pallas_call x1, Pallas kernels, body(): call(step_kernel, (full,) * 5 + (tall, tall), [SMEM, SMEM] + [VMEM] * 8,...  3.9 us
    pallas_call x1, Pallas kernels, body(): call(gradient_kernel, (jax.ShapeDtypeStruct((3, quarter, block), F32), ja...  3.44 us
  transfers between devices with their start and end apart: 32, of which 13 were waited for; matrix products, arithmetic and copies ran while one was open for 0% of the time, Pallas kernels for 6%

profile of v3, /device:TPU:1, one launch (start us, length us, event | category | flops | bytes accessed | tf_op | source)
XLA Modules:
  0.0 135.8 jit_solution(18305818597099509718)
XLA Ops:
  0.7 2.5 %shard_map.127 = bf16[8,128,256]{2,1,0:T(8,128)(2,1)} custom-call(s32[3]{0:T(128)S(1)} %pad_add_fusion.place, bf16[128,8192]{1,0:T(8,128)(2,1)} %inputs.1), custom_call_target="tpu_custom_call" | custom-call | tf_op jit(solution)/shard_map/pallas_call | solution.py:273
  3.2 9.0 %all-to-all-start = ((bf16[8,128,256]{2,1,0:T(8,128)(2,1)}), bf16[8,128,256]{2,1,0:T(8,128)(2,1)S(1)}, u32[]{:S(2)}, u32[]{:S(2)}) async-start(bf16[8,128,256]{2,1,0:T(8,128)(2,1)} %shard_map.127), calls=%async_computation | async-start | bytes 1048576 | tf_op jit(solution)/shard_map/all_to_all | solution.py:286
  14.3 3.0 %collective-permute-start.2 = (bf16[2,128,512]{2,1,0:T(8,128)(2,1)S(1)}, bf16[2,128,512]{2,1,0:T(8,128)(2,1)S(1)}, u32[]{:S(2)}, u32[]{:S(2)}) collective-permute-start(bf16[2,128,512]{2,1,0:T(8,128)(2,1)S(1)} %pad_maximum_fusion.refs_6_), channel_id=1, source_target_pairs={{0,224},{32,0},{64,32},{96,64},{128,96},{160,128},{192,160},{224,1... | collective-permute-start | bytes 786440 | tf_op jit(solution)/shard_map/ppermute | solution.py:32
  17.4 13.2 %collective-permute-done.2.refs_10_ = bf16[2,128,512]{2,1,0:T(8,128)(2,1)S(1)} collective-permute-done((bf16[2,128,512]{2,1,0:T(8,128)(2,1)S(1)}, bf16[2,128,512]{2,1,0:T(8,128)(2,1)S(1)}, u32[]{:S(2)}, u32[]{:S(2)}) %collective-permute-start.2) | collective-permute-done | bytes 262176 | tf_op jit(solution)/shard_map/ppermute | solution.py:32
  32.2 2.5 %collective-permute-start.4 = (bf16[8,128,256]{2,1,0:T(8,128)(2,1)S(1)}, bf16[8,128,256]{2,1,0:T(8,128)(2,1)S(1)}, u32[]{:S(2)}, u32[]{:S(2)}) collective-permute-start(bf16[8,128,256]{2,1,0:T(8,128)(2,1)S(1)} %all-to-all-done.refs_0_), channel_id=1, source_target_pairs={{0,3},{1,0},{2,1},{3,2},{4,7},{5,4},{6,5},{7,6},{8,11},{9,8},{10,9... | collective-permute-start | bytes 1572872 | tf_op jit(solution)/shard_map/ppermute | solution.py:32
  34.7 2.7 %collective-permute-start.9 = (bf16[2,128,512]{2,1,0:T(8,128)(2,1)S(1)}, bf16[2,128,512]{2,1,0:T(8,128)(2,1)S(1)}, u32[]{:S(2)}, u32[]{:S(2)}) collective-permute-start(bf16[2,128,512]{2,1,0:T(8,128)(2,1)S(1)} %collective-permute-done.2.refs_10_), channel_id=1, source_target_pairs={{0,224},{32,0},{64,32},{96,64},{128,96},{160,128},{192,160},{224,1... | collective-permute-start | bytes 786440 | tf_op jit(solution)/shard_map/ppermute | solution.py:32
  37.3 4.6 %collective-permute-done.8.refs_8_ = bf16[2,128,512]{2,1,0:T(8,128)(2,1)S(1)} collective-permute-done((bf16[2,128,512]{2,1,0:T(8,128)(2,1)S(1)}, bf16[2,128,512]{2,1,0:T(8,128)(2,1)S(1)}, u32[]{:S(2)}, u32[]{:S(2)}) %collective-permute-start.8) | collective-permute-done | bytes 262176 | tf_op jit(solution)/shard_map/ppermute | solution.py:32
  42.2 2.4 %collective-permute-start.11 = (bf16[2,128,512]{2,1,0:T(8,128)(2,1)S(1)}, bf16[2,128,512]{2,1,0:T(8,128)(2,1)S(1)}, u32[]{:S(2)}, u32[]{:S(2)}) collective-permute-start(bf16[2,128,512]{2,1,0:T(8,128)(2,1)S(1)} %collective-permute-done.9.refs_11_), channel_id=1, source_target_pairs={{0,224},{32,0},{64,32},{96,64},{128,96},{160,128},{192,160},{224,1... | collective-permute-start | bytes 786440 | tf_op jit(solution)/shard_map/ppermute | solution.py:32
  44.6 3.2 %collective-permute-start.6 = (bf16[8,128,256]{2,1,0:T(8,128)(2,1)S(1)}, bf16[8,128,256]{2,1,0:T(8,128)(2,1)S(1)}, u32[]{:S(2)}, u32[]{:S(2)}) collective-permute-start(bf16[8,128,256]{2,1,0:T(8,128)(2,1)S(1)} %collective-permute-done.4.refs_2_), channel_id=1, source_target_pairs={{0,8},{8,0},{1,9},{9,1},{2,10},{10,2},{3,11},{11,3},{4,12},{12,4},... | collective-permute-start | bytes 1572872 | tf_op jit(solution)/shard_map/ppermute | solution.py:32
  53.8 3.4 %shard_map.128 = (f32[3,256,512]{2,1,0:T(8,128)S(1)}, bf16[3,8,2,128,256]{4,3,2,1,0:T(8,128)(2,1)S(1)}, bf16[8,2,128,512]{3,2,1,0:T(8,128)(2,1)S(1)}) custom-call(s32[3]{0:T(128)S(1)} %pad_add_fusion.place, bf16[8,128,256]{2,1,0:T(8,128)(2,1)S(1)} %all-to-all-done.refs_0_, bf16[8,128,256]{2,1,0:T(8,128)(2,1)S(1)} %collective-permute-done.3.refs_1_, ...), custom_call_target="tpu_custom_call" | custom-call | flops 12884901888 | bytes 6291456 | tf_op jit(solution)/shard_map/pallas_call | solution.py:301
  58.6 3.0 %collective-permute-start.16 = (bf16[3,128,512]{2,1,0:T(8,128)(2,1)S(1)}, bf16[3,128,512]{2,1,0:T(8,128)(2,1)S(1)}, u32[]{:S(2)}, u32[]{:S(2)}) collective-permute-start(bf16[3,128,512]{2,1,0:T(8,128)(2,1)S(1)} %get-tuple-element.59), channel_id=1, source_target_pairs={{0,16},{16,0},{1,17},{17,1},{2,18},{18,2},{3,19},{19,3},{4,20},{20... | collective-permute-start | bytes 1179656 | tf_op jit(solution)/shard_map/ppermute | solution.py:32
  61.6 5.2 %collective-permute-start.17 = (bf16[4,128,256]{2,1,0:T(8,128)(2,1)S(1)}, bf16[4,128,256]{2,1,0:T(8,128)(2,1)S(1)}, u32[]{:S(2)}, u32[]{:S(2)}) collective-permute-start(bf16[4,128,256]{2,1,0:T(8,128)(2,1)S(1)} %collective-permute-done.14.own_r), channel_id=1, source_target_pairs={{0,8},{8,0},{1,9},{9,1},{2,10},{10,2},{3,11},{11,3},{4,12},{12,4},... | collective-permute-start | bytes 786440 | tf_op jit(solution)/shard_map/ppermute | solution.py:32
  69.9 2.5 %collective-permute-start.19 = (bf16[1,128,512]{2,1,0:T(8,128)(2,1)S(1)}, bf16[1,128,512]{2,1,0:T(8,128)(2,1)S(1)}, u32[]{:S(2)}, u32[]{:S(2)}) collective-permute-start(bf16[1,128,512]{2,1,0:T(8,128)(2,1)S(1)} %get-tuple-element.64), channel_id=1, source_target_pairs={{0,16},{16,0},{1,17},{17,1},{2,18},{18,2},{3,19},{19,3},{4,20},{20... | collective-permute-start | bytes 393224 | tf_op jit(solution)/shard_map/ppermute | solution.py:32
  72.5 3.8 %collective-permute-done.19.got1 = bf16[1,128,512]{2,1,0:T(8,128)(2,1)S(1)} collective-permute-done((bf16[1,128,512]{2,1,0:T(8,128)(2,1)S(1)}, bf16[1,128,512]{2,1,0:T(8,128)(2,1)S(1)}, u32[]{:S(2)}, u32[]{:S(2)}) %collective-permute-start.19) | collective-permute-done | bytes 131104 | tf_op jit(solution)/shard_map/ppermute | solution.py:32
  76.2 3.9 %shard_map.132 = (f32[512,512]{1,0:T(8,128)}, f32[512,512]{1,0:T(8,128)}, f32[512,512]{1,0:T(8,128)}, f32[512,512]{1,0:T(8,128)}, f32[512,512]{1,0:T(8,128)}, /*...) custom-call(s32[1]{0:T(128)S(6)} %copy.14.flag, s32[3]{0:T(128)S(1)} %pad_add_fusion.place, ...), custom_call_target="tpu_custom_call" | custom-call | tf_op jit(solution)/shard_map/pallas_call | solution.py:349
  80.1 5.5 %collective-permute-start.21 = (bf16[512,256]{1,0:T(8,128)(2,1)S(1)}, bf16[512,256]{1,0:T(8,128)(2,1)S(1)}, u32[]{:S(2)}, u32[]{:S(2)}) collective-permute-start(bf16[512,256]{1,0:T(8,128)(2,1)S(1)} %get-tuple-element.72.own_w), channel_id=1, source_target_pairs={{0,16},{16,0},{1,17},{17,1},{2,18},{18,2},{3,19},{19,3},{4,20},{20... | collective-permute-start | bytes 786440 | tf_op jit(solution)/shard_map/ppermute | solution.py:32
  85.6 6.1 %collective-permute-done.21.other_w = bf16[512,256]{1,0:T(8,128)(2,1)S(1)} collective-permute-done((bf16[512,256]{1,0:T(8,128)(2,1)S(1)}, bf16[512,256]{1,0:T(8,128)(2,1)S(1)}, u32[]{:S(2)}, u32[]{:S(2)}) %collective-permute-start.21) | collective-permute-done | bytes 262176 | tf_op jit(solution)/shard_map/ppermute | solution.py:32
  93.6 2.8 %collective-permute-done.20.other_w = bf16[512,256]{1,0:T(8,128)(2,1)S(1)} collective-permute-done((bf16[512,256]{1,0:T(8,128)(2,1)S(1)}, bf16[512,256]{1,0:T(8,128)(2,1)S(1)}, u32[]{:S(2)}, u32[]{:S(2)}) %collective-permute-start.20) | collective-permute-done | bytes 262176 | tf_op jit(solution)/shard_map/ppermute | solution.py:32
  98.3 3.6 %collective-permute-start.27 = (bf16[256,512]{1,0:T(8,128)(2,1)S(1)}, bf16[256,512]{1,0:T(8,128)(2,1)S(1)}, u32[]{:S(2)}, u32[]{:S(2)}) collective-permute-start(bf16[256,512]{1,0:T(8,128)(2,1)S(1)} %get-tuple-element.80), channel_id=1, source_target_pairs={{0,224},{32,0},{64,32},{96,64},{128,96},{160,128},{192,160},{224,1... | collective-permute-start | bytes 786440 | tf_op jit(solution)/shard_map/ppermute | solution.py:32
  102.2 3.3 %collective-permute-start.28 = (bf16[128,512]{1,0:T(8,128)(2,1)S(1)}, bf16[128,512]{1,0:T(8,128)(2,1)S(1)}, u32[]{:S(2)}, u32[]{:S(2)}) collective-permute-start(bf16[128,512]{1,0:T(8,128)(2,1)S(1)} %get-tuple-element.81), channel_id=1, source_target_pairs={{0,192},{32,224},{64,0},{96,32},{128,64},{160,96},{192,128},{224,1... | collective-permute-start | bytes 393224 | tf_op jit(solution)/shard_map/ppermute | solution.py:32
  105.5 9.7 %collective-permute-done.25.four = bf16[128,512]{1,0:T(8,128)(2,1)S(1)} collective-permute-done((bf16[128,512]{1,0:T(8,128)(2,1)S(1)}, bf16[128,512]{1,0:T(8,128)(2,1)S(1)}, u32[]{:S(2)}, u32[]{:S(2)}) %collective-permute-start.25) | collective-permute-done | bytes 131104 | tf_op jit(solution)/shard_map/ppermute | solution.py:32
  115.5 3.6 %collective-permute-start.29 = (bf16[256,512]{1,0:T(8,128)(2,1)S(1)}, bf16[256,512]{1,0:T(8,128)(2,1)S(1)}, u32[]{:S(2)}, u32[]{:S(2)}) collective-permute-start(bf16[256,512]{1,0:T(8,128)(2,1)S(1)} %shard_map.136), channel_id=1, source_target_pairs={{0,192},{32,224},{64,0},{96,32},{128,64},{160,96},{192,128},{224,1... | collective-permute-start | bytes 786440 | tf_op jit(solution)/shard_map/ppermute | solution.py:32
  119.1 5.8 %collective-permute-done.23 = bf16[256,512]{1,0:T(8,128)(2,1)S(1)} collective-permute-done((bf16[256,512]{1,0:T(8,128)(2,1)S(1)}, bf16[256,512]{1,0:T(8,128)(2,1)S(1)}, u32[]{:S(2)}, u32[]{:S(2)}) %collective-permute-start.23) | collective-permute-done | bytes 262176 | tf_op jit(solution)/shard_map/ppermute | solution.py:32
  124.9 6.8 %collective-permute-done.26 = bf16[256,512]{1,0:T(8,128)(2,1)S(1)} collective-permute-done((bf16[256,512]{1,0:T(8,128)(2,1)S(1)}, bf16[256,512]{1,0:T(8,128)(2,1)S(1)}, u32[]{:S(2)}, u32[]{:S(2)}) %collective-permute-start.26) | collective-permute-done | bytes 262176 | tf_op jit(solution)/shard_map/ppermute | solution.py:32
  (74 shorter events, 22.2 us)
Async XLA Ops:
  3.2 29.0 %all-to-all-start = ((bf16[8,128,256]{2,1,0:T(8,128)(2,1)}), bf16[8,128,256]{2,1,0:T(8,128)(2,1)S(1)}, u32[]{:S(2)}, u32[]{:S(2)}) async-start(bf16[8,128,256]{2,1,0:T(8,128)(2,1)} %shard_map.127), calls=%async_computation | async-start | bytes 1048576 | tf_op jit(solution)/shard_map/all_to_all | solution.py:286
  14.3 16.2 %collective-permute-start.2 = (bf16[2,128,512]{2,1,0:T(8,128)(2,1)S(1)}, bf16[2,128,512]{2,1,0:T(8,128)(2,1)S(1)}, u32[]{:S(2)}, u32[]{:S(2)}) collective-permute-start(bf16[2,128,512]{2,1,0:T(8,128)(2,1)S(1)} %pad_maximum_fusion.refs_6_), channel_id=1, source_target_pairs={{0,224},{32,0},{64,32},{96,64},{128,96},{160,128},{192,160},{224,1... | collective-permute-start | bytes 786440 | tf_op jit(solution)/shard_map/ppermute | solution.py:32
  17.4 14.8 %collective-permute-start.1 = (bf16[2,128,512]{2,1,0:T(8,128)(2,1)S(1)}, bf16[2,128,512]{2,1,0:T(8,128)(2,1)S(1)}, u32[]{:S(2)}, u32[]{:S(2)}) collective-permute-start(bf16[2,128,512]{2,1,0:T(8,128)(2,1)S(1)} %pad_maximum_fusion.refs_6_), channel_id=1, source_target_pairs={{0,32},{32,64},{64,96},{96,128},{128,160},{160,192},{192,224},{224... | collective-permute-start | bytes 786440 | tf_op jit(solution)/shard_map/ppermute | solution.py:32
  32.2 12.4 %collective-permute-start.4 = (bf16[8,128,256]{2,1,0:T(8,128)(2,1)S(1)}, bf16[8,128,256]{2,1,0:T(8,128)(2,1)S(1)}, u32[]{:S(2)}, u32[]{:S(2)}) collective-permute-start(bf16[8,128,256]{2,1,0:T(8,128)(2,1)S(1)} %all-to-all-done.refs_0_), channel_id=1, source_target_pairs={{0,3},{1,0},{2,1},{3,2},{4,7},{5,4},{6,5},{7,6},{8,11},{9,8},{10,9... | collective-permute-start | bytes 1572872 | tf_op jit(solution)/shard_map/ppermute | solution.py:32
  34.7 13.2 %collective-permute-start.3 = (bf16[8,128,256]{2,1,0:T(8,128)(2,1)S(1)}, bf16[8,128,256]{2,1,0:T(8,128)(2,1)S(1)}, u32[]{:S(2)}, u32[]{:S(2)}) collective-permute-start(bf16[8,128,256]{2,1,0:T(8,128)(2,1)S(1)} %all-to-all-done.refs_0_), channel_id=1, source_target_pairs={{0,1},{1,2},{2,3},{3,0},{4,5},{5,6},{6,7},{7,4},{8,9},{9,10},{10,1... | collective-permute-start | bytes 1572872 | tf_op jit(solution)/shard_map/ppermute | solution.py:32
  34.7 7.3 %collective-permute-start.8 = (bf16[2,128,512]{2,1,0:T(8,128)(2,1)S(1)}, bf16[2,128,512]{2,1,0:T(8,128)(2,1)S(1)}, u32[]{:S(2)}, u32[]{:S(2)}) collective-permute-start(bf16[2,128,512]{2,1,0:T(8,128)(2,1)S(1)} %collective-permute-done.1.refs_7_), channel_id=1, source_target_pairs={{0,32},{32,64},{64,96},{96,128},{128,160},{160,192},{192,224},{224... | collective-permute-start | bytes 786440 | tf_op jit(solution)/shard_map/ppermute | solution.py:32
  34.7 7.3 %collective-permute-start.9 = (bf16[2,128,512]{2,1,0:T(8,128)(2,1)S(1)}, bf16[2,128,512]{2,1,0:T(8,128)(2,1)S(1)}, u32[]{:S(2)}, u32[]{:S(2)}) collective-permute-start(bf16[2,128,512]{2,1,0:T(8,128)(2,1)S(1)} %collective-permute-done.2.refs_10_), channel_id=1, source_target_pairs={{0,224},{32,0},{64,32},{96,64},{128,96},{160,128},{192,160},{224,1... | collective-permute-start | bytes 786440 | tf_op jit(solution)/shard_map/ppermute | solution.py:32
  41.9 8.3 %collective-permute-start.10 = (bf16[2,128,512]{2,1,0:T(8,128)(2,1)S(1)}, bf16[2,128,512]{2,1,0:T(8,128)(2,1)S(1)}, u32[]{:S(2)}, u32[]{:S(2)}) collective-permute-start(bf16[2,128,512]{2,1,0:T(8,128)(2,1)S(1)} %collective-permute-done.8.refs_8_), channel_id=1, source_target_pairs={{0,32},{32,64},{64,96},{96,128},{128,160},{160,192},{192,224},{224... | collective-permute-start | bytes 786440 | tf_op jit(solution)/shard_map/ppermute | solution.py:32
  42.2 8.0 %collective-permute-start.11 = (bf16[2,128,512]{2,1,0:T(8,128)(2,1)S(1)}, bf16[2,128,512]{2,1,0:T(8,128)(2,1)S(1)}, u32[]{:S(2)}, u32[]{:S(2)}) collective-permute-start(bf16[2,128,512]{2,1,0:T(8,128)(2,1)S(1)} %collective-permute-done.9.refs_11_), channel_id=1, source_target_pairs={{0,224},{32,0},{64,32},{96,64},{128,96},{160,128},{192,160},{224,1... | collective-permute-start | bytes 786440 | tf_op jit(solution)/shard_map/ppermute | solution.py:32
  44.6 7.2 %collective-permute-start.6 = (bf16[8,128,256]{2,1,0:T(8,128)(2,1)S(1)}, bf16[8,128,256]{2,1,0:T(8,128)(2,1)S(1)}, u32[]{:S(2)}, u32[]{:S(2)}) collective-permute-start(bf16[8,128,256]{2,1,0:T(8,128)(2,1)S(1)} %collective-permute-done.4.refs_2_), channel_id=1, source_target_pairs={{0,8},{8,0},{1,9},{9,1},{2,10},{10,2},{3,11},{11,3},{4,12},{12,4},... | collective-permute-start | bytes 1572872 | tf_op jit(solution)/shard_map/ppermute | solution.py:32
  50.2 7.0 %collective-permute-start.13 = (bf16[128,512]{1,0:T(8,128)(2,1)S(1)}, bf16[128,512]{1,0:T(8,128)(2,1)S(1)}, u32[]{:S(2)}, u32[]{:S(2)}) collective-permute-start(bf16[128,512]{1,0:T(8,128)(2,1)S(1)} %slice_bitcast_fusion), channel_id=1, source_target_pairs={{0,224},{32,0},{64,32},{96,64},{128,96},{160,128},{192,160},{224,1... | collective-permute-start | bytes 393224 | tf_op jit(solution)/shard_map/ppermute | solution.py:32
  51.9 9.7 %collective-permute-start.15 = (bf16[4,128,256]{2,1,0:T(8,128)(2,1)S(1)}, bf16[4,128,256]{2,1,0:T(8,128)(2,1)S(1)}, u32[]{:S(2)}, u32[]{:S(2)}) collective-permute-start(bf16[4,128,256]{2,1,0:T(8,128)(2,1)S(1)} %slice.29), channel_id=1, source_target_pairs={{0,3},{1,0},{2,1},{3,2},{4,7},{5,4},{6,5},{7,6},{8,11},{9,8},{10,9... | collective-permute-start | bytes 786440 | tf_op jit(solution)/shard_map/ppermute | solution.py:32
  53.8 7.8 %collective-permute-start.14 = (bf16[4,128,256]{2,1,0:T(8,128)(2,1)S(1)}, bf16[4,128,256]{2,1,0:T(8,128)(2,1)S(1)}, u32[]{:S(2)}, u32[]{:S(2)}) collective-permute-start(bf16[4,128,256]{2,1,0:T(8,128)(2,1)S(1)} %slice.28), channel_id=1, source_target_pairs={{0,1},{1,2},{2,3},{3,0},{4,5},{5,6},{6,7},{7,4},{8,9},{9,10},{10,1... | collective-permute-start | bytes 786440 | tf_op jit(solution)/shard_map/ppermute | solution.py:32
  58.6 13.8 %collective-permute-start.16 = (bf16[3,128,512]{2,1,0:T(8,128)(2,1)S(1)}, bf16[3,128,512]{2,1,0:T(8,128)(2,1)S(1)}, u32[]{:S(2)}, u32[]{:S(2)}) collective-permute-start(bf16[3,128,512]{2,1,0:T(8,128)(2,1)S(1)} %get-tuple-element.59), channel_id=1, source_target_pairs={{0,16},{16,0},{1,17},{17,1},{2,18},{18,2},{3,19},{19,3},{4,20},{20... | collective-permute-start | bytes 1179656 | tf_op jit(solution)/shard_map/ppermute | solution.py:32
  80.1 11.6 %collective-permute-start.21 = (bf16[512,256]{1,0:T(8,128)(2,1)S(1)}, bf16[512,256]{1,0:T(8,128)(2,1)S(1)}, u32[]{:S(2)}, u32[]{:S(2)}) collective-permute-start(bf16[512,256]{1,0:T(8,128)(2,1)S(1)} %get-tuple-element.72.own_w), channel_id=1, source_target_pairs={{0,16},{16,0},{1,17},{17,1},{2,18},{18,2},{3,19},{19,3},{4,20},{20... | collective-permute-start | bytes 786440 | tf_op jit(solution)/shard_map/ppermute | solution.py:32
  85.6 10.7 %collective-permute-start.20 = (bf16[512,256]{1,0:T(8,128)(2,1)S(1)}, bf16[512,256]{1,0:T(8,128)(2,1)S(1)}, u32[]{:S(2)}, u32[]{:S(2)}) collective-permute-start(bf16[512,256]{1,0:T(8,128)(2,1)S(1)} %get-tuple-element.71.own_w), channel_id=1, source_target_pairs={{0,16},{16,0},{1,17},{17,1},{2,18},{18,2},{3,19},{19,3},{4,20},{20... | collective-permute-start | bytes 786440 | tf_op jit(solution)/shard_map/ppermute | solution.py:32
  98.2 17.0 %collective-permute-start.24 = (bf16[256,512]{1,0:T(8,128)(2,1)S(1)}, bf16[256,512]{1,0:T(8,128)(2,1)S(1)}, u32[]{:S(2)}, u32[]{:S(2)}) collective-permute-start(bf16[256,512]{1,0:T(8,128)(2,1)S(1)} %get-tuple-element.77), channel_id=1, source_target_pairs={{0,32},{32,64},{64,96},{96,128},{128,160},{160,192},{192,224},{224... | collective-permute-start | bytes 786440 | tf_op jit(solution)/shard_map/ppermute | solution.py:32
  98.3 17.1 %collective-permute-start.27 = (bf16[256,512]{1,0:T(8,128)(2,1)S(1)}, bf16[256,512]{1,0:T(8,128)(2,1)S(1)}, u32[]{:S(2)}, u32[]{:S(2)}) collective-permute-start(bf16[256,512]{1,0:T(8,128)(2,1)S(1)} %get-tuple-element.80), channel_id=1, source_target_pairs={{0,224},{32,0},{64,32},{96,64},{128,96},{160,128},{192,160},{224,1... | collective-permute-start | bytes 786440 | tf_op jit(solution)/shard_map/ppermute | solution.py:32
  101.9 13.3 %collective-permute-start.25 = (bf16[128,512]{1,0:T(8,128)(2,1)S(1)}, bf16[128,512]{1,0:T(8,128)(2,1)S(1)}, u32[]{:S(2)}, u32[]{:S(2)}) collective-permute-start(bf16[128,512]{1,0:T(8,128)(2,1)S(1)} %get-tuple-element.78), channel_id=1, source_target_pairs={{0,64},{32,96},{64,128},{96,160},{128,192},{160,224},{192,0},{224,... | collective-permute-start | bytes 393224 | tf_op jit(solution)/shard_map/ppermute | solution.py:32
  102.2 13.2 %collective-permute-start.28 = (bf16[128,512]{1,0:T(8,128)(2,1)S(1)}, bf16[128,512]{1,0:T(8,128)(2,1)S(1)}, u32[]{:S(2)}, u32[]{:S(2)}) collective-permute-start(bf16[128,512]{1,0:T(8,128)(2,1)S(1)} %get-tuple-element.81), channel_id=1, source_target_pairs={{0,192},{32,224},{64,0},{96,32},{128,64},{160,96},{192,128},{224,1... | collective-permute-start | bytes 393224 | tf_op jit(solution)/shard_map/ppermute | solution.py:32
  105.5 13.7 %collective-permute-start.22 = (bf16[256,512]{1,0:T(8,128)(2,1)S(1)}, bf16[256,512]{1,0:T(8,128)(2,1)S(1)}, u32[]{:S(2)}, u32[]{:S(2)}) collective-permute-start(bf16[256,512]{1,0:T(8,128)(2,1)S(1)} %get-tuple-element.74), channel_id=1, source_target_pairs={{0,32},{32,64},{64,96},{96,128},{128,160},{160,192},{192,224},{224... | collective-permute-start | bytes 786440 | tf_op jit(solution)/shard_map/ppermute | solution.py:32
  115.2 9.7 %collective-permute-start.23 = (bf16[256,512]{1,0:T(8,128)(2,1)S(1)}, bf16[256,512]{1,0:T(8,128)(2,1)S(1)}, u32[]{:S(2)}, u32[]{:S(2)}) collective-permute-start(bf16[256,512]{1,0:T(8,128)(2,1)S(1)} %get-tuple-element.75), channel_id=1, source_target_pairs={{0,224},{32,0},{64,32},{96,64},{128,96},{160,128},{192,160},{224,1... | collective-permute-start | bytes 786440 | tf_op jit(solution)/shard_map/ppermute | solution.py:32
  115.3 16.4 %collective-permute-start.26 = (bf16[256,512]{1,0:T(8,128)(2,1)S(1)}, bf16[256,512]{1,0:T(8,128)(2,1)S(1)}, u32[]{:S(2)}, u32[]{:S(2)}) collective-permute-start(bf16[256,512]{1,0:T(8,128)(2,1)S(1)} %shard_map.135), channel_id=1, source_target_pairs={{0,64},{32,96},{64,128},{96,160},{128,192},{160,224},{192,0},{224,... | collective-permute-start | bytes 786440 | tf_op jit(solution)/shard_map/ppermute | solution.py:32
  115.5 16.2 %collective-permute-start.29 = (bf16[256,512]{1,0:T(8,128)(2,1)S(1)}, bf16[256,512]{1,0:T(8,128)(2,1)S(1)}, u32[]{:S(2)}, u32[]{:S(2)}) collective-permute-start(bf16[256,512]{1,0:T(8,128)(2,1)S(1)} %shard_map.136), channel_id=1, source_target_pairs={{0,192},{32,224},{64,0},{96,32},{128,64},{160,96},{192,128},{224,1... | collective-permute-start | bytes 786440 | tf_op jit(solution)/shard_map/ppermute | solution.py:32
  (14 other events, 76.1 us)

commit v4 on v3

--- a/solution.py
+++ b/solution.py
@@ -18,6 +18,7 @@
 OWNER = ("yl", "x")
 F32 = jnp.float32
 BF16 = jnp.bfloat16
+WIDE = 256
 VMEM = pl.BlockSpec(memory_space=pltpu.VMEM)
 SMEM = pl.BlockSpec(memory_space=pltpu.SMEM)
 ANY = pl.BlockSpec(memory_space=pl.ANY)
@@ -193,8 +194,8 @@
     direction = direction * (direction.shape[0] / jnp.sqrt(total + 1e-12))
     update[...] = direction
     updated = (weights[...] - (0.25 / math.sqrt(8192)) * direction).astype(BF16)
-    low_cols[...] = updated[:, :256]
-    high_cols[...] = updated[:, 256:]
+    low_cols[...] = updated[:, :WIDE]
+    high_cols[...] = updated[:, WIDE:]
 
 
 def query_parts(place, feats3, feats1, own_w, other_w, rows):
@@ -221,21 +222,27 @@
         out[k] = part(k)
 
 
-def high_query_kernel(
-    place, feats3, feats1, own_w, other_w, low, up3, down3, up4, down4, up2, down2, up1, down1, here, rows
+def far_query_kernel(
+    place, feats3, feats1, own_w, other_w, low, up3, down3, up4, down4, rows
 ):
     part = query_parts(place, feats3, feats1, own_w, other_w, rows)
     for k, out in ((3, up3), (5, down3)):
-        out[:, :256] = low[k]
-        out[:, 256:] = part(k)
+        out[:, :WIDE] = low[k]
+        out[:, WIDE:] = part(k)
     both = part(4)
-    up4[:, :256] = low[4, :128]
-    up4[:, 256:] = both[:128]
-    down4[:, :256] = low[4, 128:]
-    down4[:, 256:] = both[128:]
+    up4[:, :WIDE] = low[4, :128]
+    up4[:, WIDE:] = both[:128]
+    down4[:, :WIDE] = low[4, 128:]
+    down4[:, WIDE:] = both[128:]
+
+
+def near_query_kernel(
+    place, feats3, feats1, own_w, other_w, low, up2, down2, up1, down1, here, rows
+):
+    part = query_parts(place, feats3, feats1, own_w, other_w, rows)
     for k, out in zip(NEAR, (up2, down2, up1, down1, here)):
-        out[:, :256] = low[k]
-        out[:, 256:] = part(k)
+        out[:, :WIDE] = low[k]
+        out[:, WIDE:] = part(k)
 
 
 def relay_kernel(half, mine, three, four, out):
@@ -345,10 +352,11 @@
 
     square = (block, block)
     full = jax.ShapeDtypeStruct(square, F32)
-    tall = jax.ShapeDtypeStruct((block, 256), BF16)
+    wide = jax.ShapeDtypeStruct((block, WIDE), BF16)
+    narrow = jax.ShapeDtypeStruct((block, block - WIDE), BF16)
     left_new, right_new, left_root, right_root, direction, low_w, high_w = call(
         step_kernel,
-        (full,) * 5 + (tall, tall),
+        (full,) * 5 + (wide, narrow),
         [SMEM, SMEM] + [VMEM] * 8,
         scratch=[pltpu.VMEM((NX, 128, block), F32)],
     )(
@@ -360,22 +368,29 @@
 
     half = jax.ShapeDtypeStruct((tokens, block), BF16)
     whole = jax.ShapeDtypeStruct((2 * tokens, block), BF16)
-    rows = [pltpu.VMEM((NX, 2, 128, 256), BF16)]
-    cost = (2 * NZ * 2 * tokens * NX * quarter * 256, 4 << 20)
     low_parts = call(
         low_query_kernel,
-        jax.ShapeDtypeStruct((NZ, 2 * tokens, 256), BF16),
+        jax.ShapeDtypeStruct((NZ, 2 * tokens, WIDE), BF16),
         [SMEM] + [VMEM] * 4,
-        scratch=rows,
-        cost=cost,
+        scratch=[pltpu.VMEM((NX, 2, 128, WIDE), BF16)],
+        cost=(1 << 31, 4 << 20),
     )(place, feats3, feats1, low_w, low_got)
-    up3, down3, up4, down4, up2, down2, up1, down1, here = call(
-        high_query_kernel,
-        (whole, whole, half, half) + (whole,) * 5,
+    rows = [pltpu.VMEM((NX, 2, 128, block - WIDE), BF16)]
+    operands = (place, feats3, feats1, high_w, high_got, low_parts)
+    up3, down3, up4, down4 = call(
+        far_query_kernel,
+        (whole, whole, half, half),
         [SMEM] + [VMEM] * 5,
         scratch=rows,
-        cost=cost,
-    )(place, feats3, feats1, high_w, high_got, low_parts)
+        cost=(1 << 28, 2 << 20),
+    )(*operands)
+    up2, down2, up1, down1, here = call(
+        near_query_kernel,
+        (whole,) * 5,
+        [SMEM] + [VMEM] * 5,
+        scratch=rows,
+        cost=(1 << 34, 2 << 20),
+    )(*operands)
     up3, down3 = shift(up3, "z", 1), shift(down3, "z", -1)
     up4, down4 = shift(up4, "z", 2), shift(down4, "z", -2)
     up1, down1 = shift(up1, "z", 1), shift(down1, "z", -1)

time: 136 us -> 134 us (0.985)
  waiting for transfers between devices: 57.1 us -> 51.8 us
  starting transfers between devices: 59.4 us -> 61.9 us
    ppermute x31, waiting for transfers between devices: 57.1 us -> 51.8 us  [shift(): lax.ppermute(value, axis, [(i, (i + step) % size) for i in range(size)])]
    ppermute x31, starting transfers between devices: 50.3 us -> 52.8 us  [shift(): lax.ppermute(value, axis, [(i, (i + step) % size) for i in range(size)])]
    pallas_call x3 -> x4, Pallas kernels: 7.59 us -> 8.34 us  [the longest x1 3.9 us: body(): call(step_kernel, (full,) * 5 + (wide, narrow), [SMEM, SMEM] + [VMEM] * 8...]
  transfers between devices with their start and end apart: 32 -> 32, of which waited for: 13 -> 15; matrix products, arithmetic and copies ran while one was open for 0% -> 0% of each run, Pallas kernels for 6% -> 7%
where the time goes in v4:
time: 134 us
  starting transfers between devices  61.9 us (46%)
  waiting for transfers between devices  51.8 us (39%)
  Pallas kernels  17.3 us (13%)
  between operations  1.55 us (1%)
    ppermute x31, starting transfers between devices, shift(): lax.ppermute(value, axis, [(i, (i + step) % size) for i in range(size)])  52.8 us
    ppermute x31, waiting for transfers between devices, shift(): lax.ppermute(value, axis, [(i, (i + step) % size) for i in range(size)])  51.8 us
    all_to_all x1, starting transfers between devices, body(): split = lax.all_to_all(split, 'z', 0, 0, tiled=True)  9.03 us
    pallas_call x1, Pallas kernels, body(): call(step_kernel, (full,) * 5 + (wide, narrow), [SMEM, SMEM] + [VMEM] * 8...  3.9 us
    pallas_call x1, Pallas kernels, body(): call(gradient_kernel, (jax.ShapeDtypeStruct((3, quarter, block), F32), ja...  3.44 us
  transfers between devices with their start and end apart: 32, of which 15 were waited for; matrix products, arithmetic and copies ran while one was open for 0% of the time, Pallas kernels for 7%

profile of v4, /device:TPU:1, one launch (start us, length us, event | category | flops | bytes accessed | tf_op | source)
XLA Modules:
  0.0 133.7 jit_solution(2415550321488739338)
XLA Ops:
  0.7 2.5 %shard_map.127 = bf16[8,128,256]{2,1,0:T(8,128)(2,1)} custom-call(s32[3]{0:T(128)S(1)} %pad_add_fusion.place, bf16[128,8192]{1,0:T(8,128)(2,1)} %inputs.1), custom_call_target="tpu_custom_call" | custom-call | tf_op jit(solution)/shard_map/pallas_call | solution.py:280
  3.2 9.0 %all-to-all-start = ((bf16[8,128,256]{2,1,0:T(8,128)(2,1)}), bf16[8,128,256]{2,1,0:T(8,128)(2,1)S(1)}, u32[]{:S(2)}, u32[]{:S(2)}) async-start(bf16[8,128,256]{2,1,0:T(8,128)(2,1)} %shard_map.127), calls=%async_computation | async-start | bytes 1048576 | tf_op jit(solution)/shard_map/all_to_all | solution.py:293
  14.3 3.0 %collective-permute-start.2 = (bf16[2,128,512]{2,1,0:T(8,128)(2,1)S(1)}, bf16[2,128,512]{2,1,0:T(8,128)(2,1)S(1)}, u32[]{:S(2)}, u32[]{:S(2)}) collective-permute-start(bf16[2,128,512]{2,1,0:T(8,128)(2,1)S(1)} %pad_maximum_fusion.refs_6_), channel_id=1, source_target_pairs={{0,224},{32,0},{64,32},{96,64},{128,96},{160,128},{192,160},{224,1... | collective-permute-start | bytes 786440 | tf_op jit(solution)/shard_map/ppermute | solution.py:33
  17.4 13.2 %collective-permute-done.2.refs_10_ = bf16[2,128,512]{2,1,0:T(8,128)(2,1)S(1)} collective-permute-done((bf16[2,128,512]{2,1,0:T(8,128)(2,1)S(1)}, bf16[2,128,512]{2,1,0:T(8,128)(2,1)S(1)}, u32[]{:S(2)}, u32[]{:S(2)}) %collective-permute-start.2) | collective-permute-done | bytes 262176 | tf_op jit(solution)/shard_map/ppermute | solution.py:33
  32.2 2.5 %collective-permute-start.4 = (bf16[8,128,256]{2,1,0:T(8,128)(2,1)S(1)}, bf16[8,128,256]{2,1,0:T(8,128)(2,1)S(1)}, u32[]{:S(2)}, u32[]{:S(2)}) collective-permute-start(bf16[8,128,256]{2,1,0:T(8,128)(2,1)S(1)} %all-to-all-done.refs_0_), channel_id=1, source_target_pairs={{0,3},{1,0},{2,1},{3,2},{4,7},{5,4},{6,5},{7,6},{8,11},{9,8},{10,9... | collective-permute-start | bytes 1572872 | tf_op jit(solution)/shard_map/ppermute | solution.py:33
  34.7 2.7 %collective-permute-start.9 = (bf16[2,128,512]{2,1,0:T(8,128)(2,1)S(1)}, bf16[2,128,512]{2,1,0:T(8,128)(2,1)S(1)}, u32[]{:S(2)}, u32[]{:S(2)}) collective-permute-start(bf16[2,128,512]{2,1,0:T(8,128)(2,1)S(1)} %collective-permute-done.2.refs_10_), channel_id=1, source_target_pairs={{0,224},{32,0},{64,32},{96,64},{128,96},{160,128},{192,160},{224,1... | collective-permute-start | bytes 786440 | tf_op jit(solution)/shard_map/ppermute | solution.py:33
  37.3 4.6 %collective-permute-done.8.refs_8_ = bf16[2,128,512]{2,1,0:T(8,128)(2,1)S(1)} collective-permute-done((bf16[2,128,512]{2,1,0:T(8,128)(2,1)S(1)}, bf16[2,128,512]{2,1,0:T(8,128)(2,1)S(1)}, u32[]{:S(2)}, u32[]{:S(2)}) %collective-permute-start.8) | collective-permute-done | bytes 262176 | tf_op jit(solution)/shard_map/ppermute | solution.py:33
  42.2 2.4 %collective-permute-start.11 = (bf16[2,128,512]{2,1,0:T(8,128)(2,1)S(1)}, bf16[2,128,512]{2,1,0:T(8,128)(2,1)S(1)}, u32[]{:S(2)}, u32[]{:S(2)}) collective-permute-start(bf16[2,128,512]{2,1,0:T(8,128)(2,1)S(1)} %collective-permute-done.9.refs_11_), channel_id=1, source_target_pairs={{0,224},{32,0},{64,32},{96,64},{128,96},{160,128},{192,160},{224,1... | collective-permute-start | bytes 786440 | tf_op jit(solution)/shard_map/ppermute | solution.py:33
  44.6 3.2 %collective-permute-start.6 = (bf16[8,128,256]{2,1,0:T(8,128)(2,1)S(1)}, bf16[8,128,256]{2,1,0:T(8,128)(2,1)S(1)}, u32[]{:S(2)}, u32[]{:S(2)}) collective-permute-start(bf16[8,128,256]{2,1,0:T(8,128)(2,1)S(1)} %collective-permute-done.4.refs_2_), channel_id=1, source_target_pairs={{0,8},{8,0},{1,9},{9,1},{2,10},{10,2},{3,11},{11,3},{4,12},{12,4},... | collective-permute-start | bytes 1572872 | tf_op jit(solution)/shard_map/ppermute | solution.py:33
  47.8 2.4 %collective-permute-start.5 = (bf16[8,128,256]{2,1,0:T(8,128)(2,1)S(1)}, bf16[8,128,256]{2,1,0:T(8,128)(2,1)S(1)}, u32[]{:S(2)}, u32[]{:S(2)}) collective-permute-start(bf16[8,128,256]{2,1,0:T(8,128)(2,1)S(1)} %collective-permute-done.3.refs_1_), channel_id=1, source_target_pairs={{0,8},{8,0},{1,9},{9,1},{2,10},{10,2},{3,11},{11,3},{4,12},{12,4},... | collective-permute-start | bytes 1572872 | tf_op jit(solution)/shard_map/ppermute | solution.py:33
  53.8 3.4 %shard_map.128 = (f32[3,256,512]{2,1,0:T(8,128)S(1)}, bf16[3,8,2,128,256]{4,3,2,1,0:T(8,128)(2,1)S(1)}, bf16[8,2,128,512]{3,2,1,0:T(8,128)(2,1)S(1)}) custom-call(s32[3]{0:T(128)S(1)} %pad_add_fusion.place, bf16[8,128,256]{2,1,0:T(8,128)(2,1)S(1)} %all-to-all-done.refs_0_, bf16[8,128,256]{2,1,0:T(8,128)(2,1)S(1)} %collective-permute-done.3.refs_1_, ...), custom_call_target="tpu_custom_call" | custom-call | flops 12884901888 | bytes 6291456 | tf_op jit(solution)/shard_map/pallas_call | solution.py:308
  58.6 3.0 %collective-permute-start.16 = (bf16[3,128,512]{2,1,0:T(8,128)(2,1)S(1)}, bf16[3,128,512]{2,1,0:T(8,128)(2,1)S(1)}, u32[]{:S(2)}, u32[]{:S(2)}) collective-permute-start(bf16[3,128,512]{2,1,0:T(8,128)(2,1)S(1)} %get-tuple-element.59), channel_id=1, source_target_pairs={{0,16},{16,0},{1,17},{17,1},{2,18},{18,2},{3,19},{19,3},{4,20},{20... | collective-permute-start | bytes 1179656 | tf_op jit(solution)/shard_map/ppermute | solution.py:33
  61.6 5.2 %collective-permute-start.17 = (bf16[4,128,256]{2,1,0:T(8,128)(2,1)S(1)}, bf16[4,128,256]{2,1,0:T(8,128)(2,1)S(1)}, u32[]{:S(2)}, u32[]{:S(2)}) collective-permute-start(bf16[4,128,256]{2,1,0:T(8,128)(2,1)S(1)} %collective-permute-done.14.own_r), channel_id=1, source_target_pairs={{0,8},{8,0},{1,9},{9,1},{2,10},{10,2},{3,11},{11,3},{4,12},{12,4},... | collective-permute-start | bytes 786440 | tf_op jit(solution)/shard_map/ppermute | solution.py:33
  69.9 2.5 %collective-permute-start.19 = (bf16[1,128,512]{2,1,0:T(8,128)(2,1)S(1)}, bf16[1,128,512]{2,1,0:T(8,128)(2,1)S(1)}, u32[]{:S(2)}, u32[]{:S(2)}) collective-permute-start(bf16[1,128,512]{2,1,0:T(8,128)(2,1)S(1)} %get-tuple-element.64), channel_id=1, source_target_pairs={{0,16},{16,0},{1,17},{17,1},{2,18},{18,2},{3,19},{19,3},{4,20},{20... | collective-permute-start | bytes 393224 | tf_op jit(solution)/shard_map/ppermute | solution.py:33
  72.5 3.8 %collective-permute-done.19.got1 = bf16[1,128,512]{2,1,0:T(8,128)(2,1)S(1)} collective-permute-done((bf16[1,128,512]{2,1,0:T(8,128)(2,1)S(1)}, bf16[1,128,512]{2,1,0:T(8,128)(2,1)S(1)}, u32[]{:S(2)}, u32[]{:S(2)}) %collective-permute-start.19) | collective-permute-done | bytes 131104 | tf_op jit(solution)/shard_map/ppermute | solution.py:33
  76.2 3.9 %shard_map.132 = (f32[512,512]{1,0:T(8,128)}, f32[512,512]{1,0:T(8,128)}, f32[512,512]{1,0:T(8,128)}, f32[512,512]{1,0:T(8,128)}, f32[512,512]{1,0:T(8,128)}, /*...) custom-call(s32[1]{0:T(128)S(6)} %copy.14.flag, s32[3]{0:T(128)S(1)} %pad_add_fusion.place, ...), custom_call_target="tpu_custom_call" | custom-call | tf_op jit(solution)/shard_map/pallas_call | solution.py:357
  80.1 5.5 %collective-permute-start.21 = (bf16[512,256]{1,0:T(8,128)(2,1)S(1)}, bf16[512,256]{1,0:T(8,128)(2,1)S(1)}, u32[]{:S(2)}, u32[]{:S(2)}) collective-permute-start(bf16[512,256]{1,0:T(8,128)(2,1)S(1)} %get-tuple-element.72.own_w), channel_id=1, source_target_pairs={{0,16},{16,0},{1,17},{17,1},{2,18},{18,2},{3,19},{19,3},{4,20},{20... | collective-permute-start | bytes 786440 | tf_op jit(solution)/shard_map/ppermute | solution.py:33
  85.6 5.4 %collective-permute-done.21.other_w = bf16[512,256]{1,0:T(8,128)(2,1)S(1)} collective-permute-done((bf16[512,256]{1,0:T(8,128)(2,1)S(1)}, bf16[512,256]{1,0:T(8,128)(2,1)S(1)}, u32[]{:S(2)}, u32[]{:S(2)}) %collective-permute-start.21) | collective-permute-done | bytes 262176 | tf_op jit(solution)/shard_map/ppermute | solution.py:33
  92.9 3.8 %collective-permute-done.20.other_w = bf16[512,256]{1,0:T(8,128)(2,1)S(1)} collective-permute-done((bf16[512,256]{1,0:T(8,128)(2,1)S(1)}, bf16[512,256]{1,0:T(8,128)(2,1)S(1)}, u32[]{:S(2)}, u32[]{:S(2)}) %collective-permute-start.20) | collective-permute-done | bytes 262176 | tf_op jit(solution)/shard_map/ppermute | solution.py:33
  101.5 2.7 %collective-permute-start.27 = (bf16[256,512]{1,0:T(8,128)(2,1)S(1)}, bf16[256,512]{1,0:T(8,128)(2,1)S(1)}, u32[]{:S(2)}, u32[]{:S(2)}) collective-permute-start(bf16[256,512]{1,0:T(8,128)(2,1)S(1)} %get-tuple-element.80), channel_id=1, source_target_pairs={{0,224},{32,0},{64,32},{96,64},{128,96},{160,128},{192,160},{224,1... | collective-permute-start | bytes 786440 | tf_op jit(solution)/shard_map/ppermute | solution.py:33
  105.7 2.7 %collective-permute-start.23 = (bf16[256,512]{1,0:T(8,128)(2,1)S(1)}, bf16[256,512]{1,0:T(8,128)(2,1)S(1)}, u32[]{:S(2)}, u32[]{:S(2)}) collective-permute-start(bf16[256,512]{1,0:T(8,128)(2,1)S(1)} %get-tuple-element.75), channel_id=1, source_target_pairs={{0,224},{32,0},{64,32},{96,64},{128,96},{160,128},{192,160},{224,1... | collective-permute-start | bytes 786440 | tf_op jit(solution)/shard_map/ppermute | solution.py:33
  112.5 2.4 %collective-permute-start.29 = (bf16[256,512]{1,0:T(8,128)(2,1)S(1)}, bf16[256,512]{1,0:T(8,128)(2,1)S(1)}, u32[]{:S(2)}, u32[]{:S(2)}) collective-permute-start(bf16[256,512]{1,0:T(8,128)(2,1)S(1)} %shard_map.137), channel_id=1, source_target_pairs={{0,192},{32,224},{64,0},{96,32},{128,64},{160,96},{192,128},{224,1... | collective-permute-start | bytes 786440 | tf_op jit(solution)/shard_map/ppermute | solution.py:33
  118.1 7.0 %collective-permute-done.26 = bf16[256,512]{1,0:T(8,128)(2,1)S(1)} collective-permute-done((bf16[256,512]{1,0:T(8,128)(2,1)S(1)}, bf16[256,512]{1,0:T(8,128)(2,1)S(1)}, u32[]{:S(2)}, u32[]{:S(2)}) %collective-permute-start.26) | collective-permute-done | bytes 262176 | tf_op jit(solution)/shard_map/ppermute | solution.py:33
  125.0 4.7 %collective-permute-done.29 = bf16[256,512]{1,0:T(8,128)(2,1)S(1)} collective-permute-done((bf16[256,512]{1,0:T(8,128)(2,1)S(1)}, bf16[256,512]{1,0:T(8,128)(2,1)S(1)}, u32[]{:S(2)}, u32[]{:S(2)}) %collective-permute-start.29) | collective-permute-done | bytes 262176 | tf_op jit(solution)/shard_map/ppermute | solution.py:33
  (75 shorter events, 30.9 us)
Async XLA Ops:
  3.2 29.0 %all-to-all-start = ((bf16[8,128,256]{2,1,0:T(8,128)(2,1)}), bf16[8,128,256]{2,1,0:T(8,128)(2,1)S(1)}, u32[]{:S(2)}, u32[]{:S(2)}) async-start(bf16[8,128,256]{2,1,0:T(8,128)(2,1)} %shard_map.127), calls=%async_computation | async-start | bytes 1048576 | tf_op jit(solution)/shard_map/all_to_all | solution.py:293
  14.3 16.2 %collective-permute-start.2 = (bf16[2,128,512]{2,1,0:T(8,128)(2,1)S(1)}, bf16[2,128,512]{2,1,0:T(8,128)(2,1)S(1)}, u32[]{:S(2)}, u32[]{:S(2)}) collective-permute-start(bf16[2,128,512]{2,1,0:T(8,128)(2,1)S(1)} %pad_maximum_fusion.refs_6_), channel_id=1, source_target_pairs={{0,224},{32,0},{64,32},{96,64},{128,96},{160,128},{192,160},{224,1... | collective-permute-start | bytes 786440 | tf_op jit(solution)/shard_map/ppermute | solution.py:33
  17.4 14.8 %collective-permute-start.1 = (bf16[2,128,512]{2,1,0:T(8,128)(2,1)S(1)}, bf16[2,128,512]{2,1,0:T(8,128)(2,1)S(1)}, u32[]{:S(2)}, u32[]{:S(2)}) collective-permute-start(bf16[2,128,512]{2,1,0:T(8,128)(2,1)S(1)} %pad_maximum_fusion.refs_6_), channel_id=1, source_target_pairs={{0,32},{32,64},{64,96},{96,128},{128,160},{160,192},{192,224},{224... | collective-permute-start | bytes 786440 | tf_op jit(solution)/shard_map/ppermute | solution.py:33
  32.2 12.4 %collective-permute-start.4 = (bf16[8,128,256]{2,1,0:T(8,128)(2,1)S(1)}, bf16[8,128,256]{2,1,0:T(8,128)(2,1)S(1)}, u32[]{:S(2)}, u32[]{:S(2)}) collective-permute-start(bf16[8,128,256]{2,1,0:T(8,128)(2,1)S(1)} %all-to-all-done.refs_0_), channel_id=1, source_target_pairs={{0,3},{1,0},{2,1},{3,2},{4,7},{5,4},{6,5},{7,6},{8,11},{9,8},{10,9... | collective-permute-start | bytes 1572872 | tf_op jit(solution)/shard_map/ppermute | solution.py:33
  34.7 13.2 %collective-permute-start.3 = (bf16[8,128,256]{2,1,0:T(8,128)(2,1)S(1)}, bf16[8,128,256]{2,1,0:T(8,128)(2,1)S(1)}, u32[]{:S(2)}, u32[]{:S(2)}) collective-permute-start(bf16[8,128,256]{2,1,0:T(8,128)(2,1)S(1)} %all-to-all-done.refs_0_), channel_id=1, source_target_pairs={{0,1},{1,2},{2,3},{3,0},{4,5},{5,6},{6,7},{7,4},{8,9},{9,10},{10,1... | collective-permute-start | bytes 1572872 | tf_op jit(solution)/shard_map/ppermute | solution.py:33
  34.7 7.3 %collective-permute-start.8 = (bf16[2,128,512]{2,1,0:T(8,128)(2,1)S(1)}, bf16[2,128,512]{2,1,0:T(8,128)(2,1)S(1)}, u32[]{:S(2)}, u32[]{:S(2)}) collective-permute-start(bf16[2,128,512]{2,1,0:T(8,128)(2,1)S(1)} %collective-permute-done.1.refs_7_), channel_id=1, source_target_pairs={{0,32},{32,64},{64,96},{96,128},{128,160},{160,192},{192,224},{224... | collective-permute-start | bytes 786440 | tf_op jit(solution)/shard_map/ppermute | solution.py:33
  34.7 7.3 %collective-permute-start.9 = (bf16[2,128,512]{2,1,0:T(8,128)(2,1)S(1)}, bf16[2,128,512]{2,1,0:T(8,128)(2,1)S(1)}, u32[]{:S(2)}, u32[]{:S(2)}) collective-permute-start(bf16[2,128,512]{2,1,0:T(8,128)(2,1)S(1)} %collective-permute-done.2.refs_10_), channel_id=1, source_target_pairs={{0,224},{32,0},{64,32},{96,64},{128,96},{160,128},{192,160},{224,1... | collective-permute-start | bytes 786440 | tf_op jit(solution)/shard_map/ppermute | solution.py:33
  41.9 8.3 %collective-permute-start.10 = (bf16[2,128,512]{2,1,0:T(8,128)(2,1)S(1)}, bf16[2,128,512]{2,1,0:T(8,128)(2,1)S(1)}, u32[]{:S(2)}, u32[]{:S(2)}) collective-permute-start(bf16[2,128,512]{2,1,0:T(8,128)(2,1)S(1)} %collective-permute-done.8.refs_8_), channel_id=1, source_target_pairs={{0,32},{32,64},{64,96},{96,128},{128,160},{160,192},{192,224},{224... | collective-permute-start | bytes 786440 | tf_op jit(solution)/shard_map/ppermute | solution.py:33
  42.2 8.0 %collective-permute-start.11 = (bf16[2,128,512]{2,1,0:T(8,128)(2,1)S(1)}, bf16[2,128,512]{2,1,0:T(8,128)(2,1)S(1)}, u32[]{:S(2)}, u32[]{:S(2)}) collective-permute-start(bf16[2,128,512]{2,1,0:T(8,128)(2,1)S(1)} %collective-permute-done.9.refs_11_), channel_id=1, source_target_pairs={{0,224},{32,0},{64,32},{96,64},{128,96},{160,128},{192,160},{224,1... | collective-permute-start | bytes 786440 | tf_op jit(solution)/shard_map/ppermute | solution.py:33
  44.6 7.2 %collective-permute-start.6 = (bf16[8,128,256]{2,1,0:T(8,128)(2,1)S(1)}, bf16[8,128,256]{2,1,0:T(8,128)(2,1)S(1)}, u32[]{:S(2)}, u32[]{:S(2)}) collective-permute-start(bf16[8,128,256]{2,1,0:T(8,128)(2,1)S(1)} %collective-permute-done.4.refs_2_), channel_id=1, source_target_pairs={{0,8},{8,0},{1,9},{9,1},{2,10},{10,2},{3,11},{11,3},{4,12},{12,4},... | collective-permute-start | bytes 1572872 | tf_op jit(solution)/shard_map/ppermute | solution.py:33
  50.2 7.0 %collective-permute-start.13 = (bf16[128,512]{1,0:T(8,128)(2,1)S(1)}, bf16[128,512]{1,0:T(8,128)(2,1)S(1)}, u32[]{:S(2)}, u32[]{:S(2)}) collective-permute-start(bf16[128,512]{1,0:T(8,128)(2,1)S(1)} %slice_bitcast_fusion), channel_id=1, source_target_pairs={{0,224},{32,0},{64,32},{96,64},{128,96},{160,128},{192,160},{224,1... | collective-permute-start | bytes 393224 | tf_op jit(solution)/shard_map/ppermute | solution.py:33
  51.9 9.7 %collective-permute-start.15 = (bf16[4,128,256]{2,1,0:T(8,128)(2,1)S(1)}, bf16[4,128,256]{2,1,0:T(8,128)(2,1)S(1)}, u32[]{:S(2)}, u32[]{:S(2)}) collective-permute-start(bf16[4,128,256]{2,1,0:T(8,128)(2,1)S(1)} %slice.29), channel_id=1, source_target_pairs={{0,3},{1,0},{2,1},{3,2},{4,7},{5,4},{6,5},{7,6},{8,11},{9,8},{10,9... | collective-permute-start | bytes 786440 | tf_op jit(solution)/shard_map/ppermute | solution.py:33
  53.8 7.8 %collective-permute-start.14 = (bf16[4,128,256]{2,1,0:T(8,128)(2,1)S(1)}, bf16[4,128,256]{2,1,0:T(8,128)(2,1)S(1)}, u32[]{:S(2)}, u32[]{:S(2)}) collective-permute-start(bf16[4,128,256]{2,1,0:T(8,128)(2,1)S(1)} %slice.28), channel_id=1, source_target_pairs={{0,1},{1,2},{2,3},{3,0},{4,5},{5,6},{6,7},{7,4},{8,9},{9,10},{10,1... | collective-permute-start | bytes 786440 | tf_op jit(solution)/shard_map/ppermute | solution.py:33
  58.6 13.8 %collective-permute-start.16 = (bf16[3,128,512]{2,1,0:T(8,128)(2,1)S(1)}, bf16[3,128,512]{2,1,0:T(8,128)(2,1)S(1)}, u32[]{:S(2)}, u32[]{:S(2)}) collective-permute-start(bf16[3,128,512]{2,1,0:T(8,128)(2,1)S(1)} %get-tuple-element.59), channel_id=1, source_target_pairs={{0,16},{16,0},{1,17},{17,1},{2,18},{18,2},{3,19},{19,3},{4,20},{20... | collective-permute-start | bytes 1179656 | tf_op jit(solution)/shard_map/ppermute | solution.py:33
  80.1 10.9 %collective-permute-start.21 = (bf16[512,256]{1,0:T(8,128)(2,1)S(1)}, bf16[512,256]{1,0:T(8,128)(2,1)S(1)}, u32[]{:S(2)}, u32[]{:S(2)}) collective-permute-start(bf16[512,256]{1,0:T(8,128)(2,1)S(1)} %get-tuple-element.72.own_w), channel_id=1, source_target_pairs={{0,16},{16,0},{1,17},{17,1},{2,18},{18,2},{3,19},{19,3},{4,20},{20... | collective-permute-start | bytes 786440 | tf_op jit(solution)/shard_map/ppermute | solution.py:33
  85.6 11.0 %collective-permute-start.20 = (bf16[512,256]{1,0:T(8,128)(2,1)S(1)}, bf16[512,256]{1,0:T(8,128)(2,1)S(1)}, u32[]{:S(2)}, u32[]{:S(2)}) collective-permute-start(bf16[512,256]{1,0:T(8,128)(2,1)S(1)} %get-tuple-element.71.own_w), channel_id=1, source_target_pairs={{0,16},{16,0},{1,17},{17,1},{2,18},{18,2},{3,19},{19,3},{4,20},{20... | collective-permute-start | bytes 786440 | tf_op jit(solution)/shard_map/ppermute | solution.py:33
  97.8 7.9 %collective-permute-start.25 = (bf16[128,512]{1,0:T(8,128)(2,1)S(1)}, bf16[128,512]{1,0:T(8,128)(2,1)S(1)}, u32[]{:S(2)}, u32[]{:S(2)}) collective-permute-start(bf16[128,512]{1,0:T(8,128)(2,1)S(1)} %get-tuple-element.78), channel_id=1, source_target_pairs={{0,64},{32,96},{64,128},{96,160},{128,192},{160,224},{192,0},{224,... | collective-permute-start | bytes 393224 | tf_op jit(solution)/shard_map/ppermute | solution.py:33
  99.7 12.7 %collective-permute-start.28 = (bf16[128,512]{1,0:T(8,128)(2,1)S(1)}, bf16[128,512]{1,0:T(8,128)(2,1)S(1)}, u32[]{:S(2)}, u32[]{:S(2)}) collective-permute-start(bf16[128,512]{1,0:T(8,128)(2,1)S(1)} %get-tuple-element.81), channel_id=1, source_target_pairs={{0,192},{32,224},{64,0},{96,32},{128,64},{160,96},{192,128},{224,1... | collective-permute-start | bytes 393224 | tf_op jit(solution)/shard_map/ppermute | solution.py:33
  101.5 8.8 %collective-permute-start.24 = (bf16[256,512]{1,0:T(8,128)(2,1)S(1)}, bf16[256,512]{1,0:T(8,128)(2,1)S(1)}, u32[]{:S(2)}, u32[]{:S(2)}) collective-permute-start(bf16[256,512]{1,0:T(8,128)(2,1)S(1)} %get-tuple-element.77), channel_id=1, source_target_pairs={{0,32},{32,64},{64,96},{96,128},{128,160},{160,192},{192,224},{224... | collective-permute-start | bytes 786440 | tf_op jit(solution)/shard_map/ppermute | solution.py:33
  101.5 11.0 %collective-permute-start.27 = (bf16[256,512]{1,0:T(8,128)(2,1)S(1)}, bf16[256,512]{1,0:T(8,128)(2,1)S(1)}, u32[]{:S(2)}, u32[]{:S(2)}) collective-permute-start(bf16[256,512]{1,0:T(8,128)(2,1)S(1)} %get-tuple-element.80), channel_id=1, source_target_pairs={{0,224},{32,0},{64,32},{96,64},{128,96},{160,128},{192,160},{224,1... | collective-permute-start | bytes 786440 | tf_op jit(solution)/shard_map/ppermute | solution.py:33
  105.6 10.3 %collective-permute-start.22 = (bf16[256,512]{1,0:T(8,128)(2,1)S(1)}, bf16[256,512]{1,0:T(8,128)(2,1)S(1)}, u32[]{:S(2)}, u32[]{:S(2)}) collective-permute-start(bf16[256,512]{1,0:T(8,128)(2,1)S(1)} %get-tuple-element.74), channel_id=1, source_target_pairs={{0,32},{32,64},{64,96},{96,128},{128,160},{160,192},{192,224},{224... | collective-permute-start | bytes 786440 | tf_op jit(solution)/shard_map/ppermute | solution.py:33
  105.7 12.4 %collective-permute-start.23 = (bf16[256,512]{1,0:T(8,128)(2,1)S(1)}, bf16[256,512]{1,0:T(8,128)(2,1)S(1)}, u32[]{:S(2)}, u32[]{:S(2)}) collective-permute-start(bf16[256,512]{1,0:T(8,128)(2,1)S(1)} %get-tuple-element.75), channel_id=1, source_target_pairs={{0,224},{32,0},{64,32},{96,64},{128,96},{160,128},{192,160},{224,1... | collective-permute-start | bytes 786440 | tf_op jit(solution)/shard_map/ppermute | solution.py:33
  110.4 14.7 %collective-permute-start.26 = (bf16[256,512]{1,0:T(8,128)(2,1)S(1)}, bf16[256,512]{1,0:T(8,128)(2,1)S(1)}, u32[]{:S(2)}, u32[]{:S(2)}) collective-permute-start(bf16[256,512]{1,0:T(8,128)(2,1)S(1)} %shard_map.136), channel_id=1, source_target_pairs={{0,64},{32,96},{64,128},{96,160},{128,192},{160,224},{192,0},{224,... | collective-permute-start | bytes 786440 | tf_op jit(solution)/shard_map/ppermute | solution.py:33
  112.5 17.2 %collective-permute-start.29 = (bf16[256,512]{1,0:T(8,128)(2,1)S(1)}, bf16[256,512]{1,0:T(8,128)(2,1)S(1)}, u32[]{:S(2)}, u32[]{:S(2)}) collective-permute-start(bf16[256,512]{1,0:T(8,128)(2,1)S(1)} %shard_map.137), channel_id=1, source_target_pairs={{0,192},{32,224},{64,0},{96,32},{128,64},{160,96},{192,128},{224,1... | collective-permute-start | bytes 786440 | tf_op jit(solution)/shard_map/ppermute | solution.py:33
  (14 other events, 76.0 us)

commit v5 on v4

--- a/solution.py
+++ b/solution.py
@@ -88,6 +88,11 @@
         sums[piece] = dot(left, right, ((0,), (0,)))
 
 
+def forward_kernel(up, down, up_out, down_out):
+    up_out[...] = up[...]
+    down_out[...] = down[...]
+
+
 def put(total, yh, piece, keep, send):
     total = total * (1.0 / 4096)
     upper, lower = total[:128], total[128:]
@@ -296,6 +301,8 @@
     other0 = shift(split, "c", 1)
     up2, down2 = shift(up1, "z", 1), shift(down1, "z", -1)
     up2, down2 = tie(up2, down2)
+    step = jax.ShapeDtypeStruct((2, tokens, block), BF16)
+    up2, down2 = call(forward_kernel, (step, step), [VMEM, VMEM], cost=(1 << 31, 2 << 20))(up2, down2)
     up3, down3 = tie(shift(up2, "z", 1), shift(down2, "z", -1))
     far_low, far_high = shift(up3[0], "z", 1), shift(down3[1], "z", -1)
     other1, other2 = shift(right, "c", 1), shift(left, "c", 1)

time: 134 us -> 133 us (level)
  transfers between devices with their start and end apart: 32 -> 32, of which waited for: 15 -> 17; matrix products, arithmetic and copies ran while one was open for 0% -> 0% of each run, Pallas kernels for 7% -> 7%
where the time goes in v5:
time: 133 us; the launch traced here: 134 us
  starting transfers between devices  60.9 us (46%)
  waiting for transfers between devices  52.5 us (39%)
  Pallas kernels  17.4 us (13%)
  between operations  1.56 us (1%)
    ppermute x31, waiting for transfers between devices, shift(): lax.ppermute(value, axis, [(i, (i + step) % size) for i in range(size)])  52.5 us
    ppermute x31, starting transfers between devices, shift(): lax.ppermute(value, axis, [(i, (i + step) % size) for i in range(size)])  51.9 us
    all_to_all x1, starting transfers between devices, body(): split = lax.all_to_all(split, 'z', 0, 0, tiled=True)  9.03 us
    pallas_call x1, Pallas kernels, body(): call(step_kernel, (full,) * 5 + (wide, narrow), [SMEM, SMEM] + [VMEM] * 8...  3.9 us
    pallas_call x1, Pallas kernels, body(): call(gradient_kernel, (jax.ShapeDtypeStruct((3, quarter, block), F32), ja...  3.43 us
  transfers between devices with their start and end apart: 32, of which 17 were waited for; matrix products, arithmetic and copies ran while one was open for 0% of the time, Pallas kernels for 7%

profile of v5, /device:TPU:1, one launch (start us, length us, event | category | flops | bytes accessed | tf_op | source)
XLA Modules:
  0.0 133.5 jit_solution(14960654445653014700)
XLA Ops:
  0.7 2.5 %shard_map.127 = bf16[8,128,256]{2,1,0:T(8,128)(2,1)} custom-call(s32[3]{0:T(128)S(1)} %pad_add_fusion.place, bf16[128,8192]{1,0:T(8,128)(2,1)} %inputs.1), custom_call_target="tpu_custom_call" | custom-call | tf_op jit(solution)/shard_map/pallas_call | solution.py:285
  3.2 9.0 %all-to-all-start = ((bf16[8,128,256]{2,1,0:T(8,128)(2,1)}), bf16[8,128,256]{2,1,0:T(8,128)(2,1)S(1)}, u32[]{:S(2)}, u32[]{:S(2)}) async-start(bf16[8,128,256]{2,1,0:T(8,128)(2,1)} %shard_map.127), calls=%async_computation | async-start | bytes 1048576 | tf_op jit(solution)/shard_map/all_to_all | solution.py:298
  14.3 3.0 %collective-permute-start.2 = (bf16[2,128,512]{2,1,0:T(8,128)(2,1)S(1)}, bf16[2,128,512]{2,1,0:T(8,128)(2,1)S(1)}, u32[]{:S(2)}, u32[]{:S(2)}) collective-permute-start(bf16[2,128,512]{2,1,0:T(8,128)(2,1)S(1)} %pad_maximum_fusion.refs_6_), channel_id=1, source_target_pairs={{0,224},{32,0},{64,32},{96,64},{128,96},{160,128},{192,160},{224,1... | collective-permute-start | bytes 786440 | tf_op jit(solution)/shard_map/ppermute | solution.py:33
  17.4 13.2 %collective-permute-done.2.refs_10_ = bf16[2,128,512]{2,1,0:T(8,128)(2,1)S(1)} collective-permute-done((bf16[2,128,512]{2,1,0:T(8,128)(2,1)S(1)}, bf16[2,128,512]{2,1,0:T(8,128)(2,1)S(1)}, u32[]{:S(2)}, u32[]{:S(2)}) %collective-permute-start.2) | collective-permute-done | bytes 262176 | tf_op jit(solution)/shard_map/ppermute | solution.py:33
  32.2 2.7 %collective-permute-start.9 = (bf16[2,128,512]{2,1,0:T(8,128)(2,1)S(1)}, bf16[2,128,512]{2,1,0:T(8,128)(2,1)S(1)}, u32[]{:S(2)}, u32[]{:S(2)}) collective-permute-start(bf16[2,128,512]{2,1,0:T(8,128)(2,1)S(1)} %collective-permute-done.2.refs_10_), channel_id=1, source_target_pairs={{0,224},{32,0},{64,32},{96,64},{128,96},{160,128},{192,160},{224,1... | collective-permute-start | bytes 786440 | tf_op jit(solution)/shard_map/ppermute | solution.py:33
  34.9 2.5 %collective-permute-start.4 = (bf16[8,128,256]{2,1,0:T(8,128)(2,1)S(1)}, bf16[8,128,256]{2,1,0:T(8,128)(2,1)S(1)}, u32[]{:S(2)}, u32[]{:S(2)}) collective-permute-start(bf16[8,128,256]{2,1,0:T(8,128)(2,1)S(1)} %all-to-all-done.refs_0_), channel_id=1, source_target_pairs={{0,3},{1,0},{2,1},{3,2},{4,7},{5,4},{6,5},{7,6},{8,11},{9,8},{10,9... | collective-permute-start | bytes 1572872 | tf_op jit(solution)/shard_map/ppermute | solution.py:33
  37.3 2.4 %collective-permute-done.8.up = bf16[2,128,512]{2,1,0:T(8,128)(2,1)S(1)} collective-permute-done((bf16[2,128,512]{2,1,0:T(8,128)(2,1)S(1)}, bf16[2,128,512]{2,1,0:T(8,128)(2,1)S(1)}, u32[]{:S(2)}, u32[]{:S(2)}) %collective-permute-start.8) | collective-permute-done | bytes 262176 | tf_op jit(solution)/shard_map/ppermute | solution.py:33
  40.1 2.4 %collective-permute-start.11 = (bf16[2,128,512]{2,1,0:T(8,128)(2,1)S(1)}, bf16[2,128,512]{2,1,0:T(8,128)(2,1)S(1)}, u32[]{:S(2)}, u32[]{:S(2)}) collective-permute-start(bf16[2,128,512]{2,1,0:T(8,128)(2,1)S(1)} %get-tuple-element.56.refs_11_), channel_id=1, source_target_pairs={{0,224},{32,0},{64,32},{96,64},{128,96},{160,128},{192,160},{224,1... | collective-permute-start | bytes 786440 | tf_op jit(solution)/shard_map/ppermute | solution.py:33
  42.5 4.0 %collective-permute-done.4.refs_2_ = bf16[8,128,256]{2,1,0:T(8,128)(2,1)S(1)} collective-permute-done((bf16[8,128,256]{2,1,0:T(8,128)(2,1)S(1)}, bf16[8,128,256]{2,1,0:T(8,128)(2,1)S(1)}, u32[]{:S(2)}, u32[]{:S(2)}) %collective-permute-start.4) | collective-permute-done | bytes 524320 | tf_op jit(solution)/shard_map/ppermute | solution.py:33
  46.5 2.9 %collective-permute-start.6 = (bf16[8,128,256]{2,1,0:T(8,128)(2,1)S(1)}, bf16[8,128,256]{2,1,0:T(8,128)(2,1)S(1)}, u32[]{:S(2)}, u32[]{:S(2)}) collective-permute-start(bf16[8,128,256]{2,1,0:T(8,128)(2,1)S(1)} %collective-permute-done.4.refs_2_), channel_id=1, source_target_pairs={{0,8},{8,0},{1,9},{9,1},{2,10},{10,2},{3,11},{11,3},{4,12},{12,4},... | collective-permute-start | bytes 1572872 | tf_op jit(solution)/shard_map/ppermute | solution.py:33
  49.7 3.2 %collective-permute-start.5 = (bf16[8,128,256]{2,1,0:T(8,128)(2,1)S(1)}, bf16[8,128,256]{2,1,0:T(8,128)(2,1)S(1)}, u32[]{:S(2)}, u32[]{:S(2)}) collective-permute-start(bf16[8,128,256]{2,1,0:T(8,128)(2,1)S(1)} %collective-permute-done.3.refs_1_), channel_id=1, source_target_pairs={{0,8},{8,0},{1,9},{9,1},{2,10},{10,2},{3,11},{11,3},{4,12},{12,4},... | collective-permute-start | bytes 1572872 | tf_op jit(solution)/shard_map/ppermute | solution.py:33
  56.2 3.4 %shard_map.129 = (f32[3,256,512]{2,1,0:T(8,128)S(1)}, bf16[3,8,2,128,256]{4,3,2,1,0:T(8,128)(2,1)S(1)}, bf16[8,2,128,512]{3,2,1,0:T(8,128)(2,1)S(1)}) custom-call(s32[3]{0:T(128)S(1)} %pad_add_fusion.place, bf16[8,128,256]{2,1,0:T(8,128)(2,1)S(1)} %all-to-all-done.refs_0_, bf16[8,128,256]{2,1,0:T(8,128)(2,1)S(1)} %collective-permute-done.3.refs_1_, ...), custom_call_target="tpu_custom_call" | custom-call | flops 12884901888 | bytes 6291456 | tf_op jit(solution)/shard_map/pallas_call | solution.py:315
  61.0 3.0 %collective-permute-start.16 = (bf16[3,128,512]{2,1,0:T(8,128)(2,1)S(1)}, bf16[3,128,512]{2,1,0:T(8,128)(2,1)S(1)}, u32[]{:S(2)}, u32[]{:S(2)}) collective-permute-start(bf16[3,128,512]{2,1,0:T(8,128)(2,1)S(1)} %get-tuple-element.63), channel_id=1, source_target_pairs={{0,16},{16,0},{1,17},{17,1},{2,18},{18,2},{3,19},{19,3},{4,20},{20... | collective-permute-start | bytes 1179656 | tf_op jit(solution)/shard_map/ppermute | solution.py:33
  69.0 2.3 %collective-permute-start.19 = (bf16[1,128,512]{2,1,0:T(8,128)(2,1)S(1)}, bf16[1,128,512]{2,1,0:T(8,128)(2,1)S(1)}, u32[]{:S(2)}, u32[]{:S(2)}) collective-permute-start(bf16[1,128,512]{2,1,0:T(8,128)(2,1)S(1)} %get-tuple-element.68), channel_id=1, source_target_pairs={{0,16},{16,0},{1,17},{17,1},{2,18},{18,2},{3,19},{19,3},{4,20},{20... | collective-permute-start | bytes 393224 | tf_op jit(solution)/shard_map/ppermute | solution.py:33
  71.6 4.5 %collective-permute-done.19.got1 = bf16[1,128,512]{2,1,0:T(8,128)(2,1)S(1)} collective-permute-done((bf16[1,128,512]{2,1,0:T(8,128)(2,1)S(1)}, bf16[1,128,512]{2,1,0:T(8,128)(2,1)S(1)}, u32[]{:S(2)}, u32[]{:S(2)}) %collective-permute-start.19) | collective-permute-done | bytes 131104 | tf_op jit(solution)/shard_map/ppermute | solution.py:33
  76.2 3.9 %shard_map.133 = (f32[512,512]{1,0:T(8,128)}, f32[512,512]{1,0:T(8,128)}, f32[512,512]{1,0:T(8,128)}, f32[512,512]{1,0:T(8,128)}, f32[512,512]{1,0:T(8,128)}, /*...) custom-call(s32[1]{0:T(128)S(6)} %copy.14.flag, s32[3]{0:T(128)S(1)} %pad_add_fusion.place, ...), custom_call_target="tpu_custom_call" | custom-call | tf_op jit(solution)/shard_map/pallas_call | solution.py:364
  83.0 3.8 %collective-permute-done.21.other_w = bf16[512,256]{1,0:T(8,128)(2,1)S(1)} collective-permute-done((bf16[512,256]{1,0:T(8,128)(2,1)S(1)}, bf16[512,256]{1,0:T(8,128)(2,1)S(1)}, u32[]{:S(2)}, u32[]{:S(2)}) %collective-permute-start.21) | collective-permute-done | bytes 262176 | tf_op jit(solution)/shard_map/ppermute | solution.py:33
  88.6 2.5 %collective-permute-done.20.other_w = bf16[512,256]{1,0:T(8,128)(2,1)S(1)} collective-permute-done((bf16[512,256]{1,0:T(8,128)(2,1)S(1)}, bf16[512,256]{1,0:T(8,128)(2,1)S(1)}, u32[]{:S(2)}, u32[]{:S(2)}) %collective-permute-start.20) | collective-permute-done | bytes 262176 | tf_op jit(solution)/shard_map/ppermute | solution.py:33
  94.5 2.6 %collective-permute-start.28 = (bf16[128,512]{1,0:T(8,128)(2,1)S(1)}, bf16[128,512]{1,0:T(8,128)(2,1)S(1)}, u32[]{:S(2)}, u32[]{:S(2)}) collective-permute-start(bf16[128,512]{1,0:T(8,128)(2,1)S(1)} %get-tuple-element.85), channel_id=1, source_target_pairs={{0,192},{32,224},{64,0},{96,32},{128,64},{160,96},{192,128},{224,1... | collective-permute-start | bytes 393224 | tf_op jit(solution)/shard_map/ppermute | solution.py:33
  97.1 4.6 %collective-permute-start.24 = (bf16[256,512]{1,0:T(8,128)(2,1)S(1)}, bf16[256,512]{1,0:T(8,128)(2,1)S(1)}, u32[]{:S(2)}, u32[]{:S(2)}) collective-permute-start(bf16[256,512]{1,0:T(8,128)(2,1)S(1)} %get-tuple-element.81), channel_id=1, source_target_pairs={{0,32},{32,64},{64,96},{96,128},{128,160},{160,192},{192,224},{224... | collective-permute-start | bytes 786440 | tf_op jit(solution)/shard_map/ppermute | solution.py:33
  107.7 6.3 %collective-permute-start.26 = (bf16[256,512]{1,0:T(8,128)(2,1)S(1)}, bf16[256,512]{1,0:T(8,128)(2,1)S(1)}, u32[]{:S(2)}, u32[]{:S(2)}) collective-permute-start(bf16[256,512]{1,0:T(8,128)(2,1)S(1)} %shard_map.137), channel_id=1, source_target_pairs={{0,64},{32,96},{64,128},{96,160},{128,192},{160,224},{192,0},{224,... | collective-permute-start | bytes 786440 | tf_op jit(solution)/shard_map/ppermute | solution.py:33
  114.2 4.5 %collective-permute-done.23 = bf16[256,512]{1,0:T(8,128)(2,1)S(1)} collective-permute-done((bf16[256,512]{1,0:T(8,128)(2,1)S(1)}, bf16[256,512]{1,0:T(8,128)(2,1)S(1)}, u32[]{:S(2)}, u32[]{:S(2)}) %collective-permute-start.23) | collective-permute-done | bytes 262176 | tf_op jit(solution)/shard_map/ppermute | solution.py:33
  118.7 7.2 %collective-permute-done.26 = bf16[256,512]{1,0:T(8,128)(2,1)S(1)} collective-permute-done((bf16[256,512]{1,0:T(8,128)(2,1)S(1)}, bf16[256,512]{1,0:T(8,128)(2,1)S(1)}, u32[]{:S(2)}, u32[]{:S(2)}) %collective-permute-start.26) | collective-permute-done | bytes 262176 | tf_op jit(solution)/shard_map/ppermute | solution.py:33
  125.9 3.9 %collective-permute-done.29 = bf16[256,512]{1,0:T(8,128)(2,1)S(1)} collective-permute-done((bf16[256,512]{1,0:T(8,128)(2,1)S(1)}, bf16[256,512]{1,0:T(8,128)(2,1)S(1)}, u32[]{:S(2)}, u32[]{:S(2)}) %collective-permute-start.29) | collective-permute-done | bytes 262176 | tf_op jit(solution)/shard_map/ppermute | solution.py:33
  (76 shorter events, 31.5 us)
Async XLA Ops:
  3.2 29.0 %all-to-all-start = ((bf16[8,128,256]{2,1,0:T(8,128)(2,1)}), bf16[8,128,256]{2,1,0:T(8,128)(2,1)S(1)}, u32[]{:S(2)}, u32[]{:S(2)}) async-start(bf16[8,128,256]{2,1,0:T(8,128)(2,1)} %shard_map.127), calls=%async_computation | async-start | bytes 1048576 | tf_op jit(solution)/shard_map/all_to_all | solution.py:298
  14.3 16.2 %collective-permute-start.2 = (bf16[2,128,512]{2,1,0:T(8,128)(2,1)S(1)}, bf16[2,128,512]{2,1,0:T(8,128)(2,1)S(1)}, u32[]{:S(2)}, u32[]{:S(2)}) collective-permute-start(bf16[2,128,512]{2,1,0:T(8,128)(2,1)S(1)} %pad_maximum_fusion.refs_6_), channel_id=1, source_target_pairs={{0,224},{32,0},{64,32},{96,64},{128,96},{160,128},{192,160},{224,1... | collective-permute-start | bytes 786440 | tf_op jit(solution)/shard_map/ppermute | solution.py:33
  17.4 14.8 %collective-permute-start.1 = (bf16[2,128,512]{2,1,0:T(8,128)(2,1)S(1)}, bf16[2,128,512]{2,1,0:T(8,128)(2,1)S(1)}, u32[]{:S(2)}, u32[]{:S(2)}) collective-permute-start(bf16[2,128,512]{2,1,0:T(8,128)(2,1)S(1)} %pad_maximum_fusion.refs_6_), channel_id=1, source_target_pairs={{0,32},{32,64},{64,96},{96,128},{128,160},{160,192},{192,224},{224... | collective-permute-start | bytes 786440 | tf_op jit(solution)/shard_map/ppermute | solution.py:33
  32.2 7.6 %collective-permute-start.8 = (bf16[2,128,512]{2,1,0:T(8,128)(2,1)S(1)}, bf16[2,128,512]{2,1,0:T(8,128)(2,1)S(1)}, u32[]{:S(2)}, u32[]{:S(2)}) collective-permute-start(bf16[2,128,512]{2,1,0:T(8,128)(2,1)S(1)} %collective-permute-done.1.refs_7_), channel_id=1, source_target_pairs={{0,32},{32,64},{64,96},{96,128},{128,160},{160,192},{192,224},{224... | collective-permute-start | bytes 786440 | tf_op jit(solution)/shard_map/ppermute | solution.py:33
  32.2 7.6 %collective-permute-start.9 = (bf16[2,128,512]{2,1,0:T(8,128)(2,1)S(1)}, bf16[2,128,512]{2,1,0:T(8,128)(2,1)S(1)}, u32[]{:S(2)}, u32[]{:S(2)}) collective-permute-start(bf16[2,128,512]{2,1,0:T(8,128)(2,1)S(1)} %collective-permute-done.2.refs_10_), channel_id=1, source_target_pairs={{0,224},{32,0},{64,32},{96,64},{128,96},{160,128},{192,160},{224,1... | collective-permute-start | bytes 786440 | tf_op jit(solution)/shard_map/ppermute | solution.py:33
  34.9 11.7 %collective-permute-start.4 = (bf16[8,128,256]{2,1,0:T(8,128)(2,1)S(1)}, bf16[8,128,256]{2,1,0:T(8,128)(2,1)S(1)}, u32[]{:S(2)}, u32[]{:S(2)}) collective-permute-start(bf16[8,128,256]{2,1,0:T(8,128)(2,1)S(1)} %all-to-all-done.refs_0_), channel_id=1, source_target_pairs={{0,3},{1,0},{2,1},{3,2},{4,7},{5,4},{6,5},{7,6},{8,11},{9,8},{10,9... | collective-permute-start | bytes 1572872 | tf_op jit(solution)/shard_map/ppermute | solution.py:33
  37.3 12.3 %collective-permute-start.3 = (bf16[8,128,256]{2,1,0:T(8,128)(2,1)S(1)}, bf16[8,128,256]{2,1,0:T(8,128)(2,1)S(1)}, u32[]{:S(2)}, u32[]{:S(2)}) collective-permute-start(bf16[8,128,256]{2,1,0:T(8,128)(2,1)S(1)} %all-to-all-done.refs_0_), channel_id=1, source_target_pairs={{0,1},{1,2},{2,3},{3,0},{4,5},{5,6},{6,7},{7,4},{8,9},{9,10},{10,1... | collective-permute-start | bytes 1572872 | tf_op jit(solution)/shard_map/ppermute | solution.py:33
  39.8 13.1 %collective-permute-start.10 = (bf16[2,128,512]{2,1,0:T(8,128)(2,1)S(1)}, bf16[2,128,512]{2,1,0:T(8,128)(2,1)S(1)}, u32[]{:S(2)}, u32[]{:S(2)}) collective-permute-start(bf16[2,128,512]{2,1,0:T(8,128)(2,1)S(1)} %get-tuple-element.55.refs_8_), channel_id=1, source_target_pairs={{0,32},{32,64},{64,96},{96,128},{128,160},{160,192},{192,224},{224... | collective-permute-start | bytes 786440 | tf_op jit(solution)/shard_map/ppermute | solution.py:33
  40.1 12.8 %collective-permute-start.11 = (bf16[2,128,512]{2,1,0:T(8,128)(2,1)S(1)}, bf16[2,128,512]{2,1,0:T(8,128)(2,1)S(1)}, u32[]{:S(2)}, u32[]{:S(2)}) collective-permute-start(bf16[2,128,512]{2,1,0:T(8,128)(2,1)S(1)} %get-tuple-element.56.refs_11_), channel_id=1, source_target_pairs={{0,224},{32,0},{64,32},{96,64},{128,96},{160,128},{192,160},{224,1... | collective-permute-start | bytes 786440 | tf_op jit(solution)/shard_map/ppermute | solution.py:33
  46.5 8.0 %collective-permute-start.6 = (bf16[8,128,256]{2,1,0:T(8,128)(2,1)S(1)}, bf16[8,128,256]{2,1,0:T(8,128)(2,1)S(1)}, u32[]{:S(2)}, u32[]{:S(2)}) collective-permute-start(bf16[8,128,256]{2,1,0:T(8,128)(2,1)S(1)} %collective-permute-done.4.refs_2_), channel_id=1, source_target_pairs={{0,8},{8,0},{1,9},{9,1},{2,10},{10,2},{3,11},{11,3},{4,12},{12,4},... | collective-permute-start | bytes 1572872 | tf_op jit(solution)/shard_map/ppermute | solution.py:33
  54.6 9.4 %collective-permute-start.15 = (bf16[4,128,256]{2,1,0:T(8,128)(2,1)S(1)}, bf16[4,128,256]{2,1,0:T(8,128)(2,1)S(1)}, u32[]{:S(2)}, u32[]{:S(2)}) collective-permute-start(bf16[4,128,256]{2,1,0:T(8,128)(2,1)S(1)} %slice.29), channel_id=1, source_target_pairs={{0,3},{1,0},{2,1},{3,2},{4,7},{5,4},{6,5},{7,6},{8,11},{9,8},{10,9... | collective-permute-start | bytes 786440 | tf_op jit(solution)/shard_map/ppermute | solution.py:33
  55.3 8.7 %collective-permute-start.14 = (bf16[4,128,256]{2,1,0:T(8,128)(2,1)S(1)}, bf16[4,128,256]{2,1,0:T(8,128)(2,1)S(1)}, u32[]{:S(2)}, u32[]{:S(2)}) collective-permute-start(bf16[4,128,256]{2,1,0:T(8,128)(2,1)S(1)} %slice.28), channel_id=1, source_target_pairs={{0,1},{1,2},{2,3},{3,0},{4,5},{5,6},{6,7},{7,4},{8,9},{9,10},{10,1... | collective-permute-start | bytes 786440 | tf_op jit(solution)/shard_map/ppermute | solution.py:33
  61.0 10.6 %collective-permute-start.16 = (bf16[3,128,512]{2,1,0:T(8,128)(2,1)S(1)}, bf16[3,128,512]{2,1,0:T(8,128)(2,1)S(1)}, u32[]{:S(2)}, u32[]{:S(2)}) collective-permute-start(bf16[3,128,512]{2,1,0:T(8,128)(2,1)S(1)} %get-tuple-element.63), channel_id=1, source_target_pairs={{0,16},{16,0},{1,17},{17,1},{2,18},{18,2},{3,19},{19,3},{4,20},{20... | collective-permute-start | bytes 1179656 | tf_op jit(solution)/shard_map/ppermute | solution.py:33
  69.0 7.2 %collective-permute-start.19 = (bf16[1,128,512]{2,1,0:T(8,128)(2,1)S(1)}, bf16[1,128,512]{2,1,0:T(8,128)(2,1)S(1)}, u32[]{:S(2)}, u32[]{:S(2)}) collective-permute-start(bf16[1,128,512]{2,1,0:T(8,128)(2,1)S(1)} %get-tuple-element.68), channel_id=1, source_target_pairs={{0,16},{16,0},{1,17},{17,1},{2,18},{18,2},{3,19},{19,3},{4,20},{20... | collective-permute-start | bytes 393224 | tf_op jit(solution)/shard_map/ppermute | solution.py:33
  80.0 6.7 %collective-permute-start.21 = (bf16[512,256]{1,0:T(8,128)(2,1)S(1)}, bf16[512,256]{1,0:T(8,128)(2,1)S(1)}, u32[]{:S(2)}, u32[]{:S(2)}) collective-permute-start(bf16[512,256]{1,0:T(8,128)(2,1)S(1)} %get-tuple-element.76.own_w), channel_id=1, source_target_pairs={{0,16},{16,0},{1,17},{17,1},{2,18},{18,2},{3,19},{19,3},{4,20},{20... | collective-permute-start | bytes 786440 | tf_op jit(solution)/shard_map/ppermute | solution.py:33
  82.3 8.8 %collective-permute-start.20 = (bf16[512,256]{1,0:T(8,128)(2,1)S(1)}, bf16[512,256]{1,0:T(8,128)(2,1)S(1)}, u32[]{:S(2)}, u32[]{:S(2)}) collective-permute-start(bf16[512,256]{1,0:T(8,128)(2,1)S(1)} %get-tuple-element.75.own_w), channel_id=1, source_target_pairs={{0,16},{16,0},{1,17},{17,1},{2,18},{18,2},{3,19},{19,3},{4,20},{20... | collective-permute-start | bytes 786440 | tf_op jit(solution)/shard_map/ppermute | solution.py:33
  92.3 12.4 %collective-permute-start.25 = (bf16[128,512]{1,0:T(8,128)(2,1)S(1)}, bf16[128,512]{1,0:T(8,128)(2,1)S(1)}, u32[]{:S(2)}, u32[]{:S(2)}) collective-permute-start(bf16[128,512]{1,0:T(8,128)(2,1)S(1)} %get-tuple-element.82), channel_id=1, source_target_pairs={{0,64},{32,96},{64,128},{96,160},{128,192},{160,224},{192,0},{224,... | collective-permute-start | bytes 393224 | tf_op jit(solution)/shard_map/ppermute | solution.py:33
  94.5 19.5 %collective-permute-start.28 = (bf16[128,512]{1,0:T(8,128)(2,1)S(1)}, bf16[128,512]{1,0:T(8,128)(2,1)S(1)}, u32[]{:S(2)}, u32[]{:S(2)}) collective-permute-start(bf16[128,512]{1,0:T(8,128)(2,1)S(1)} %get-tuple-element.85), channel_id=1, source_target_pairs={{0,192},{32,224},{64,0},{96,32},{128,64},{160,96},{192,128},{224,1... | collective-permute-start | bytes 393224 | tf_op jit(solution)/shard_map/ppermute | solution.py:33
  97.1 10.5 %collective-permute-start.24 = (bf16[256,512]{1,0:T(8,128)(2,1)S(1)}, bf16[256,512]{1,0:T(8,128)(2,1)S(1)}, u32[]{:S(2)}, u32[]{:S(2)}) collective-permute-start(bf16[256,512]{1,0:T(8,128)(2,1)S(1)} %get-tuple-element.81), channel_id=1, source_target_pairs={{0,32},{32,64},{64,96},{96,128},{128,160},{160,192},{192,224},{224... | collective-permute-start | bytes 786440 | tf_op jit(solution)/shard_map/ppermute | solution.py:33
  101.7 12.3 %collective-permute-start.27 = (bf16[256,512]{1,0:T(8,128)(2,1)S(1)}, bf16[256,512]{1,0:T(8,128)(2,1)S(1)}, u32[]{:S(2)}, u32[]{:S(2)}) collective-permute-start(bf16[256,512]{1,0:T(8,128)(2,1)S(1)} %get-tuple-element.84), channel_id=1, source_target_pairs={{0,224},{32,0},{64,32},{96,64},{128,96},{160,128},{192,160},{224,1... | collective-permute-start | bytes 786440 | tf_op jit(solution)/shard_map/ppermute | solution.py:33
  103.2 11.0 %collective-permute-start.22 = (bf16[256,512]{1,0:T(8,128)(2,1)S(1)}, bf16[256,512]{1,0:T(8,128)(2,1)S(1)}, u32[]{:S(2)}, u32[]{:S(2)}) collective-permute-start(bf16[256,512]{1,0:T(8,128)(2,1)S(1)} %get-tuple-element.78), channel_id=1, source_target_pairs={{0,32},{32,64},{64,96},{96,128},{128,160},{160,192},{192,224},{224... | collective-permute-start | bytes 786440 | tf_op jit(solution)/shard_map/ppermute | solution.py:33
  104.7 14.0 %collective-permute-start.23 = (bf16[256,512]{1,0:T(8,128)(2,1)S(1)}, bf16[256,512]{1,0:T(8,128)(2,1)S(1)}, u32[]{:S(2)}, u32[]{:S(2)}) collective-permute-start(bf16[256,512]{1,0:T(8,128)(2,1)S(1)} %get-tuple-element.79), channel_id=1, source_target_pairs={{0,224},{32,0},{64,32},{96,64},{128,96},{160,128},{192,160},{224,1... | collective-permute-start | bytes 786440 | tf_op jit(solution)/shard_map/ppermute | solution.py:33
  107.7 18.2 %collective-permute-start.26 = (bf16[256,512]{1,0:T(8,128)(2,1)S(1)}, bf16[256,512]{1,0:T(8,128)(2,1)S(1)}, u32[]{:S(2)}, u32[]{:S(2)}) collective-permute-start(bf16[256,512]{1,0:T(8,128)(2,1)S(1)} %shard_map.137), channel_id=1, source_target_pairs={{0,64},{32,96},{64,128},{96,160},{128,192},{160,224},{192,0},{224,... | collective-permute-start | bytes 786440 | tf_op jit(solution)/shard_map/ppermute | solution.py:33
  114.1 15.7 %collective-permute-start.29 = (bf16[256,512]{1,0:T(8,128)(2,1)S(1)}, bf16[256,512]{1,0:T(8,128)(2,1)S(1)}, u32[]{:S(2)}, u32[]{:S(2)}) collective-permute-start(bf16[256,512]{1,0:T(8,128)(2,1)S(1)} %shard_map.138), channel_id=1, source_target_pairs={{0,192},{32,224},{64,0},{96,32},{128,64},{160,96},{192,128},{224,1... | collective-permute-start | bytes 786440 | tf_op jit(solution)/shard_map/ppermute | solution.py:33
  (14 other events, 78.4 us)
